TPU v7x, 32 devices: a whole 2x2x4 slice. The times are simulated.
32 devices in a mesh: groups: 2 (over y), chol: 4 (over z), occ: 4 (over x, core).
Axes of the slice: x: 2, y: 2, z: 4, core: 2. Of those that a mesh axis runs over, the one named last changes fastest.
Arguments:
- chol_rot: bfloat16 [96, 256, 2048], P(('groups', 'chol'), 'occ'), parts along dimension 0, may hold values from -0.1875 to 0.1875
- green: bfloat16 [4, 256, 2048], P('groups', 'occ', 'chol'), parts along dimension 0, may hold values from -6 to 6
Outputs:
- gradient: float32 [256, 4, 2048], P('occ', 'groups', 'chol'), parts along dimension 1
There are 2 independent parts, one for each index of `groups`. A program takes and returns all parts, laid end to end along the dimension named above; each array names one. Nothing has to cross between parts.
All inputs are finite; a program needn't handle non-finite values.
Results may differ from a plain program's by a relative error of at most 0.0085.
Values may be sent and summed in bfloat16 or wider, within the bound.
No kernel may reach another device: no remote copies, remote signals or barrier semaphores. Data moves between devices by JAX's collectives and lax.ppermute only.
A program may use at most 64 MiB of HBM per device.

v0:
```python
import math

import jax
import jax.numpy as jnp
from jax import lax
from jax.sharding import PartitionSpec as P


def local(chol_rot, green):
    chol_loc, occ_loc, orbitals = chol_rot.shape
    walkers = green.shape[0]
    occupied = occ_loc * lax.axis_size("occ")
    nvec = chol_loc * lax.axis_size("chol")
    factor = -math.sqrt(orbitals / (nvec * occupied))
    vec_mat = chol_rot.reshape(chol_loc * occ_loc, orbitals)
    green_all = lax.all_gather(green, "occ", axis=1, tiled=True)
    piece = lax.all_gather(green_all, "chol", axis=2, tiled=True)
    flat = piece.reshape(-1, piece.shape[2])
    pair_sum = jnp.dot(vec_mat, flat.T, preferred_element_type=jnp.float32)
    pairs = pair_sum.astype(jnp.bfloat16).reshape(chol_loc, occ_loc, walkers, occupied)
    swapped = lax.all_to_all(pairs, "occ", split_axis=3, concat_axis=1, tiled=True)
    occ_summed = lax.psum_scatter(
        jnp.einsum("gjwi,gip->jwp", swapped, chol_rot, preferred_element_type=jnp.float32).astype(
            jnp.bfloat16
        ),
        "occ",
        scatter_dimension=0,
        tiled=True,
    ).astype(jnp.float32)
    summed = lax.psum_scatter(occ_summed, "chol", scatter_dimension=2, tiled=True)
    return summed * factor


def solution(mesh):
    return jax.shard_map(
        local,
        mesh=mesh,
        in_specs=(P(("groups", "chol"), "occ", None), P("groups", "occ", "chol")),
        out_specs=P("occ", "groups", "chol"),
        check_vma=False,
    )
```

profile of v0, /device:TPU:0, one launch (start us, length us, event | category | flops | bytes accessed | tf_op | source)
XLA Modules:
  0.0 178.3 jit_solution(8074986663680790082)
XLA Ops:
  6.5 0.0 copy-start
  6.5 0.0 all-gather.2.cloned.1.call-start
  6.5 10.5 %all_gather.6 = bf16[2,256,512]{2,1,0:T(8,128)(2,1)} all-gather(bf16[2,64,512]{2,1,0:T(8,128)(2,1)} %param.3), channel_id=1, replica_groups=mesh['groups'=2,'chol'=4,'occ'=4] {'occ'}, dimensions={1}, use_global_device_ids=true | all-gather | bytes 655360 | tf_op jit(solution)/shard_map/all_gather | solution.py:16
  17.0 0.0 all-gather.2.cloned.1.call-update
  17.0 0.0 reduce-scatter.3.cloned.1.call-start
  17.1 46.1 %all-gather.2.cloned.1.call-done = bf16[2,256,2048]{2,1,0:T(8,128)(2,1)} async-done(((bf16[2,256,512]{2,1,0:T(8,128)(2,1)}), bf16[2,256,2048]{2,1,0:T(8,128)(2,1)}) %all-gather.2.cloned.1.call-update) | async-done | bytes 2097168 | tf_op jit(solution)/shard_map/all_gather | solution.py:17
  63.2 0.0 copy-done
  63.2 4.3 %convolution_convert_fusion = bf16[768,512]{1,0:T(8,128)(2,1)} fusion(bf16[768,2048]{1,0:T(8,128)(2,1)S(1)} %bitcast.19, bf16[512,2048]{1,0:T(8,128)(2,1)} %bitcast.23), kind=kOutput, calls=%fused_computation.3 | convolution fusion | flops 1611005952 | bytes 6029312 | tf_op jit(solution)/shard_map/dot_general | solution.py:19
  67.5 2.9 %reshape.11 = bf16[12,64,2,256]{3,2,1,0:T(2,128)(2,1)} reshape(bf16[768,512]{1,0:T(8,128)(2,1)} %convolution_convert_fusion) | data formatting | bytes 1572864 | tf_op jit(solution)/shard_map/reshape | solution.py:20
  70.4 5.0 %copy.8 = bf16[12,64,2,256]{1,2,0,3:T(2,128)(2,1)} copy(bf16[12,64,2,256]{3,2,1,0:T(2,128)(2,1)} %reshape.11) | data formatting | bytes 1572864 | tf_op jit(solution)/shard_map/reshape | solution.py:20
  75.4 4.0 %reshape.14 = bf16[4,2,49152]{2,1,0:T(2,128)(2,1)} reshape(bf16[256,12,2,64]{3,2,1,0:T(2,128)(2,1)} %bitcast.20) | data formatting | bytes 1572864
  79.5 15.9 %all_to_all.18 = bf16[4,2,49152]{2,1,0:T(2,128)(2,1)} all-to-all(bf16[4,2,49152]{2,1,0:T(2,128)(2,1)} %reshape.14), channel_id=1, replica_groups=mesh['groups'=2,'chol'=4,'occ'=4] {'occ'}, dimensions={0} | all-to-all | bytes 1572864 | tf_op jit(solution)/shard_map/all_to_all | solution.py:21
  95.4 4.0 %reshape.15 = bf16[256,12,2,64]{3,2,1,0:T(2,128)(2,1)} reshape(bf16[4,2,49152]{2,1,0:T(2,128)(2,1)} %all_to_all.18) | data formatting | bytes 1572864
  99.3 3.8 %copy.13 = bf16[12,64,2,4,64]{1,3,4,0,2:T(4,128)(2,1)} copy(bf16[12,64,2,4,64]{1,2,0,4,3:T(2,128)(2,1)} %bitcast.21) | data formatting | bytes 1572864 | tf_op jit(solution)/shard_map/all_to_all | solution.py:21
  103.1 3.6 %all_to_all.16 = bf16[12,256,2,64]{1,3,0,2:T(8,128)(2,1)} reshape(bf16[12,4,64,2,64]{2,1,4,0,3:T(4,128)(2,1)} %bitcast.22) | data formatting | bytes 1572864 | tf_op jit(solution)/shard_map/all_to_all | solution.py:21
  106.7 4.3 %bitcast_convert_fusion = bf16[256,2,2048]{2,0,1:T(8,128)(2,1)} fusion(bf16[12,256,2,64]{1,3,0,2:T(8,128)(2,1)} %all_to_all.16, bf16[12,64,2048]{2,1,0:T(8,128)(2,1)S(1)} %copy-done), kind=kOutput, calls=%fused_computation | convolution fusion | flops 1611661312 | bytes 6029312 | tf_op jit(solution)/shard_map/gjwi,gip->jwp/dot_general | solution.py:23
  111.0 0.0 reduce-scatter.3.cloned.1.call-update
  111.0 0.0 reduce-scatter.5.cloned.1.call-start
  111.1 29.2 %reduce-scatter.3.cloned.1.call-done = bf16[64,2,2048]{2,0,1:T(8,128)(2,1)} async-done(((bf16[256,2,2048]{2,0,1:T(8,128)(2,1)}), bf16[64,2,2048]{2,0,1:T(8,128)(2,1)}) %reduce-scatter.3.cloned.1.call-update) | async-done | bytes 524304 | tf_op jit(solution)/shard_map/reduce_scatter | solution.py:22
  140.2 2.1 %convert_element_type.11 = f32[64,2,2048]{2,0,1:T(8,128)} convert(bf16[64,2,2048]{2,0,1:T(8,128)(2,1)} %reduce-scatter.3.cloned.1.call-done) | non-fusion elementwise | flops 262144 | bytes 1572864 | tf_op jit(solution)/shard_map/convert_element_type | solution.py:29
  142.3 0.0 reduce-scatter.5.cloned.1.call-update
  142.4 27.5 %reduce-scatter.5.cloned.1.call-done = f32[64,2,512]{2,0,1:T(8,128)} async-done(((f32[64,2,2048]{2,0,1:T(8,128)}), f32[64,2,512]{2,0,1:T(8,128)}) %reduce-scatter.5.cloned.1.call-update) | async-done | bytes 262160 | tf_op jit(solution)/shard_map/reduce_scatter | solution.py:30
  169.9 1.0 broadcast_multiply_fusion
  170.8 0.9 copy.10
Async XLA Ops:
  6.5 56.6 %copy-start = (bf16[12,64,2048]{2,1,0:T(8,128)(2,1)S(1)}, bf16[12,64,2048]{2,1,0:T(8,128)(2,1)}, u32[]{:S(2)}) copy-start(bf16[12,64,2048]{2,1,0:T(8,128)(2,1)} %param.2) | copy-start | bytes 9437188
  6.5 56.6 %all-gather.2.cloned.1.call-start = ((), (), s32[]{:S(2)}) async-start(), calls=%async_computation.3 | async-start | bytes 2621440 | tf_op jit(solution)/shard_map/all_gather | solution.py:17
  17.0 123.2 %reduce-scatter.3.cloned.1.call-start = ((), (), s32[]{:S(2)}) async-start(), calls=%async_computation.4 | async-start | bytes 2621440 | tf_op jit(solution)/shard_map/reduce_scatter | solution.py:22
  111.0 58.9 %reduce-scatter.5.cloned.1.call-start = ((), (), s32[]{:S(2)}) async-start(), calls=%async_computation.5 | async-start | bytes 1310720 | tf_op jit(solution)/shard_map/reduce_scatter | solution.py:30
Sparse Core Ops, SparseCore 0:
  17.2 45.9 all-gather.1
  111.1 29.0 reduce-scatter.2
  142.5 27.3 reduce-scatter.4
where the time goes:
time: 179 us; the launch traced here: 178 us
  waiting for transfers between devices  103 us (58%)
  blocking collectives  26.4 us (15%)
  local copies, waits for them, and re-layouts  24.2 us (14%)
  between operations  13.1 us (7%)
  matrix products  8.59 us (5%)
  other arithmetic  3.09 us (2%)
    all_gather x1, waiting for transfers between devices, local(): piece = lax.all_gather(green_all, 'chol', axis=2, tiled=True)  46.1 us
    reduce_scatter x1, waiting for transfers between devices, local(): lax.psum_scatter(jnp.einsum('gjwi,gip->jwp', swapped, chol_rot, preferred...  29.2 us
    reduce_scatter x1, waiting for transfers between devices, local(): lax.psum_scatter(occ_summed, 'chol', scatter_dimension=2, tiled=True)  27.5 us
    all_to_all x1, blocking collectives, local(): lax.all_to_all(pairs, 'occ', split_axis=3, concat_axis=1, tiled=True)  15.9 us
    all_gather x1, blocking collectives, local(): green_all = lax.all_gather(green, 'occ', axis=1, tiled=True)  10.5 us
    unnamed x4, local copies, waits for them, and re-layouts  8.02 us
    reshape x2, local copies, waits for them, and re-layouts, local(): pair_sum.astype(jnp.bfloat16).reshape(chol_loc, occ_loc, walkers, occupied)  7.95 us
    all_to_all x2, local copies, waits for them, and re-layouts, local(): lax.all_to_all(pairs, 'occ', split_axis=3, concat_axis=1, tiled=True)  7.37 us
  transfers between devices with their start and end apart: 3, of which 3 were waited for; matrix products, arithmetic and copies ran while one was open for 0% of the time, Pallas kernels for 0%

commit v1 on v0

v1 whole, which is shorter than its diff:
```python
import functools
import math

import jax
import jax.numpy as jnp
from jax import lax
from jax.experimental import pallas as pl
from jax.experimental.pallas import tpu as pltpu
from jax.sharding import PartitionSpec as P

BF16 = jnp.bfloat16
F32 = jnp.float32


def general(chol_rot, green):
    chol_loc, occ_loc, orbitals = chol_rot.shape
    walkers = green.shape[0]
    occupied = occ_loc * lax.axis_size("occ")
    nvec = chol_loc * lax.axis_size("chol")
    factor = -math.sqrt(orbitals / (nvec * occupied))
    vec_mat = chol_rot.reshape(chol_loc * occ_loc, orbitals)
    green_all = lax.all_gather(green, "occ", axis=1, tiled=True)
    piece = lax.all_gather(green_all, "chol", axis=2, tiled=True)
    flat = piece.reshape(-1, piece.shape[2])
    pair_sum = jnp.dot(vec_mat, flat.T, preferred_element_type=F32)
    pairs = pair_sum.astype(BF16).reshape(chol_loc, occ_loc, walkers, occupied)
    swapped = lax.all_to_all(pairs, "occ", split_axis=3, concat_axis=1, tiled=True)
    partial = jnp.einsum("gjwi,gip->jwp", swapped, chol_rot, preferred_element_type=F32)
    occ_summed = lax.psum_scatter(
        partial.astype(BF16), "occ", scatter_dimension=0, tiled=True
    ).astype(F32)
    summed = lax.psum_scatter(occ_summed, "chol", scatter_dimension=2, tiled=True)
    return summed * factor


def xor_permute(x, axis, bits):
    size = lax.axis_size(axis)
    return lax.ppermute(x, axis, [(i, i ^ bits) for i in range(size)])


def pair_kernel(walkers, occ_loc, vecs, blocks, where_ref, own_ref, sib_ref, *refs):
    green_refs, (near_ref, far_ref), flat = refs[: 2 * blocks], refs[2 * blocks : 2 * blocks + 2], refs[-1]
    width = flat.shape[1] // blocks
    rows = walkers * occ_loc

    @pl.when((pl.program_id(0) == 0) & (pl.program_id(1) == 0))
    def _():
        for side in range(2):
            for r in range(blocks):
                start = pl.multiple_of(where_ref[r] * width, width)
                flat[pl.ds(side * rows, rows), pl.ds(start, width)] = green_refs[side * blocks + r][...]

    def body(vec_ref):
        sums = lax.dot_general(
            vec_ref[...], flat[...], (((1,), (1,)), ((), ())), preferred_element_type=F32
        ).astype(BF16)
        for side, out_ref in enumerate((near_ref, far_ref)):
            for w in range(walkers):
                lane = side * rows + w * occ_loc
                tiles = [sums[g * occ_loc : (g + 1) * occ_loc, lane : lane + occ_loc] for g in range(vecs)]
                out_ref[0, w] = jnp.concatenate(tiles, axis=1)

    @pl.when(pl.program_id(0) == 0)
    def _():
        body(own_ref)

    @pl.when(pl.program_id(0) == 1)
    def _():
        body(sib_ref)


def pair_products(where, own, sib, greens, walkers, occ_loc, vecs):
    total, orbitals = own.shape
    chol_loc = total // occ_loc
    steps = chol_loc // vecs
    blocks = len(greens) // 2
    shape = jax.ShapeDtypeStruct((2, walkers, occ_loc, total), BF16)
    green_spec = pl.BlockSpec(greens[0].shape, lambda t, i, w: (0, 0))
    out_spec = pl.BlockSpec((1, walkers, occ_loc, vecs * occ_loc), lambda t, i, w: (t, 0, 0, i))
    return pl.pallas_call(
        functools.partial(pair_kernel, walkers, occ_loc, vecs, blocks),
        out_shape=(shape, shape),
        grid_spec=pltpu.PrefetchScalarGridSpec(
            num_scalar_prefetch=1,
            grid=(2, steps),
            in_specs=[
                pl.BlockSpec((vecs * occ_loc, orbitals), lambda t, i, w: (jnp.where(t == 0, i, steps - 1), 0)),
                pl.BlockSpec((vecs * occ_loc, orbitals), lambda t, i, w: (jnp.where(t == 0, 0, i), 0)),
            ]
            + [green_spec] * len(greens),
            out_specs=(out_spec, out_spec),
            scratch_shapes=[pltpu.VMEM((2 * walkers * occ_loc, orbitals), BF16)],
        ),
        cost_estimate=pl.CostEstimate(
            flops=2 * 2 * total * orbitals * 2 * walkers * occ_loc,
            bytes_accessed=4 * total * orbitals + 4 * walkers * occ_loc * orbitals + 4 * shape.size,
            transcendentals=0,
        ),
        compiler_params=pltpu.CompilerParams(vmem_limit_bytes=14 << 20),
        name="pairs",
    )(where, own, sib, *greens)


def partial_kernel(where_ref, near_ref, far_ref, vec_ref, keep_near_ref, keep_far_ref, send_ref):
    del where_ref
    rows = keep_near_ref.shape[0]
    for side, (left_ref, keep_ref) in enumerate(((near_ref, keep_near_ref), (far_ref, keep_far_ref))):
        sums = jnp.dot(left_ref[...], vec_ref[...], preferred_element_type=F32).astype(BF16)
        keep_ref[...] = sums[:rows]
        send_ref[pl.ds(side * rows, rows), :] = sums[rows:]


def partial_products(where, r, near, far, own, width):
    rows, total = near.shape
    half = rows // 2
    keep = jax.ShapeDtypeStruct((half, width), BF16)
    send = jax.ShapeDtypeStruct((rows, width), BF16)
    whole = lambda shape: pl.BlockSpec(shape, lambda i, w: (0, 0))
    return pl.pallas_call(
        partial_kernel,
        out_shape=(keep, keep, send),
        grid_spec=pltpu.PrefetchScalarGridSpec(
            num_scalar_prefetch=1,
            grid=(1,),
            in_specs=[whole(near.shape), whole(far.shape), pl.BlockSpec((total, width), lambda i, w: (0, w[r]))],
            out_specs=(whole(keep.shape), whole(keep.shape), whole(send.shape)),
        ),
        cost_estimate=pl.CostEstimate(
            flops=2 * 2 * rows * total * width,
            bytes_accessed=4 * rows * total + 2 * total * width + 4 * rows * width,
            transcendentals=0,
        ),
        compiler_params=pltpu.CompilerParams(vmem_limit_bytes=8 << 20),
        name="partial",
    )(where, near, far, own)


def finish_kernel(factor, first_ref, second_ref, third_ref, *refs):
    out_ref = refs[-1]
    occ_loc, walkers, _ = out_ref.shape
    total = first_ref[...].astype(F32) + second_ref[...].astype(F32) + third_ref[...].astype(F32)
    for ref in refs[:-1]:
        total = total + ref[...].astype(F32)
    total = total * factor
    for w in range(walkers):
        out_ref[:, w, :] = total[w * occ_loc : (w + 1) * occ_loc]


def relative(chol_rot, green):
    chol_loc, occ_loc, orbitals = chol_rot.shape
    walkers, _, width = green.shape
    n_chol = lax.axis_size("chol")
    occupied = occ_loc * lax.axis_size("occ")
    factor = -math.sqrt(orbitals / (chol_loc * n_chol * occupied))
    total = chol_loc * occ_loc
    rows = walkers * occ_loc
    vecs = max(v for v in (4, 2, 1) if chol_loc % v == 0)

    where = lax.axis_index("chol") ^ jnp.arange(n_chol, dtype=jnp.int32)
    own = chol_rot.reshape(total, orbitals)
    sib = xor_permute(own, "occ", 1)
    block = green.reshape(rows, width)
    near = [block] + [xor_permute(block, "chol", r) for r in range(1, n_chol)]
    far = [xor_permute(piece, "occ", 2) for piece in near]
    stay, leave = pair_products(where, own, sib, near + far, walkers, occ_loc, vecs)
    come = xor_permute(leave.reshape(2 * rows, total), "occ", 2)
    stay = stay.reshape(2 * rows, total)

    arrived = []
    for r in reversed(range(n_chol)):
        keep_near, keep_far, send = partial_products(where, r, stay, come, own, width)
        got = xor_permute(send, "occ", 1)
        over = (keep_far.astype(F32) + got[rows:].astype(F32)).astype(BF16)
        crossed = xor_permute(over, "occ", 2)
        if r:
            here = keep_near.astype(F32) + got[:rows].astype(F32) + crossed.astype(F32)
            arrived.append(xor_permute(here.astype(BF16), "chol", r))
        else:
            mine = (keep_near, got[:rows], crossed)

    return pl.pallas_call(
        functools.partial(finish_kernel, factor),
        out_shape=jax.ShapeDtypeStruct((occ_loc, walkers, width), F32),
        compiler_params=pltpu.CompilerParams(vmem_limit_bytes=4 << 20),
        name="finish",
    )(*mine, *arrived)


def local(chol_rot, green):
    occ_loc, width = chol_rot.shape[1], green.shape[2]
    n_chol = lax.axis_size("chol")
    fits = (
        lax.axis_size("occ") == 4
        and n_chol & (n_chol - 1) == 0
        and width % 128 == 0
        and occ_loc % 16 == 0
        and (chol_rot.shape[0] * occ_loc) % 128 == 0
    )
    return relative(chol_rot, green) if fits else general(chol_rot, green)


def solution(mesh):
    return jax.shard_map(
        local,
        mesh=mesh,
        in_specs=(P(("groups", "chol"), "occ", None), P("groups", "occ", "chol")),
        out_specs=P("occ", "groups", "chol"),
        check_vma=False,
    )
```

time: 179 us -> 70.7 us (0.39)
  waiting for transfers between devices: 103 us -> 33.8 us
  blocking collectives: 26.4 us -> 0 us
  starting transfers between devices: 0.09 us -> 22.9 us
  local copies, waits for them, and re-layouts: 24.2 us -> 2.8 us
  between operations: 13.1 us -> 0.12 us
  Pallas kernels: 0 us -> 10.7 us
  matrix products: 8.59 us -> 0 us
  other arithmetic: 3.09 us -> 0.29 us
    reduce_scatter x2 -> x0, waiting for transfers between devices: 56.7 us -> none  [the longest x1 29.2 us: local(): lax.psum_scatter(jnp.einsum('gjwi,gip->jwp', swapped, chol_rot, preferred...]
    all_gather x1 -> x0, waiting for transfers between devices: 46.1 us -> none  [local(): piece = lax.all_gather(green_all, 'chol', axis=2, tiled=True)]
    ppermute x0 -> x20, waiting for transfers between devices: none -> 33.8 us  [xor_permute(): return lax.ppermute(x, axis, [(i, i ^ bits) for i in range(size)])]
    ppermute x0 -> x20, starting transfers between devices: none -> 22.9 us  [xor_permute(): return lax.ppermute(x, axis, [(i, i ^ bits) for i in range(size)])]
    all_to_all x1 -> x0, blocking collectives: 15.9 us -> none  [local(): lax.all_to_all(pairs, 'occ', split_axis=3, concat_axis=1, tiled=True)]
    pallas_call x0 -> x6, Pallas kernels: none -> 10.7 us  [the longest x1 5.34 us: pair_products(): pl.pallas_call(functools.partial(pair_kernel, walkers, occ_loc, vecs, blo...]
    all_gather x1 -> x0, blocking collectives: 10.5 us -> none  [local(): green_all = lax.all_gather(green, 'occ', axis=1, tiled=True)]
    dot_general x2 -> x0, matrix products: 8.59 us -> none  [the longest x1 4.3 us: local(): pair_sum = jnp.dot(vec_mat, flat.T, preferred_element_type=jnp.float32)]
  transfers between devices with their start and end apart: 3 -> 20, of which waited for: 3 -> 9; matrix products, arithmetic and copies ran while one was open for 0% -> 0% of each run, Pallas kernels for 0% -> 5%
where the time goes in v1:
time: 70.7 us; the launch traced here: 70.5 us
  waiting for transfers between devices  33.8 us (48%)
  starting transfers between devices  22.9 us (32%)
  Pallas kernels  10.7 us (15%)
  local copies, waits for them, and re-layouts  2.8 us (4%)
    ppermute x20, waiting for transfers between devices, xor_permute(): return lax.ppermute(x, axis, [(i, i ^ bits) for i in range(size)])  33.8 us
    ppermute x20, starting transfers between devices, xor_permute(): return lax.ppermute(x, axis, [(i, i ^ bits) for i in range(size)])  22.9 us
    pallas_call x1, Pallas kernels, pair_products(): pl.pallas_call(functools.partial(pair_kernel, walkers, occ_loc, vecs, blo...  5.34 us
    pallas_call x4, Pallas kernels, partial_products(): pl.pallas_call(partial_kernel, out_shape=(keep, keep, send), grid_spec=pl...  4.47 us
    unnamed x4, local copies, waits for them, and re-layouts  2.79 us
  transfers between devices with their start and end apart: 20, of which 9 were waited for; matrix products, arithmetic and copies ran while one was open for 0% of the time, Pallas kernels for 5%

profile of v1, /device:TPU:0, one launch (start us, length us, event | category | flops | bytes accessed | tf_op | source)
XLA Modules:
  0.0 70.5 jit_solution(16656565906273626448)
XLA Ops:
  0.5 4.6 %collective-permute-start.3 = (bf16[128,512]{1,0:T(8,128)(2,1)}, bf16[128,512]{1,0:T(8,128)(2,1)S(1)}, u32[]{:S(2)}, u32[]{:S(2)}) collective-permute-start(bf16[128,512]{1,0:T(8,128)(2,1)} %bitcast.14), channel_id=1, source_target_pairs={{0,12},{4,8},{8,4},{12,0},{1,13},{5,9},{9,5},{13,1},{2,14},{6,10},... | collective-permute-start | bytes 393224 | tf_op jit(solution)/shard_map/ppermute | solution.py:38
  5.7 1.6 %collective-permute-start.4 = (bf16[128,512]{1,0:T(8,128)(2,1)}, bf16[128,512]{1,0:T(8,128)(2,1)}, u32[]{:S(2)}, u32[]{:S(2)}) collective-permute-start(bf16[128,512]{1,0:T(8,128)(2,1)} %bitcast.17), channel_id=1, source_target_pairs={{0,2},{1,3},{2,0},{3,1},{4,6},{5,7},{6,4},{7,5},{8,10},{9,11},{10,... | collective-permute-start | bytes 393224 | tf_op jit(solution)/shard_map/ppermute | solution.py:38
  7.4 2.4 %collective-permute-done.3.refs_3_ = bf16[128,512]{1,0:T(8,128)(2,1)S(1)} collective-permute-done((bf16[128,512]{1,0:T(8,128)(2,1)}, bf16[128,512]{1,0:T(8,128)(2,1)S(1)}, u32[]{:S(2)}, u32[]{:S(2)}) %collective-permute-start.3) | collective-permute-done | bytes 131104 | tf_op jit(solution)/shard_map/ppermute | solution.py:38
  9.7 1.7 %collective-permute-start.7 = (bf16[128,512]{1,0:T(8,128)(2,1)S(1)}, bf16[128,512]{1,0:T(8,128)(2,1)}, u32[]{:S(2)}, u32[]{:S(2)}) collective-permute-start(bf16[128,512]{1,0:T(8,128)(2,1)S(1)} %collective-permute-done.3.refs_3_), channel_id=1, source_target_pairs={{0,2},{1,3},{2,0},{3,1},{4,6},{5,7},{6,4},{7,5},{8,10},{9,11},{10,... | collective-permute-start | bytes 393224 | tf_op jit(solution)/shard_map/ppermute | solution.py:38
  11.5 5.6 %collective-permute-done.2.refs_2_ = bf16[128,512]{1,0:T(8,128)(2,1)S(1)} collective-permute-done((bf16[128,512]{1,0:T(8,128)(2,1)}, bf16[128,512]{1,0:T(8,128)(2,1)S(1)}, u32[]{:S(2)}, u32[]{:S(2)}) %collective-permute-start.2) | collective-permute-done | bytes 131104 | tf_op jit(solution)/shard_map/ppermute | solution.py:38
  17.0 1.5 %collective-permute-start.6 = (bf16[128,512]{1,0:T(8,128)(2,1)S(1)}, bf16[128,512]{1,0:T(8,128)(2,1)}, u32[]{:S(2)}, u32[]{:S(2)}) collective-permute-start(bf16[128,512]{1,0:T(8,128)(2,1)S(1)} %collective-permute-done.2.refs_2_), channel_id=1, source_target_pairs={{0,2},{1,3},{2,0},{3,1},{4,6},{5,7},{6,4},{7,5},{8,10},{9,11},{10,... | collective-permute-start | bytes 393224 | tf_op jit(solution)/shard_map/ppermute | solution.py:38
  19.1 4.4 %collective-permute-done.6.refs_6_ = bf16[128,512]{1,0:T(8,128)(2,1)} collective-permute-done((bf16[128,512]{1,0:T(8,128)(2,1)S(1)}, bf16[128,512]{1,0:T(8,128)(2,1)}, u32[]{:S(2)}, u32[]{:S(2)}) %collective-permute-start.6) | collective-permute-done | bytes 131104 | tf_op jit(solution)/shard_map/ppermute | solution.py:38
  23.5 1.5 %collective-permute-done.5.refs_5_ = bf16[128,512]{1,0:T(8,128)(2,1)} collective-permute-done((bf16[128,512]{1,0:T(8,128)(2,1)S(1)}, bf16[128,512]{1,0:T(8,128)(2,1)}, u32[]{:S(2)}, u32[]{:S(2)}) %collective-permute-start.5) | collective-permute-done | bytes 131104 | tf_op jit(solution)/shard_map/ppermute | solution.py:38
  25.0 1.9 %copy-done = bf16[12,64,2048]{2,1,0:T(8,128)(2,1)S(1)} copy-done((bf16[12,64,2048]{2,1,0:T(8,128)(2,1)S(1)}, bf16[12,64,2048]{2,1,0:T(8,128)(2,1)}, u32[]{:S(2)}) %copy-start) | copy-done | bytes 3145752
  27.8 5.3 %pairs.1 = (bf16[2,2,64,768]{3,2,1,0:T(8,128)(2,1)S(1)}, bf16[2,2,64,768]{3,2,1,0:T(8,128)(2,1)S(1)}) custom-call(s32[4]{0:T(128)S(1)} %iota_xor_fusion.where_ref, bf16[768,2048]{1,0:T(8,128)(2,1)S(1)} %bitcast.5, bf16[768,2048]{1,0:T(8,128)(2,1)S(1)} %collective-permute-done.sib_ref, bf16[128,512]{1,0:T(8,128)(2,1)S(1)} %bitcast.18, ...), custom_call_target="tpu_custom_call" | custom-call | flops 1610612736 | bytes 8126464 | tf_op jit(solution)/shard_map/pairs/pallas_call | solution.py:80
  33.1 1.6 %collective-permute-start.8 = (bf16[256,768]{1,0:T(8,128)(2,1)S(1)}, bf16[256,768]{1,0:T(8,128)(2,1)S(1)}, u32[]{:S(2)}, u32[]{:S(2)}) collective-permute-start(bf16[256,768]{1,0:T(8,128)(2,1)S(1)} %bitcast.19), channel_id=1, source_target_pairs={{0,2},{1,3},{2,0},{3,1},{4,6},{5,7},{6,4},{7,5},{8,10},{9,11},{10,... | collective-permute-start | bytes 1179656 | tf_op jit(solution)/shard_map/ppermute | solution.py:38
  34.7 8.3 %collective-permute-done.8.far_ref = bf16[256,768]{1,0:T(8,128)(2,1)S(1)} collective-permute-done((bf16[256,768]{1,0:T(8,128)(2,1)S(1)}, bf16[256,768]{1,0:T(8,128)(2,1)S(1)}, u32[]{:S(2)}, u32[]{:S(2)}) %collective-permute-start.8) | collective-permute-done | bytes 393248 | tf_op jit(solution)/shard_map/ppermute | solution.py:38
  43.0 1.1 %partial.7 = (bf16[128,512]{1,0:T(8,128)(2,1)S(1)}, bf16[128,512]{1,0:T(8,128)(2,1)S(1)}, bf16[256,512]{1,0:T(8,128)(2,1)S(1)}) custom-call(s32[4]{0:T(128)S(1)} %iota_xor_fusion.where_ref, bf16[256,768]{1,0:T(8,128)(2,1)S(1)} %bitcast.10, bf16[256,768]{1,0:T(8,128)(2,1)S(1)} %collective-permute-done.8.far_ref, bf16[768,2048]{1,0:T(8,128)(2,1)S(1)} %bitcast.6), custom_call_target="tpu_custom_call" | custom-call | flops 402653184 | bytes 2097152 | tf_op jit(solution)/shard_map/partial/pallas_call | solution.py:119
  44.2 1.1 %partial.6 = (bf16[128,512]{1,0:T(8,128)(2,1)S(1)}, bf16[128,512]{1,0:T(8,128)(2,1)S(1)}, bf16[256,512]{1,0:T(8,128)(2,1)S(1)}) custom-call(s32[4]{0:T(128)S(1)} %iota_xor_fusion.where_ref, bf16[256,768]{1,0:T(8,128)(2,1)S(1)} %bitcast.11, bf16[256,768]{1,0:T(8,128)(2,1)S(1)} %collective-permute-done.8.far_ref, bf16[768,2048]{1,0:T(8,128)(2,1)S(1)} %bitcast.7), custom_call_target="tpu_custom_call" | custom-call | flops 402653184 | bytes 2097152 | tf_op jit(solution)/shard_map/partial/pallas_call | solution.py:119
  45.9 1.1 %partial.5 = (bf16[128,512]{1,0:T(8,128)(2,1)S(1)}, bf16[128,512]{1,0:T(8,128)(2,1)S(1)}, bf16[256,512]{1,0:T(8,128)(2,1)S(1)}) custom-call(s32[4]{0:T(128)S(1)} %iota_xor_fusion.where_ref, bf16[256,768]{1,0:T(8,128)(2,1)S(1)} %bitcast.12, bf16[256,768]{1,0:T(8,128)(2,1)S(1)} %collective-permute-done.8.far_ref, bf16[768,2048]{1,0:T(8,128)(2,1)S(1)} %bitcast.8), custom_call_target="tpu_custom_call" | custom-call | flops 402653184 | bytes 2097152 | tf_op jit(solution)/shard_map/partial/pallas_call | solution.py:119
  47.1 1.1 %partial.4 = (bf16[128,512]{1,0:T(8,128)(2,1)S(1)}, bf16[128,512]{1,0:T(8,128)(2,1)S(1)}, bf16[256,512]{1,0:T(8,128)(2,1)S(1)}) custom-call(s32[4]{0:T(128)S(1)} %iota_xor_fusion.where_ref, bf16[256,768]{1,0:T(8,128)(2,1)S(1)} %bitcast.13, bf16[256,768]{1,0:T(8,128)(2,1)S(1)} %collective-permute-done.8.far_ref, bf16[768,2048]{1,0:T(8,128)(2,1)S(1)} %bitcast.9), custom_call_target="tpu_custom_call" | custom-call | flops 402653184 | bytes 2097152 | tf_op jit(solution)/shard_map/partial/pallas_call | solution.py:119
  48.8 1.6 %collective-permute-start.18 = (bf16[128,512]{1,0:T(8,128)(2,1)S(1)}, bf16[128,512]{1,0:T(8,128)(2,1)S(1)}, u32[]{:S(2)}, u32[]{:S(2)}) collective-permute-start(bf16[128,512]{1,0:T(8,128)(2,1)S(1)} %add_convert_fusion.1), channel_id=1, source_target_pairs={{0,2},{1,3},{2,0},{3,1},{4,6},{5,7},{6,4},{7,5},{8,10},{9,11},{10,... | collective-permute-start | bytes 393224 | tf_op jit(solution)/shard_map/ppermute | solution.py:38
  51.1 1.6 %collective-permute-start.12 = (bf16[128,512]{1,0:T(8,128)(2,1)S(1)}, bf16[128,512]{1,0:T(8,128)(2,1)S(1)}, u32[]{:S(2)}, u32[]{:S(2)}) collective-permute-start(bf16[128,512]{1,0:T(8,128)(2,1)S(1)} %add_convert_fusion.5), channel_id=1, source_target_pairs={{0,2},{1,3},{2,0},{3,1},{4,6},{5,7},{6,4},{7,5},{8,10},{9,11},{10,... | collective-permute-start | bytes 393224 | tf_op jit(solution)/shard_map/ppermute | solution.py:38
  53.3 2.0 %collective-permute-done.18 = bf16[128,512]{1,0:T(8,128)(2,1)S(1)} collective-permute-done((bf16[128,512]{1,0:T(8,128)(2,1)S(1)}, bf16[128,512]{1,0:T(8,128)(2,1)S(1)}, u32[]{:S(2)}, u32[]{:S(2)}) %collective-permute-start.18) | collective-permute-done | bytes 131104 | tf_op jit(solution)/shard_map/ppermute | solution.py:38
  55.3 1.2 %collective-permute-start.19 = (bf16[128,512]{1,0:T(8,128)(2,1)S(1)}, bf16[128,512]{1,0:T(8,128)(2,1)S(1)}, u32[]{:S(2)}, u32[]{:S(2)}) collective-permute-start(bf16[128,512]{1,0:T(8,128)(2,1)S(1)} %add_convert_fusion), channel_id=1, source_target_pairs={{0,4},{4,0},{8,12},{12,8},{1,5},{5,1},{9,13},{13,9},{2,6},{6,2},{1... | collective-permute-start | bytes 393224 | tf_op jit(solution)/shard_map/ppermute | solution.py:38
  56.5 1.6 %collective-permute-done.15 = bf16[128,512]{1,0:T(8,128)(2,1)S(1)} collective-permute-done((bf16[128,512]{1,0:T(8,128)(2,1)S(1)}, bf16[128,512]{1,0:T(8,128)(2,1)S(1)}, u32[]{:S(2)}, u32[]{:S(2)}) %collective-permute-start.15) | collective-permute-done | bytes 131104 | tf_op jit(solution)/shard_map/ppermute | solution.py:38
  59.1 1.8 %collective-permute-done.12 = bf16[128,512]{1,0:T(8,128)(2,1)S(1)} collective-permute-done((bf16[128,512]{1,0:T(8,128)(2,1)S(1)}, bf16[128,512]{1,0:T(8,128)(2,1)S(1)}, u32[]{:S(2)}, u32[]{:S(2)}) %collective-permute-start.12) | collective-permute-done | bytes 131104 | tf_op jit(solution)/shard_map/ppermute | solution.py:38
  61.0 2.6 %collective-permute-start.13 = (bf16[128,512]{1,0:T(8,128)(2,1)S(1)}, bf16[128,512]{1,0:T(8,128)(2,1)S(1)}, u32[]{:S(2)}, u32[]{:S(2)}) collective-permute-start(bf16[128,512]{1,0:T(8,128)(2,1)S(1)} %add_convert_fusion.4), channel_id=1, source_target_pairs={{0,12},{4,8},{8,4},{12,0},{1,13},{5,9},{9,5},{13,1},{2,14},{6,10},... | collective-permute-start | bytes 393224 | tf_op jit(solution)/shard_map/ppermute | solution.py:38
  63.6 6.1 %collective-permute-done.16.refs_1_ = bf16[128,512]{1,0:T(8,128)(2,1)S(1)} collective-permute-done((bf16[128,512]{1,0:T(8,128)(2,1)S(1)}, bf16[128,512]{1,0:T(8,128)(2,1)S(1)}, u32[]{:S(2)}, u32[]{:S(2)}) %collective-permute-start.16) | collective-permute-done | bytes 131104 | tf_op jit(solution)/shard_map/ppermute | solution.py:38
  (35 shorter events, 7.1 us)
Async XLA Ops:
  0.0 25.0 %collective-permute-start = (bf16[768,2048]{1,0:T(8,128)(2,1)}, bf16[768,2048]{1,0:T(8,128)(2,1)S(1)}, u32[]{:S(2)}, u32[]{:S(2)}) collective-permute-start(bf16[768,2048]{1,0:T(8,128)(2,1)} %bitcast.4), channel_id=1, source_target_pairs={{0,1},{1,0},{2,3},{3,2},{4,5},{5,4},{6,7},{7,6},{8,9},{9,8},{10,11... | collective-permute-start | bytes 9437192 | tf_op jit(solution)/shard_map/ppermute | solution.py:38
  0.5 9.2 %collective-permute-start.3 = (bf16[128,512]{1,0:T(8,128)(2,1)}, bf16[128,512]{1,0:T(8,128)(2,1)S(1)}, u32[]{:S(2)}, u32[]{:S(2)}) collective-permute-start(bf16[128,512]{1,0:T(8,128)(2,1)} %bitcast.14), channel_id=1, source_target_pairs={{0,12},{4,8},{8,4},{12,0},{1,13},{5,9},{9,5},{13,1},{2,14},{6,10},... | collective-permute-start | bytes 393224 | tf_op jit(solution)/shard_map/ppermute | solution.py:38
  5.1 12.0 %collective-permute-start.2 = (bf16[128,512]{1,0:T(8,128)(2,1)}, bf16[128,512]{1,0:T(8,128)(2,1)S(1)}, u32[]{:S(2)}, u32[]{:S(2)}) collective-permute-start(bf16[128,512]{1,0:T(8,128)(2,1)} %bitcast.15), channel_id=1, source_target_pairs={{0,8},{4,12},{8,0},{12,4},{1,9},{5,13},{9,1},{13,5},{2,10},{6,14},... | collective-permute-start | bytes 393224 | tf_op jit(solution)/shard_map/ppermute | solution.py:38
  5.1 13.4 %collective-permute-start.1 = (bf16[128,512]{1,0:T(8,128)(2,1)}, bf16[128,512]{1,0:T(8,128)(2,1)S(1)}, u32[]{:S(2)}, u32[]{:S(2)}) collective-permute-start(bf16[128,512]{1,0:T(8,128)(2,1)} %bitcast.16), channel_id=1, source_target_pairs={{0,4},{4,0},{8,12},{12,8},{1,5},{5,1},{9,13},{13,9},{2,6},{6,2},{1... | collective-permute-start | bytes 393224 | tf_op jit(solution)/shard_map/ppermute | solution.py:38
  5.7 13.4 %collective-permute-start.4 = (bf16[128,512]{1,0:T(8,128)(2,1)}, bf16[128,512]{1,0:T(8,128)(2,1)}, u32[]{:S(2)}, u32[]{:S(2)}) collective-permute-start(bf16[128,512]{1,0:T(8,128)(2,1)} %bitcast.17), channel_id=1, source_target_pairs={{0,2},{1,3},{2,0},{3,1},{4,6},{5,7},{6,4},{7,5},{8,10},{9,11},{10,... | collective-permute-start | bytes 393224 | tf_op jit(solution)/shard_map/ppermute | solution.py:38
  9.7 9.3 %collective-permute-start.7 = (bf16[128,512]{1,0:T(8,128)(2,1)S(1)}, bf16[128,512]{1,0:T(8,128)(2,1)}, u32[]{:S(2)}, u32[]{:S(2)}) collective-permute-start(bf16[128,512]{1,0:T(8,128)(2,1)S(1)} %collective-permute-done.3.refs_3_), channel_id=1, source_target_pairs={{0,2},{1,3},{2,0},{3,1},{4,6},{5,7},{6,4},{7,5},{8,10},{9,11},{10,... | collective-permute-start | bytes 393224 | tf_op jit(solution)/shard_map/ppermute | solution.py:38
  17.0 6.5 %collective-permute-start.6 = (bf16[128,512]{1,0:T(8,128)(2,1)S(1)}, bf16[128,512]{1,0:T(8,128)(2,1)}, u32[]{:S(2)}, u32[]{:S(2)}) collective-permute-start(bf16[128,512]{1,0:T(8,128)(2,1)S(1)} %collective-permute-done.2.refs_2_), channel_id=1, source_target_pairs={{0,2},{1,3},{2,0},{3,1},{4,6},{5,7},{6,4},{7,5},{8,10},{9,11},{10,... | collective-permute-start | bytes 393224 | tf_op jit(solution)/shard_map/ppermute | solution.py:38
  18.5 6.5 %collective-permute-start.5 = (bf16[128,512]{1,0:T(8,128)(2,1)S(1)}, bf16[128,512]{1,0:T(8,128)(2,1)}, u32[]{:S(2)}, u32[]{:S(2)}) collective-permute-start(bf16[128,512]{1,0:T(8,128)(2,1)S(1)} %collective-permute-done.1.refs_1_), channel_id=1, source_target_pairs={{0,2},{1,3},{2,0},{3,1},{4,6},{5,7},{6,4},{7,5},{8,10},{9,11},{10,... | collective-permute-start | bytes 393224 | tf_op jit(solution)/shard_map/ppermute | solution.py:38
  25.0 1.9 %copy-start = (bf16[12,64,2048]{2,1,0:T(8,128)(2,1)S(1)}, bf16[12,64,2048]{2,1,0:T(8,128)(2,1)}, u32[]{:S(2)}) copy-start(bf16[12,64,2048]{2,1,0:T(8,128)(2,1)} %param.2) | copy-start | bytes 9437188
  26.9 0.9 %copy-start.1 = (bf16[2,64,512]{2,1,0:T(8,128)(2,1)S(1)}, bf16[2,64,512]{2,1,0:T(8,128)(2,1)}, u32[]{:S(2)}) copy-start(bf16[2,64,512]{2,1,0:T(8,128)(2,1)} %param.3) | copy-start | bytes 393220
  33.1 9.9 %collective-permute-start.8 = (bf16[256,768]{1,0:T(8,128)(2,1)S(1)}, bf16[256,768]{1,0:T(8,128)(2,1)S(1)}, u32[]{:S(2)}, u32[]{:S(2)}) collective-permute-start(bf16[256,768]{1,0:T(8,128)(2,1)S(1)} %bitcast.19), channel_id=1, source_target_pairs={{0,2},{1,3},{2,0},{3,1},{4,6},{5,7},{6,4},{7,5},{8,10},{9,11},{10,... | collective-permute-start | bytes 1179656 | tf_op jit(solution)/shard_map/ppermute | solution.py:38
  44.2 4.7 %collective-permute-start.17 = (bf16[256,512]{1,0:T(8,128)(2,1)S(1)}, bf16[256,512]{1,0:T(8,128)(2,1)S(1)}, u32[]{:S(2)}, u32[]{:S(2)}) collective-permute-start(bf16[256,512]{1,0:T(8,128)(2,1)S(1)} %get-tuple-element.31), channel_id=1, source_target_pairs={{0,1},{1,0},{2,3},{3,2},{4,5},{5,4},{6,7},{7,6},{8,9},{9,8},{10,11... | collective-permute-start | bytes 786440 | tf_op jit(solution)/shard_map/ppermute | solution.py:38
  45.4 5.1 %collective-permute-start.14 = (bf16[256,512]{1,0:T(8,128)(2,1)S(1)}, bf16[256,512]{1,0:T(8,128)(2,1)S(1)}, u32[]{:S(2)}, u32[]{:S(2)}) collective-permute-start(bf16[256,512]{1,0:T(8,128)(2,1)S(1)} %get-tuple-element.28), channel_id=1, source_target_pairs={{0,1},{1,0},{2,3},{3,2},{4,5},{5,4},{6,7},{7,6},{8,9},{9,8},{10,11... | collective-permute-start | bytes 786440 | tf_op jit(solution)/shard_map/ppermute | solution.py:38
  47.0 4.0 %collective-permute-start.11 = (bf16[256,512]{1,0:T(8,128)(2,1)S(1)}, bf16[256,512]{1,0:T(8,128)(2,1)S(1)}, u32[]{:S(2)}, u32[]{:S(2)}) collective-permute-start(bf16[256,512]{1,0:T(8,128)(2,1)S(1)} %get-tuple-element.25), channel_id=1, source_target_pairs={{0,1},{1,0},{2,3},{3,2},{4,5},{5,4},{6,7},{7,6},{8,9},{9,8},{10,11... | collective-permute-start | bytes 786440 | tf_op jit(solution)/shard_map/ppermute | solution.py:38
  48.2 4.4 %collective-permute-start.9 = (bf16[256,512]{1,0:T(8,128)(2,1)S(1)}, bf16[256,512]{1,0:T(8,128)(2,1)S(1)}, u32[]{:S(2)}, u32[]{:S(2)}) collective-permute-start(bf16[256,512]{1,0:T(8,128)(2,1)S(1)} %get-tuple-element.22), channel_id=1, source_target_pairs={{0,1},{1,0},{2,3},{3,2},{4,5},{5,4},{6,7},{7,6},{8,9},{9,8},{10,11... | collective-permute-start | bytes 786440 | tf_op jit(solution)/shard_map/ppermute | solution.py:38
  48.8 6.4 %collective-permute-start.18 = (bf16[128,512]{1,0:T(8,128)(2,1)S(1)}, bf16[128,512]{1,0:T(8,128)(2,1)S(1)}, u32[]{:S(2)}, u32[]{:S(2)}) collective-permute-start(bf16[128,512]{1,0:T(8,128)(2,1)S(1)} %add_convert_fusion.1), channel_id=1, source_target_pairs={{0,2},{1,3},{2,0},{3,1},{4,6},{5,7},{6,4},{7,5},{8,10},{9,11},{10,... | collective-permute-start | bytes 393224 | tf_op jit(solution)/shard_map/ppermute | solution.py:38
  50.4 7.6 %collective-permute-start.15 = (bf16[128,512]{1,0:T(8,128)(2,1)S(1)}, bf16[128,512]{1,0:T(8,128)(2,1)S(1)}, u32[]{:S(2)}, u32[]{:S(2)}) collective-permute-start(bf16[128,512]{1,0:T(8,128)(2,1)S(1)} %add_convert_fusion.3), channel_id=1, source_target_pairs={{0,2},{1,3},{2,0},{3,1},{4,6},{5,7},{6,4},{7,5},{8,10},{9,11},{10,... | collective-permute-start | bytes 393224 | tf_op jit(solution)/shard_map/ppermute | solution.py:38
  51.1 9.8 %collective-permute-start.12 = (bf16[128,512]{1,0:T(8,128)(2,1)S(1)}, bf16[128,512]{1,0:T(8,128)(2,1)S(1)}, u32[]{:S(2)}, u32[]{:S(2)}) collective-permute-start(bf16[128,512]{1,0:T(8,128)(2,1)S(1)} %add_convert_fusion.5), channel_id=1, source_target_pairs={{0,2},{1,3},{2,0},{3,1},{4,6},{5,7},{6,4},{7,5},{8,10},{9,11},{10,... | collective-permute-start | bytes 393224 | tf_op jit(solution)/shard_map/ppermute | solution.py:38
  52.7 10.9 %collective-permute-start.10 = (bf16[128,512]{1,0:T(8,128)(2,1)S(1)}, bf16[128,512]{1,0:T(8,128)(2,1)S(1)}, u32[]{:S(2)}, u32[]{:S(2)}) collective-permute-start(bf16[128,512]{1,0:T(8,128)(2,1)S(1)} %add_convert_fusion.6), channel_id=1, source_target_pairs={{0,2},{1,3},{2,0},{3,1},{4,6},{5,7},{6,4},{7,5},{8,10},{9,11},{10,... | collective-permute-start | bytes 393224 | tf_op jit(solution)/shard_map/ppermute | solution.py:38
  55.3 8.2 %collective-permute-start.19 = (bf16[128,512]{1,0:T(8,128)(2,1)S(1)}, bf16[128,512]{1,0:T(8,128)(2,1)S(1)}, u32[]{:S(2)}, u32[]{:S(2)}) collective-permute-start(bf16[128,512]{1,0:T(8,128)(2,1)S(1)} %add_convert_fusion), channel_id=1, source_target_pairs={{0,4},{4,0},{8,12},{12,8},{1,5},{5,1},{9,13},{13,9},{2,6},{6,2},{1... | collective-permute-start | bytes 393224 | tf_op jit(solution)/shard_map/ppermute | solution.py:38
  58.1 11.5 %collective-permute-start.16 = (bf16[128,512]{1,0:T(8,128)(2,1)S(1)}, bf16[128,512]{1,0:T(8,128)(2,1)S(1)}, u32[]{:S(2)}, u32[]{:S(2)}) collective-permute-start(bf16[128,512]{1,0:T(8,128)(2,1)S(1)} %add_convert_fusion.2), channel_id=1, source_target_pairs={{0,8},{4,12},{8,0},{12,4},{1,9},{5,13},{9,1},{13,5},{2,10},{6,14},... | collective-permute-start | bytes 393224 | tf_op jit(solution)/shard_map/ppermute | solution.py:38
  61.0 8.7 %collective-permute-start.13 = (bf16[128,512]{1,0:T(8,128)(2,1)S(1)}, bf16[128,512]{1,0:T(8,128)(2,1)S(1)}, u32[]{:S(2)}, u32[]{:S(2)}) collective-permute-start(bf16[128,512]{1,0:T(8,128)(2,1)S(1)} %add_convert_fusion.4), channel_id=1, source_target_pairs={{0,12},{4,8},{8,4},{12,0},{1,13},{5,9},{9,5},{13,1},{2,14},{6,10},... | collective-permute-start | bytes 393224 | tf_op jit(solution)/shard_map/ppermute | solution.py:38

commit v2 on v0

v2 whole, which is shorter than its diff:
```python
import functools
import math

import jax
import jax.numpy as jnp
from jax import lax
from jax.experimental import pallas as pl
from jax.experimental.pallas import tpu as pltpu
from jax.sharding import PartitionSpec as P


BF16 = jnp.bfloat16
F32 = jnp.float32


def general(chol_rot, green):
    chol_loc, occ_loc, orbitals = chol_rot.shape
    walkers = green.shape[0]
    occupied = occ_loc * lax.axis_size("occ")
    nvec = chol_loc * lax.axis_size("chol")
    factor = -math.sqrt(orbitals / (nvec * occupied))
    vec_mat = chol_rot.reshape(chol_loc * occ_loc, orbitals)
    green_all = lax.all_gather(green, "occ", axis=1, tiled=True)
    piece = lax.all_gather(green_all, "chol", axis=2, tiled=True)
    flat = piece.reshape(-1, piece.shape[2])
    pair_sum = jnp.dot(vec_mat, flat.T, preferred_element_type=F32)
    pairs = pair_sum.astype(BF16).reshape(chol_loc, occ_loc, walkers, occupied)
    swapped = lax.all_to_all(pairs, "occ", split_axis=3, concat_axis=1, tiled=True)
    partial = jnp.einsum("gjwi,gip->jwp", swapped, chol_rot, preferred_element_type=F32)
    occ_summed = lax.psum_scatter(
        partial.astype(BF16), "occ", scatter_dimension=0, tiled=True
    ).astype(F32)
    summed = lax.psum_scatter(occ_summed, "chol", scatter_dimension=2, tiled=True)
    return summed * factor


def xor_permute(x, axis, bits):
    size = lax.axis_size(axis)
    return lax.ppermute(x, axis, [(i, i ^ bits) for i in range(size)])


def after(x, earlier):
    return lax.optimization_barrier((x, earlier))[0]


VMEM = pl.BlockSpec(memory_space=pltpu.VMEM)
SMEM = pl.BlockSpec(memory_space=pltpu.SMEM)


def stage_kernel(from_ref, to_ref, sem):
    copy = pltpu.make_async_copy(from_ref, to_ref, sem)
    copy.start()
    copy.wait()


def stage(x):
    return pl.pallas_call(
        stage_kernel,
        out_shape=jax.ShapeDtypeStruct(x.shape, x.dtype),
        in_specs=[pl.BlockSpec(memory_space=pltpu.HBM)],
        out_specs=VMEM,
        scratch_shapes=[pltpu.SemaphoreType.DMA],
        compiler_params=pltpu.CompilerParams(vmem_limit_bytes=4 << 20),
        cost_estimate=pl.CostEstimate(flops=0, bytes_accessed=4 * x.size, transcendentals=0),
        name="stage",
    )(x)


def pair_kernel(walkers, occ_loc, blocks, where_ref, own_ref, sib_ref, *refs):
    green_refs, (near_ref, far_ref), flat = refs[: 2 * blocks], refs[2 * blocks : 2 * blocks + 2], refs[-1]
    width = flat.shape[1] // blocks
    rows = walkers * occ_loc
    for side in range(2):
        for r in range(blocks):
            start = pl.multiple_of((where_ref[0] ^ r) * width, width)
            flat[pl.ds(side * rows, rows), pl.ds(start, width)] = green_refs[side * blocks + r][...]
    for core, vec_ref in enumerate((own_ref, sib_ref)):
        sums = lax.dot_general(
            vec_ref[...], flat[...], (((1,), (1,)), ((), ())), preferred_element_type=F32
        ).astype(BF16)
        for side, out_ref in enumerate((near_ref, far_ref)):
            for w in range(walkers):
                lane = side * rows + w * occ_loc
                tiles = [
                    sums[start : start + occ_loc, lane : lane + occ_loc]
                    for start in range(0, sums.shape[0], occ_loc)
                ]
                first = core * rows + w * occ_loc
                out_ref[first : first + occ_loc, :] = jnp.concatenate(tiles, axis=1)


def pair_products(where, own, sib, greens, walkers, occ_loc):
    total, orbitals = own.shape
    rows = walkers * occ_loc
    shape = jax.ShapeDtypeStruct((2 * rows, total), BF16)
    return pl.pallas_call(
        functools.partial(pair_kernel, walkers, occ_loc, len(greens) // 2),
        out_shape=(shape, shape),
        in_specs=[SMEM] + [VMEM] * (2 + len(greens)),
        out_specs=(VMEM, VMEM),
        scratch_shapes=[pltpu.VMEM((2 * rows, orbitals), BF16)],
        compiler_params=pltpu.CompilerParams(vmem_limit_bytes=14 << 20),
        cost_estimate=pl.CostEstimate(
            flops=8 * total * orbitals * rows,
            bytes_accessed=4 * total * orbitals + 4 * rows * orbitals + 4 * shape.size,
            transcendentals=0,
        ),
        name="pairs",
    )(where, own, sib, *greens)


def partial_kernel(which, where_ref, left_ref, vec_ref, *refs):
    keep_refs, send_ref = refs[:-1], refs[-1]
    rows, width = keep_refs[0].shape
    for n, r in enumerate(which):
        start = pl.multiple_of((where_ref[0] ^ r) * width, width)
        sums = jnp.dot(left_ref[...], vec_ref[:, pl.ds(start, width)], preferred_element_type=F32).astype(BF16)
        keep_refs[n][...] = sums[:rows]
        send_ref[n * rows : (n + 1) * rows, :] = sums[rows:]


def partial_products(which, where, left, own, width):
    rows, total = left.shape
    half = rows // 2
    keep = jax.ShapeDtypeStruct((half, width), BF16)
    send = jax.ShapeDtypeStruct((half * len(which), width), BF16)
    call = pl.pallas_call(
        functools.partial(partial_kernel, which),
        out_shape=(keep,) * len(which) + (send,),
        in_specs=[SMEM, VMEM, VMEM],
        out_specs=(VMEM,) * (len(which) + 1),
        compiler_params=pltpu.CompilerParams(vmem_limit_bytes=10 << 20),
        cost_estimate=pl.CostEstimate(
            flops=2 * rows * total * width * len(which),
            bytes_accessed=2 * rows * total + 2 * total * width * len(which) + 2 * rows * width * len(which),
            transcendentals=0,
        ),
        name="partial",
    )
    *keeps, send = call(where, left, own)
    got = xor_permute(send, "occ", 1)
    return {r: (keeps[n], got[n * half : (n + 1) * half]) for n, r in enumerate(which)}


def finish_kernel(factor, *refs):
    out_ref = refs[-1]
    occ_loc, walkers, _ = out_ref.shape
    total = refs[0][...].astype(F32)
    for ref in refs[1:-1]:
        total = total + ref[...].astype(F32)
    total = total * factor
    for w in range(walkers):
        out_ref[:, w, :] = total[w * occ_loc : (w + 1) * occ_loc]


def relative(chol_rot, green):
    chol_loc, occ_loc, orbitals = chol_rot.shape
    walkers, _, width = green.shape
    n_chol = lax.axis_size("chol")
    occupied = occ_loc * lax.axis_size("occ")
    factor = -math.sqrt(orbitals / (chol_loc * n_chol * occupied))
    total = chol_loc * occ_loc
    rows = walkers * occ_loc

    where = lax.axis_index("chol").astype(jnp.int32).reshape(1)
    chol_rot, green = after(chol_rot, where), after(green, where)
    sib = xor_permute(chol_rot.reshape(total, orbitals), "occ", 1)
    own = stage(chol_rot.reshape(total, orbitals))
    near = {0: green.reshape(rows, width)}
    bit = n_chol // 2
    while bit:
        near |= {r | bit: xor_permute(piece, "chol", bit) for r, piece in near.items()}
        if bit * 2 == n_chol:
            near[bit] = after(near[bit], own)
        bit //= 2
    far = {r: xor_permute(near[r], "occ", 2) for r in range(n_chol)}
    greens = [side[r] for side in (near, far) for r in range(n_chol)]
    stay, leave = pair_products(where, own, sib, greens, walkers, occ_loc)
    come = xor_permute(leave, "occ", 2)

    order = tuple(reversed(range(n_chol)))
    half = (n_chol + 1) // 2
    here = partial_products(order, where, stay, own, width)
    come = after(come, here[0][0])
    there = partial_products(order[:half], where, come, own, width)
    there |= partial_products(order[half:], where, come, own, width)
    add = lambda pair: pair[0].astype(F32) + pair[1].astype(F32)
    arrived = []
    for r in order:
        crossed = xor_permute(add(there[r]).astype(BF16), "occ", 2)
        if r:
            if arrived:
                crossed = after(crossed, ready)
            ready = (add(here[r]) + crossed.astype(F32)).astype(BF16)
            arrived.append(xor_permute(ready, "chol", r))
        else:
            mine = (*here[r], crossed)

    return pl.pallas_call(
        functools.partial(finish_kernel, factor),
        out_shape=jax.ShapeDtypeStruct((occ_loc, walkers, width), F32),
        compiler_params=pltpu.CompilerParams(vmem_limit_bytes=4 << 20),
        name="finish",
    )(*mine, *arrived)


def local(chol_rot, green):
    occ_loc, width = chol_rot.shape[1], green.shape[2]
    n_chol = lax.axis_size("chol")
    fits = (
        lax.axis_size("occ") == 4
        and n_chol & (n_chol - 1) == 0
        and width % 128 == 0
        and occ_loc % 16 == 0
        and (chol_rot.shape[0] * occ_loc) % 128 == 0
    )
    return relative(chol_rot, green) if fits else general(chol_rot, green)


def solution(mesh):
    return jax.shard_map(
        local,
        mesh=mesh,
        in_specs=(P(("groups", "chol"), "occ", None), P("groups", "occ", "chol")),
        out_specs=P("occ", "groups", "chol"),
        check_vma=False,
    )
```

time: 179 us -> 66.7 us (0.37)
  waiting for transfers between devices: 103 us -> 36.7 us
  blocking collectives: 26.4 us -> 0 us
  starting transfers between devices: 0.09 us -> 22.4 us
  local copies, waits for them, and re-layouts: 24.2 us -> 1.9 us
  between operations: 13.1 us -> 0.11 us
  matrix products: 8.59 us -> 0 us
  Pallas kernels: 0 us -> 5.2 us
  other arithmetic: 3.09 us -> 0.29 us
    reduce_scatter x2 -> x0, waiting for transfers between devices: 56.7 us -> none  [the longest x1 29.2 us: local(): lax.psum_scatter(jnp.einsum('gjwi,gip->jwp', swapped, chol_rot, preferred...]
    all_gather x1 -> x0, waiting for transfers between devices: 46.1 us -> none  [local(): piece = lax.all_gather(green_all, 'chol', axis=2, tiled=True)]
    ppermute x0 -> x19, waiting for transfers between devices: none -> 36.7 us  [xor_permute(): return lax.ppermute(x, axis, [(i, i ^ bits) for i in range(size)])]
    ppermute x0 -> x19, starting transfers between devices: none -> 22.4 us  [xor_permute(): return lax.ppermute(x, axis, [(i, i ^ bits) for i in range(size)])]
    all_to_all x1 -> x0, blocking collectives: 15.9 us -> none  [local(): lax.all_to_all(pairs, 'occ', split_axis=3, concat_axis=1, tiled=True)]
    all_gather x1 -> x0, blocking collectives: 10.5 us -> none  [local(): green_all = lax.all_gather(green, 'occ', axis=1, tiled=True)]
    dot_general x2 -> x0, matrix products: 8.59 us -> none  [the longest x1 4.3 us: local(): pair_sum = jnp.dot(vec_mat, flat.T, preferred_element_type=jnp.float32)]
    reshape x2 -> x0, local copies, waits for them, and re-layouts: 7.95 us -> none  [local(): pair_sum.astype(jnp.bfloat16).reshape(chol_loc, occ_loc, walkers, occupied)]
  transfers between devices with their start and end apart: 3 -> 19, of which waited for: 3 -> 11; matrix products, arithmetic and copies ran while one was open for 0% -> 0% of each run, Pallas kernels for 0% -> 3%
where the time goes in v2:
time: 66.7 us; the launch traced here: 66.6 us
  waiting for transfers between devices  36.7 us (55%)
  starting transfers between devices  22.4 us (34%)
  Pallas kernels  5.2 us (8%)
  local copies, waits for them, and re-layouts  1.9 us (3%)
    ppermute x19, waiting for transfers between devices, xor_permute(): return lax.ppermute(x, axis, [(i, i ^ bits) for i in range(size)])  36.7 us
    ppermute x19, starting transfers between devices, xor_permute(): return lax.ppermute(x, axis, [(i, i ^ bits) for i in range(size)])  22.4 us
    pallas_call x3, Pallas kernels, partial_products(): *keeps, send = call(where, left, own)  2.15 us
    pallas_call x1, Pallas kernels, pair_products(): pl.pallas_call(functools.partial(pair_kernel, walkers, occ_loc, len(green...  1.98 us
    unnamed x4, local copies, waits for them, and re-layouts  1.89 us
  transfers between devices with their start and end apart: 19, of which 11 were waited for; matrix products, arithmetic and copies ran while one was open for 0% of the time, Pallas kernels for 3%

profile of v2, /device:TPU:0, one launch (start us, length us, event | category | flops | bytes accessed | tf_op | source)
XLA Modules:
  0.0 66.6 jit_solution(18391483589982394097)
XLA Ops:
  0.5 3.6 %collective-permute-start.2 = (bf16[128,512]{1,0:T(8,128)(2,1)}, bf16[128,512]{1,0:T(8,128)(2,1)S(1)}, u32[]{:S(2)}, u32[]{:S(2)}) collective-permute-start(bf16[128,512]{1,0:T(8,128)(2,1)} %bitcast.5), channel_id=1, source_target_pairs={{0,8},{4,12},{8,0},{12,4},{1,9},{5,13},{9,1},{13,5},{2,10},{6,14},... | collective-permute-start | bytes 393224 | tf_op jit(solution)/shard_map/ppermute | solution.py:39
  4.1 1.6 %collective-permute-start.1 = (bf16[128,512]{1,0:T(8,128)(2,1)}, bf16[128,512]{1,0:T(8,128)(2,1)S(1)}, u32[]{:S(2)}, u32[]{:S(2)}) collective-permute-start(bf16[128,512]{1,0:T(8,128)(2,1)} %bitcast.6), channel_id=1, source_target_pairs={{0,4},{4,0},{8,12},{12,8},{1,5},{5,1},{9,13},{13,9},{2,6},{6,2},{1... | collective-permute-start | bytes 393224 | tf_op jit(solution)/shard_map/ppermute | solution.py:39
  5.6 1.9 %copy-done = bf16[12,64,2048]{2,1,0:T(8,128)(2,1)S(1)} copy-done((bf16[12,64,2048]{2,1,0:T(8,128)(2,1)S(1)}, bf16[12,64,2048]{2,1,0:T(8,128)(2,1)}, u32[]{:S(2)}) %copy-start) | copy-done | bytes 3145752
  7.8 3.6 %collective-permute-done.2.refs_2_ = bf16[128,512]{1,0:T(8,128)(2,1)S(1)} collective-permute-done((bf16[128,512]{1,0:T(8,128)(2,1)}, bf16[128,512]{1,0:T(8,128)(2,1)S(1)}, u32[]{:S(2)}, u32[]{:S(2)}) %collective-permute-start.2) | collective-permute-done | bytes 131104 | tf_op jit(solution)/shard_map/ppermute | solution.py:39
  12.1 1.5 %collective-permute-start.4 = (bf16[128,512]{1,0:T(8,128)(2,1)S(1)}, bf16[128,512]{1,0:T(8,128)(2,1)S(1)}, u32[]{:S(2)}, u32[]{:S(2)}) collective-permute-start(bf16[128,512]{1,0:T(8,128)(2,1)S(1)} %bitcast.7), channel_id=1, source_target_pairs={{0,2},{1,3},{2,0},{3,1},{4,6},{5,7},{6,4},{7,5},{8,10},{9,11},{10,... | collective-permute-start | bytes 393224 | tf_op jit(solution)/shard_map/ppermute | solution.py:39
  14.1 1.5 %collective-permute-start.5 = (bf16[128,512]{1,0:T(8,128)(2,1)S(1)}, bf16[128,512]{1,0:T(8,128)(2,1)S(1)}, u32[]{:S(2)}, u32[]{:S(2)}) collective-permute-start(bf16[128,512]{1,0:T(8,128)(2,1)S(1)} %collective-permute-done.1.refs_1_), channel_id=1, source_target_pairs={{0,2},{1,3},{2,0},{3,1},{4,6},{5,7},{6,4},{7,5},{8,10},{9,11},{10,... | collective-permute-start | bytes 393224 | tf_op jit(solution)/shard_map/ppermute | solution.py:39
  15.6 1.0 %collective-permute-done.3.refs_3_ = bf16[128,512]{1,0:T(8,128)(2,1)S(1)} collective-permute-done((bf16[128,512]{1,0:T(8,128)(2,1)S(1)}, bf16[128,512]{1,0:T(8,128)(2,1)S(1)}, u32[]{:S(2)}, u32[]{:S(2)}) %collective-permute-start.3) | collective-permute-done | bytes 131104 | tf_op jit(solution)/shard_map/ppermute | solution.py:39
  16.6 1.2 %collective-permute-start.7 = (bf16[128,512]{1,0:T(8,128)(2,1)S(1)}, bf16[128,512]{1,0:T(8,128)(2,1)S(1)}, u32[]{:S(2)}, u32[]{:S(2)}) collective-permute-start(bf16[128,512]{1,0:T(8,128)(2,1)S(1)} %collective-permute-done.3.refs_3_), channel_id=1, source_target_pairs={{0,2},{1,3},{2,0},{3,1},{4,6},{5,7},{6,4},{7,5},{8,10},{9,11},{10,... | collective-permute-start | bytes 393224 | tf_op jit(solution)/shard_map/ppermute | solution.py:39
  18.5 5.6 %collective-permute-done.5.refs_5_ = bf16[128,512]{1,0:T(8,128)(2,1)S(1)} collective-permute-done((bf16[128,512]{1,0:T(8,128)(2,1)S(1)}, bf16[128,512]{1,0:T(8,128)(2,1)S(1)}, u32[]{:S(2)}, u32[]{:S(2)}) %collective-permute-start.5) | collective-permute-done | bytes 131104 | tf_op jit(solution)/shard_map/ppermute | solution.py:39
  24.1 1.6 %collective-permute-done.7.refs_7_ = bf16[128,512]{1,0:T(8,128)(2,1)S(1)} collective-permute-done((bf16[128,512]{1,0:T(8,128)(2,1)S(1)}, bf16[128,512]{1,0:T(8,128)(2,1)S(1)}, u32[]{:S(2)}, u32[]{:S(2)}) %collective-permute-start.7) | collective-permute-done | bytes 131104 | tf_op jit(solution)/shard_map/ppermute | solution.py:39
  25.7 2.0 %pairs.1 = (bf16[256,768]{1,0:T(8,128)(2,1)S(1)}, bf16[256,768]{1,0:T(8,128)(2,1)S(1)}) custom-call(s32[1]{0:T(128)} %bitcast.where_ref, bf16[768,2048]{1,0:T(8,128)(2,1)S(1)} %stage.1.own_ref.vec_ref, bf16[768,2048]{1,0:T(8,128)(2,1)S(1)} %collective-permute-done.sib_ref, bf16[128,512]{1,0:T(8,128)(2,1)S(1)} %bitcast.8, ...), custom_call_target="tpu_custom_call" | custom-call | flops 1610612736 | bytes 8126464 | tf_op jit(solution)/shard_map/pairs/pallas_call | solution.py:96
  27.7 1.6 %collective-permute-start.9 = (bf16[256,768]{1,0:T(8,128)(2,1)S(1)}, bf16[256,768]{1,0:T(8,128)(2,1)S(1)}, u32[]{:S(2)}, u32[]{:S(2)}) collective-permute-start(bf16[256,768]{1,0:T(8,128)(2,1)S(1)} %get-tuple-element.30), channel_id=1, source_target_pairs={{0,2},{1,3},{2,0},{3,1},{4,6},{5,7},{6,4},{7,5},{8,10},{9,11},{10,... | collective-permute-start | bytes 1179656 | tf_op jit(solution)/shard_map/ppermute | solution.py:39
  29.3 1.0 %partial.3 = (bf16[128,512]{1,0:T(8,128)(2,1)S(1)}, bf16[128,512]{1,0:T(8,128)(2,1)S(1)}, bf16[128,512]{1,0:T(8,128)(2,1)S(1)}, bf16[128,512]{1,0:T(8,128)(2,1)S(1)}, bf16[512,512]{1,0:T(8,128)(2,1)S(1)}) custom-call(s32[1]{0:T(128)} %bitcast.where_ref, bf16[256,768]{1,0:T(8,128)(2,1)S(1)} %get-tuple-element.27.left_ref, ...), custom_call_target="tpu_custom_call" | custom-call | flops 805306368 | bytes 4587520 | tf_op jit(solution)/shard_map/partial/pallas_call | solution.py:140
  30.3 7.5 %collective-permute-done.9.left_ref = bf16[256,768]{1,0:T(8,128)(2,1)S(1)} collective-permute-done((bf16[256,768]{1,0:T(8,128)(2,1)S(1)}, bf16[256,768]{1,0:T(8,128)(2,1)S(1)}, u32[]{:S(2)}, u32[]{:S(2)}) %collective-permute-start.9) | collective-permute-done | bytes 393248 | tf_op jit(solution)/shard_map/ppermute | solution.py:39
  40.0 1.6 %collective-permute-start.15 = (bf16[128,512]{1,0:T(8,128)(2,1)S(1)}, bf16[128,512]{1,0:T(8,128)(2,1)S(1)}, u32[]{:S(2)}, u32[]{:S(2)}) collective-permute-start(bf16[128,512]{1,0:T(8,128)(2,1)S(1)} %get-tuple-element.45), channel_id=1, source_target_pairs={{0,2},{1,3},{2,0},{3,1},{4,6},{5,7},{6,4},{7,5},{8,10},{9,11},{10,... | collective-permute-start | bytes 393224 | tf_op jit(solution)/shard_map/ppermute | solution.py:39
  42.1 1.6 %collective-permute-start.17 = (bf16[128,512]{1,0:T(8,128)(2,1)S(1)}, bf16[128,512]{1,0:T(8,128)(2,1)S(1)}, u32[]{:S(2)}, u32[]{:S(2)}) collective-permute-start(bf16[128,512]{1,0:T(8,128)(2,1)S(1)} %get-tuple-element.43), channel_id=1, source_target_pairs={{0,2},{1,3},{2,0},{3,1},{4,6},{5,7},{6,4},{7,5},{8,10},{9,11},{10,... | collective-permute-start | bytes 393224 | tf_op jit(solution)/shard_map/ppermute | solution.py:39
  44.2 5.0 %collective-permute-done.13 = bf16[128,512]{1,0:T(8,128)(2,1)S(1)} collective-permute-done((bf16[128,512]{1,0:T(8,128)(2,1)S(1)}, bf16[128,512]{1,0:T(8,128)(2,1)S(1)}, u32[]{:S(2)}, u32[]{:S(2)}) %collective-permute-start.13) | collective-permute-done | bytes 131104 | tf_op jit(solution)/shard_map/ppermute | solution.py:39
  49.3 2.7 %collective-permute-done.17 = bf16[128,512]{1,0:T(8,128)(2,1)S(1)} collective-permute-done((bf16[128,512]{1,0:T(8,128)(2,1)S(1)}, bf16[128,512]{1,0:T(8,128)(2,1)S(1)}, u32[]{:S(2)}, u32[]{:S(2)}) %collective-permute-start.17) | collective-permute-done | bytes 131104 | tf_op jit(solution)/shard_map/ppermute | solution.py:39
  52.1 1.0 %collective-permute-start.18 = (bf16[128,512]{1,0:T(8,128)(2,1)S(1)}, bf16[128,512]{1,0:T(8,128)(2,1)S(1)}, u32[]{:S(2)}, u32[]{:S(2)}) collective-permute-start(bf16[128,512]{1,0:T(8,128)(2,1)S(1)} %add_convert_fusion), channel_id=1, source_target_pairs={{0,4},{4,0},{8,12},{12,8},{1,5},{5,1},{9,13},{13,9},{2,6},{6,2},{1... | collective-permute-start | bytes 393224 | tf_op jit(solution)/shard_map/ppermute | solution.py:39
  53.1 2.9 %collective-permute-start.16 = (bf16[128,512]{1,0:T(8,128)(2,1)S(1)}, bf16[128,512]{1,0:T(8,128)(2,1)S(1)}, u32[]{:S(2)}, u32[]{:S(2)}) collective-permute-start(bf16[128,512]{1,0:T(8,128)(2,1)S(1)} %add_convert_fusion.2), channel_id=1, source_target_pairs={{0,8},{4,12},{8,0},{12,4},{1,9},{5,13},{9,1},{13,5},{2,10},{6,14},... | collective-permute-start | bytes 393224 | tf_op jit(solution)/shard_map/ppermute | solution.py:39
  56.0 0.9 %collective-permute-start.14 = (bf16[128,512]{1,0:T(8,128)(2,1)S(1)}, bf16[128,512]{1,0:T(8,128)(2,1)S(1)}, u32[]{:S(2)}, u32[]{:S(2)}) collective-permute-start(bf16[128,512]{1,0:T(8,128)(2,1)S(1)} %add_convert_fusion.4), channel_id=1, source_target_pairs={{0,12},{4,8},{8,4},{12,0},{1,13},{5,9},{9,5},{13,1},{2,14},{6,10},... | collective-permute-start | bytes 393224 | tf_op jit(solution)/shard_map/ppermute | solution.py:39
  56.9 1.0 %collective-permute-done.18.refs_5_ = bf16[128,512]{1,0:T(8,128)(2,1)S(1)} collective-permute-done((bf16[128,512]{1,0:T(8,128)(2,1)S(1)}, bf16[128,512]{1,0:T(8,128)(2,1)S(1)}, u32[]{:S(2)}, u32[]{:S(2)}) %collective-permute-start.18) | collective-permute-done | bytes 131104 | tf_op jit(solution)/shard_map/ppermute | solution.py:39
  57.9 7.9 %collective-permute-done.16.refs_4_ = bf16[128,512]{1,0:T(8,128)(2,1)S(1)} collective-permute-done((bf16[128,512]{1,0:T(8,128)(2,1)S(1)}, bf16[128,512]{1,0:T(8,128)(2,1)S(1)}, u32[]{:S(2)}, u32[]{:S(2)}) %collective-permute-start.16) | collective-permute-done | bytes 131104 | tf_op jit(solution)/shard_map/ppermute | solution.py:39
  65.7 0.9 %finish.1 = f32[64,2,512]{2,1,0:T(2,128)} custom-call(bf16[128,512]{1,0:T(8,128)(2,1)S(1)} %get-tuple-element.28.refs_0_, bf16[128,512]{1,0:T(8,128)(2,1)S(1)} %slice.32.refs_1_, bf16[128,512]{1,0:T(8,128)(2,1)S(1)} %collective-permute-done.11.refs_2_, bf16[128,512]{1,0:T(8,128)(2,1)S(1)} %collective-permute-done.14.refs_3_, ...), custom_call_target="tpu_custom_call" | custom-call | tf_op jit(solution)/shard_map/finish/pallas_call | solution.py:199
  (30 shorter events, 6.1 us)
Async XLA Ops:
  0.0 25.7 %collective-permute-start = (bf16[768,2048]{1,0:T(8,128)(2,1)}, bf16[768,2048]{1,0:T(8,128)(2,1)S(1)}, u32[]{:S(2)}, u32[]{:S(2)}) collective-permute-start(bf16[768,2048]{1,0:T(8,128)(2,1)} %bitcast.3), channel_id=1, source_target_pairs={{0,1},{1,0},{2,3},{3,2},{4,5},{5,4},{6,7},{7,6},{8,9},{9,8},{10,11... | collective-permute-start | bytes 9437192 | tf_op jit(solution)/shard_map/ppermute | solution.py:39
  0.5 10.9 %collective-permute-start.2 = (bf16[128,512]{1,0:T(8,128)(2,1)}, bf16[128,512]{1,0:T(8,128)(2,1)S(1)}, u32[]{:S(2)}, u32[]{:S(2)}) collective-permute-start(bf16[128,512]{1,0:T(8,128)(2,1)} %bitcast.5), channel_id=1, source_target_pairs={{0,8},{4,12},{8,0},{12,4},{1,9},{5,13},{9,1},{13,5},{2,10},{6,14},... | collective-permute-start | bytes 393224 | tf_op jit(solution)/shard_map/ppermute | solution.py:39
  4.1 10.0 %collective-permute-start.1 = (bf16[128,512]{1,0:T(8,128)(2,1)}, bf16[128,512]{1,0:T(8,128)(2,1)S(1)}, u32[]{:S(2)}, u32[]{:S(2)}) collective-permute-start(bf16[128,512]{1,0:T(8,128)(2,1)} %bitcast.6), channel_id=1, source_target_pairs={{0,4},{4,0},{8,12},{12,8},{1,5},{5,1},{9,13},{13,9},{2,6},{6,2},{1... | collective-permute-start | bytes 393224 | tf_op jit(solution)/shard_map/ppermute | solution.py:39
  5.6 1.9 %copy-start = (bf16[12,64,2048]{2,1,0:T(8,128)(2,1)S(1)}, bf16[12,64,2048]{2,1,0:T(8,128)(2,1)}, u32[]{:S(2)}) copy-start(bf16[12,64,2048]{2,1,0:T(8,128)(2,1)} %param.2) | copy-start | bytes 9437188
  7.5 4.6 %copy-start.1 = (bf16[2,64,512]{2,1,0:T(8,128)(2,1)S(1)}, bf16[2,64,512]{2,1,0:T(8,128)(2,1)}, u32[]{:S(2)}) copy-start(bf16[2,64,512]{2,1,0:T(8,128)(2,1)} %param.3) | copy-start | bytes 393220
  11.4 5.3 %collective-permute-start.3 = (bf16[128,512]{1,0:T(8,128)(2,1)S(1)}, bf16[128,512]{1,0:T(8,128)(2,1)S(1)}, u32[]{:S(2)}, u32[]{:S(2)}) collective-permute-start(bf16[128,512]{1,0:T(8,128)(2,1)S(1)} %collective-permute-done.2.refs_2_), channel_id=1, source_target_pairs={{0,4},{4,0},{8,12},{12,8},{1,5},{5,1},{9,13},{13,9},{2,6},{6,2},{1... | collective-permute-start | bytes 393224 | tf_op jit(solution)/shard_map/ppermute | solution.py:39
  12.1 6.4 %collective-permute-start.4 = (bf16[128,512]{1,0:T(8,128)(2,1)S(1)}, bf16[128,512]{1,0:T(8,128)(2,1)S(1)}, u32[]{:S(2)}, u32[]{:S(2)}) collective-permute-start(bf16[128,512]{1,0:T(8,128)(2,1)S(1)} %bitcast.7), channel_id=1, source_target_pairs={{0,2},{1,3},{2,0},{3,1},{4,6},{5,7},{6,4},{7,5},{8,10},{9,11},{10,... | collective-permute-start | bytes 393224 | tf_op jit(solution)/shard_map/ppermute | solution.py:39
  13.6 10.5 %collective-permute-start.6 = (bf16[128,512]{1,0:T(8,128)(2,1)S(1)}, bf16[128,512]{1,0:T(8,128)(2,1)S(1)}, u32[]{:S(2)}, u32[]{:S(2)}) collective-permute-start(bf16[128,512]{1,0:T(8,128)(2,1)S(1)} %collective-permute-done.2.refs_2_), channel_id=1, source_target_pairs={{0,2},{1,3},{2,0},{3,1},{4,6},{5,7},{6,4},{7,5},{8,10},{9,11},{10,... | collective-permute-start | bytes 393224 | tf_op jit(solution)/shard_map/ppermute | solution.py:39
  14.1 10.0 %collective-permute-start.5 = (bf16[128,512]{1,0:T(8,128)(2,1)S(1)}, bf16[128,512]{1,0:T(8,128)(2,1)S(1)}, u32[]{:S(2)}, u32[]{:S(2)}) collective-permute-start(bf16[128,512]{1,0:T(8,128)(2,1)S(1)} %collective-permute-done.1.refs_1_), channel_id=1, source_target_pairs={{0,2},{1,3},{2,0},{3,1},{4,6},{5,7},{6,4},{7,5},{8,10},{9,11},{10,... | collective-permute-start | bytes 393224 | tf_op jit(solution)/shard_map/ppermute | solution.py:39
  16.6 9.1 %collective-permute-start.7 = (bf16[128,512]{1,0:T(8,128)(2,1)S(1)}, bf16[128,512]{1,0:T(8,128)(2,1)S(1)}, u32[]{:S(2)}, u32[]{:S(2)}) collective-permute-start(bf16[128,512]{1,0:T(8,128)(2,1)S(1)} %collective-permute-done.3.refs_3_), channel_id=1, source_target_pairs={{0,2},{1,3},{2,0},{3,1},{4,6},{5,7},{6,4},{7,5},{8,10},{9,11},{10,... | collective-permute-start | bytes 393224 | tf_op jit(solution)/shard_map/ppermute | solution.py:39
  27.7 10.0 %collective-permute-start.9 = (bf16[256,768]{1,0:T(8,128)(2,1)S(1)}, bf16[256,768]{1,0:T(8,128)(2,1)S(1)}, u32[]{:S(2)}, u32[]{:S(2)}) collective-permute-start(bf16[256,768]{1,0:T(8,128)(2,1)S(1)} %get-tuple-element.30), channel_id=1, source_target_pairs={{0,2},{1,3},{2,0},{3,1},{4,6},{5,7},{6,4},{7,5},{8,10},{9,11},{10,... | collective-permute-start | bytes 1179656 | tf_op jit(solution)/shard_map/ppermute | solution.py:39
  38.3 1.6 %collective-permute-start.12 = (bf16[256,512]{1,0:T(8,128)(2,1)S(1)}, bf16[256,512]{1,0:T(8,128)(2,1)S(1)}, u32[]{:S(2)}, u32[]{:S(2)}) collective-permute-start(bf16[256,512]{1,0:T(8,128)(2,1)S(1)} %get-tuple-element.36), channel_id=1, source_target_pairs={{0,1},{1,0},{2,3},{3,2},{4,5},{5,4},{6,7},{7,6},{8,9},{9,8},{10,11... | collective-permute-start | bytes 786440 | tf_op jit(solution)/shard_map/ppermute | solution.py:39
  38.4 5.9 %collective-permute-start.8 = (bf16[512,512]{1,0:T(8,128)(2,1)S(1)}, bf16[512,512]{1,0:T(8,128)(2,1)S(1)}, u32[]{:S(2)}, u32[]{:S(2)}) collective-permute-start(bf16[512,512]{1,0:T(8,128)(2,1)S(1)} %get-tuple-element.29), channel_id=1, source_target_pairs={{0,1},{1,0},{2,3},{3,2},{4,5},{5,4},{6,7},{7,6},{8,9},{9,8},{10,11... | collective-permute-start | bytes 1572872 | tf_op jit(solution)/shard_map/ppermute | solution.py:39
  39.5 2.6 %collective-permute-start.10 = (bf16[256,512]{1,0:T(8,128)(2,1)S(1)}, bf16[256,512]{1,0:T(8,128)(2,1)S(1)}, u32[]{:S(2)}, u32[]{:S(2)}) collective-permute-start(bf16[256,512]{1,0:T(8,128)(2,1)S(1)} %get-tuple-element.33), channel_id=1, source_target_pairs={{0,1},{1,0},{2,3},{3,2},{4,5},{5,4},{6,7},{7,6},{8,9},{9,8},{10,11... | collective-permute-start | bytes 786440 | tf_op jit(solution)/shard_map/ppermute | solution.py:39
  40.0 9.3 %collective-permute-start.15 = (bf16[128,512]{1,0:T(8,128)(2,1)S(1)}, bf16[128,512]{1,0:T(8,128)(2,1)S(1)}, u32[]{:S(2)}, u32[]{:S(2)}) collective-permute-start(bf16[128,512]{1,0:T(8,128)(2,1)S(1)} %get-tuple-element.45), channel_id=1, source_target_pairs={{0,2},{1,3},{2,0},{3,1},{4,6},{5,7},{6,4},{7,5},{8,10},{9,11},{10,... | collective-permute-start | bytes 393224 | tf_op jit(solution)/shard_map/ppermute | solution.py:39
  41.5 7.7 %collective-permute-start.13 = (bf16[128,512]{1,0:T(8,128)(2,1)S(1)}, bf16[128,512]{1,0:T(8,128)(2,1)S(1)}, u32[]{:S(2)}, u32[]{:S(2)}) collective-permute-start(bf16[128,512]{1,0:T(8,128)(2,1)S(1)} %get-tuple-element.46), channel_id=1, source_target_pairs={{0,2},{1,3},{2,0},{3,1},{4,6},{5,7},{6,4},{7,5},{8,10},{9,11},{10,... | collective-permute-start | bytes 393224 | tf_op jit(solution)/shard_map/ppermute | solution.py:39
  42.1 9.9 %collective-permute-start.17 = (bf16[128,512]{1,0:T(8,128)(2,1)S(1)}, bf16[128,512]{1,0:T(8,128)(2,1)S(1)}, u32[]{:S(2)}, u32[]{:S(2)}) collective-permute-start(bf16[128,512]{1,0:T(8,128)(2,1)S(1)} %get-tuple-element.43), channel_id=1, source_target_pairs={{0,2},{1,3},{2,0},{3,1},{4,6},{5,7},{6,4},{7,5},{8,10},{9,11},{10,... | collective-permute-start | bytes 393224 | tf_op jit(solution)/shard_map/ppermute | solution.py:39
  43.7 13.2 %collective-permute-start.11 = (bf16[128,512]{1,0:T(8,128)(2,1)S(1)}, bf16[128,512]{1,0:T(8,128)(2,1)S(1)}, u32[]{:S(2)}, u32[]{:S(2)}) collective-permute-start(bf16[128,512]{1,0:T(8,128)(2,1)S(1)} %get-tuple-element.44), channel_id=1, source_target_pairs={{0,2},{1,3},{2,0},{3,1},{4,6},{5,7},{6,4},{7,5},{8,10},{9,11},{10,... | collective-permute-start | bytes 393224 | tf_op jit(solution)/shard_map/ppermute | solution.py:39
  52.1 5.8 %collective-permute-start.18 = (bf16[128,512]{1,0:T(8,128)(2,1)S(1)}, bf16[128,512]{1,0:T(8,128)(2,1)S(1)}, u32[]{:S(2)}, u32[]{:S(2)}) collective-permute-start(bf16[128,512]{1,0:T(8,128)(2,1)S(1)} %add_convert_fusion), channel_id=1, source_target_pairs={{0,4},{4,0},{8,12},{12,8},{1,5},{5,1},{9,13},{13,9},{2,6},{6,2},{1... | collective-permute-start | bytes 393224 | tf_op jit(solution)/shard_map/ppermute | solution.py:39
  53.1 12.7 %collective-permute-start.16 = (bf16[128,512]{1,0:T(8,128)(2,1)S(1)}, bf16[128,512]{1,0:T(8,128)(2,1)S(1)}, u32[]{:S(2)}, u32[]{:S(2)}) collective-permute-start(bf16[128,512]{1,0:T(8,128)(2,1)S(1)} %add_convert_fusion.2), channel_id=1, source_target_pairs={{0,8},{4,12},{8,0},{12,4},{1,9},{5,13},{9,1},{13,5},{2,10},{6,14},... | collective-permute-start | bytes 393224 | tf_op jit(solution)/shard_map/ppermute | solution.py:39
  56.0 9.7 %collective-permute-start.14 = (bf16[128,512]{1,0:T(8,128)(2,1)S(1)}, bf16[128,512]{1,0:T(8,128)(2,1)S(1)}, u32[]{:S(2)}, u32[]{:S(2)}) collective-permute-start(bf16[128,512]{1,0:T(8,128)(2,1)S(1)} %add_convert_fusion.4), channel_id=1, source_target_pairs={{0,12},{4,8},{8,4},{12,0},{1,13},{5,9},{9,5},{13,1},{2,14},{6,10},... | collective-permute-start | bytes 393224 | tf_op jit(solution)/shard_map/ppermute | solution.py:39

commit v3 on v2

--- a/solution.py
+++ b/solution.py
@@ -109,45 +109,43 @@
     )(where, own, sib, *greens)
 
 
-def partial_kernel(which, where_ref, left_ref, vec_ref, *refs):
-    keep_refs, send_ref = refs[:-1], refs[-1]
-    rows, width = keep_refs[0].shape
+def partial_kernel(which, where_ref, left_ref, vec_ref, keep_ref, send_ref):
+    width = keep_ref.shape[1]
+    rows = left_ref.shape[0] // 2
     for n, r in enumerate(which):
         start = pl.multiple_of((where_ref[0] ^ r) * width, width)
         sums = jnp.dot(left_ref[...], vec_ref[:, pl.ds(start, width)], preferred_element_type=F32).astype(BF16)
-        keep_refs[n][...] = sums[:rows]
+        keep_ref[n * rows : (n + 1) * rows, :] = sums[:rows]
         send_ref[n * rows : (n + 1) * rows, :] = sums[rows:]
 
 
 def partial_products(which, where, left, own, width):
     rows, total = left.shape
-    half = rows // 2
-    keep = jax.ShapeDtypeStruct((half, width), BF16)
-    send = jax.ShapeDtypeStruct((half * len(which), width), BF16)
+    out = jax.ShapeDtypeStruct((rows // 2 * len(which), width), BF16)
     call = pl.pallas_call(
         functools.partial(partial_kernel, which),
-        out_shape=(keep,) * len(which) + (send,),
+        out_shape=(out, out),
         in_specs=[SMEM, VMEM, VMEM],
-        out_specs=(VMEM,) * (len(which) + 1),
+        out_specs=(VMEM, VMEM),
         compiler_params=pltpu.CompilerParams(vmem_limit_bytes=10 << 20),
         cost_estimate=pl.CostEstimate(
-            flops=2 * rows * total * width * len(which),
-            bytes_accessed=2 * rows * total + 2 * total * width * len(which) + 2 * rows * width * len(which),
+            flops=4 * out.size * total,
+            bytes_accessed=2 * rows * total + 2 * total * width * len(which) + 4 * out.size,
             transcendentals=0,
         ),
         name="partial",
     )
-    *keeps, send = call(where, left, own)
-    got = xor_permute(send, "occ", 1)
-    return {r: (keeps[n], got[n * half : (n + 1) * half]) for n, r in enumerate(which)}
-
-
-def finish_kernel(factor, *refs):
+    keep, send = call(where, left, own)
+    return keep, xor_permute(send, "occ", 1)
+
+
+def finish_kernel(factor, keep_ref, got_ref, *refs):
     out_ref = refs[-1]
     occ_loc, walkers, _ = out_ref.shape
-    total = refs[0][...].astype(F32)
-    for ref in refs[1:-1]:
-        total = total + ref[...].astype(F32)
+    rows = walkers * occ_loc
+    total = keep_ref[-rows:].astype(F32) + got_ref[-rows:].astype(F32)
+    for ref in refs[:-1]:
+        total = total + ref[-rows:].astype(F32)
     total = total * factor
     for w in range(walkers):
         out_ref[:, w, :] = total[w * occ_loc : (w + 1) * occ_loc]
@@ -167,41 +165,63 @@
     sib = xor_permute(chol_rot.reshape(total, orbitals), "occ", 1)
     own = stage(chol_rot.reshape(total, orbitals))
     near = {0: green.reshape(rows, width)}
+    far = {0: xor_permute(near[0], "occ", 2)}
     bit = n_chol // 2
     while bit:
         near |= {r | bit: xor_permute(piece, "chol", bit) for r, piece in near.items()}
         if bit * 2 == n_chol:
             near[bit] = after(near[bit], own)
         bit //= 2
-    far = {r: xor_permute(near[r], "occ", 2) for r in range(n_chol)}
+    for r in range(1, n_chol):
+        if r == 1:
+            far[r] = xor_permute(far[0], "chol", r)
+        else:
+            far[r] = xor_permute(near[r], "occ", 2)
     greens = [side[r] for side in (near, far) for r in range(n_chol)]
     stay, leave = pair_products(where, own, sib, greens, walkers, occ_loc)
     come = xor_permute(leave, "occ", 2)
 
-    order = tuple(reversed(range(n_chol)))
-    half = (n_chol + 1) // 2
-    here = partial_products(order, where, stay, own, width)
-    come = after(come, here[0][0])
-    there = partial_products(order[:half], where, come, own, width)
-    there |= partial_products(order[half:], where, come, own, width)
-    add = lambda pair: pair[0].astype(F32) + pair[1].astype(F32)
-    arrived = []
-    for r in order:
-        crossed = xor_permute(add(there[r]).astype(BF16), "occ", 2)
-        if r:
-            if arrived:
-                crossed = after(crossed, ready)
-            ready = (add(here[r]) + crossed.astype(F32)).astype(BF16)
-            arrived.append(xor_permute(ready, "chol", r))
-        else:
-            mine = (*here[r], crossed)
+    odds = tuple(range(n_chol - 1, 0, -2))
+    evens = tuple(r - 1 for r in odds)
+
+    def part(x, n):
+        return x[n * rows : (n + 1) * rows].astype(F32)
+
+    near_keep, near_got = partial_products(odds + evens, where, stay, own, width)
+    half = len(odds) * rows
+    near_odd = (near_keep[:half].astype(F32) + near_got[:half].astype(F32)).astype(BF16)
+    come = after(come, near_odd)
+    near_came = xor_permute(near_odd, "chol", 1)
+    far = {}
+    for which in (odds[:1], odds[1:] + evens):
+        pair = partial_products(which, where, come, own, width)
+        far |= {r: part(pair[0], n) + part(pair[1], n) for n, r in enumerate(which)}
+    far |= {r - 1: far[r - 1] + xor_permute(far[r].astype(BF16), "chol", 1).astype(F32) for r in odds}
+    crossed = {r: xor_permute(far[r].astype(BF16), "occ", 2) for r in evens}
+    summed = {
+        r: part(near_keep, len(odds) + n) + part(near_got, len(odds) + n) + part(near_came, n)
+        + crossed[r].astype(F32)
+        for n, r in enumerate(evens) if r
+    }
+    came = []
+    bit = n_chol // 2
+    while bit > 1:
+        for r in evens:
+            if r & bit and r < 2 * bit:
+                moved = xor_permute(summed[r].astype(BF16), "chol", bit)
+                if r == bit:
+                    came.append(moved)
+                else:
+                    summed[r ^ bit] = summed[r ^ bit] + moved.astype(F32)
+        bit //= 2
 
     return pl.pallas_call(
         functools.partial(finish_kernel, factor),
         out_shape=jax.ShapeDtypeStruct((occ_loc, walkers, width), F32),
+        in_specs=[VMEM] * (4 + len(came)),
         compiler_params=pltpu.CompilerParams(vmem_limit_bytes=4 << 20),
         name="finish",
-    )(*mine, *arrived)
+    )(near_keep, near_got, near_came, crossed[0], *came)
 
 
 def local(chol_rot, green):
@@ -209,9 +229,11 @@
     n_chol = lax.axis_size("chol")
     fits = (
         lax.axis_size("occ") == 4
+        and n_chol > 1
         and n_chol & (n_chol - 1) == 0
         and width % 128 == 0
         and occ_loc % 16 == 0
+        and green.shape[0] * occ_loc % 32 == 0
         and (chol_rot.shape[0] * occ_loc) % 128 == 0
     )
     return relative(chol_rot, green) if fits else general(chol_rot, green)

time: 66.7 us -> 60.1 us (0.901)
  waiting for transfers between devices: 36.7 us -> 30.5 us
    ppermute x19 -> x18, waiting for transfers between devices: 36.7 us -> 30.5 us  [xor_permute(): return lax.ppermute(x, axis, [(i, i ^ bits) for i in range(size)])]
    ppermute x19 -> x18, starting transfers between devices: 22.4 us -> 22 us  [xor_permute(): return lax.ppermute(x, axis, [(i, i ^ bits) for i in range(size)])]
  transfers between devices with their start and end apart: 19 -> 18, of which waited for: 11 -> 10; matrix products, arithmetic and copies ran while one was open for 0% -> 1% of each run, Pallas kernels for 3% -> 2%
where the time goes in v3:
time: 60.1 us; the launch traced here: 59.9 us
  waiting for transfers between devices  30.5 us (51%)
  starting transfers between devices  22 us (37%)
  Pallas kernels  5.2 us (9%)
  local copies, waits for them, and re-layouts  1.89 us (3%)
    ppermute x18, waiting for transfers between devices, xor_permute(): return lax.ppermute(x, axis, [(i, i ^ bits) for i in range(size)])  30.5 us
    ppermute x18, starting transfers between devices, xor_permute(): return lax.ppermute(x, axis, [(i, i ^ bits) for i in range(size)])  22 us
    pallas_call x3, Pallas kernels, partial_products(): keep, send = call(where, left, own)  2.15 us
    pallas_call x1, Pallas kernels, pair_products(): pl.pallas_call(functools.partial(pair_kernel, walkers, occ_loc, len(green...  1.99 us
    unnamed x4, local copies, waits for them, and re-layouts  1.89 us
  transfers between devices with their start and end apart: 18, of which 10 were waited for; matrix products, arithmetic and copies ran while one was open for 1% of the time, Pallas kernels for 2%

profile of v3, /device:TPU:0, one launch (start us, length us, event | category | flops | bytes accessed | tf_op | source)
XLA Modules:
  0.0 59.9 jit_solution(2275539115444004655)
XLA Ops:
  0.5 3.6 %collective-permute-start.2 = (bf16[128,512]{1,0:T(8,128)(2,1)}, bf16[128,512]{1,0:T(8,128)(2,1)S(1)}, u32[]{:S(2)}, u32[]{:S(2)}) collective-permute-start(bf16[128,512]{1,0:T(8,128)(2,1)} %bitcast.5), channel_id=1, source_target_pairs={{0,8},{4,12},{8,0},{12,4},{1,9},{5,13},{9,1},{13,5},{2,10},{6,14},... | collective-permute-start | bytes 393224 | tf_op jit(solution)/shard_map/ppermute | solution.py:39
  4.1 1.5 %collective-permute-start.4 = (bf16[128,512]{1,0:T(8,128)(2,1)}, bf16[128,512]{1,0:T(8,128)(2,1)S(1)}, u32[]{:S(2)}, u32[]{:S(2)}) collective-permute-start(bf16[128,512]{1,0:T(8,128)(2,1)} %bitcast.6), channel_id=1, source_target_pairs={{0,2},{1,3},{2,0},{3,1},{4,6},{5,7},{6,4},{7,5},{8,10},{9,11},{10,... | collective-permute-start | bytes 393224 | tf_op jit(solution)/shard_map/ppermute | solution.py:39
  5.6 1.9 %copy-done = bf16[12,64,2048]{2,1,0:T(8,128)(2,1)S(1)} copy-done((bf16[12,64,2048]{2,1,0:T(8,128)(2,1)S(1)}, bf16[12,64,2048]{2,1,0:T(8,128)(2,1)}, u32[]{:S(2)}) %copy-start) | copy-done | bytes 3145752
  7.7 3.6 %collective-permute-done.2.refs_2_ = bf16[128,512]{1,0:T(8,128)(2,1)S(1)} collective-permute-done((bf16[128,512]{1,0:T(8,128)(2,1)}, bf16[128,512]{1,0:T(8,128)(2,1)S(1)}, u32[]{:S(2)}, u32[]{:S(2)}) %collective-permute-start.2) | collective-permute-done | bytes 131104 | tf_op jit(solution)/shard_map/ppermute | solution.py:39
  11.3 0.8 %collective-permute-start.3 = (bf16[128,512]{1,0:T(8,128)(2,1)S(1)}, bf16[128,512]{1,0:T(8,128)(2,1)S(1)}, u32[]{:S(2)}, u32[]{:S(2)}) collective-permute-start(bf16[128,512]{1,0:T(8,128)(2,1)S(1)} %collective-permute-done.2.refs_2_), channel_id=1, source_target_pairs={{0,4},{4,0},{8,12},{12,8},{1,5},{5,1},{9,13},{13,9},{2,6},{6,2},{1... | collective-permute-start | bytes 393224 | tf_op jit(solution)/shard_map/ppermute | solution.py:39
  12.1 1.2 %collective-permute-start.1 = (bf16[128,512]{1,0:T(8,128)(2,1)S(1)}, bf16[128,512]{1,0:T(8,128)(2,1)S(1)}, u32[]{:S(2)}, u32[]{:S(2)}) collective-permute-start(bf16[128,512]{1,0:T(8,128)(2,1)S(1)} %bitcast.7), channel_id=1, source_target_pairs={{0,4},{4,0},{8,12},{12,8},{1,5},{5,1},{9,13},{13,9},{2,6},{6,2},{1... | collective-permute-start | bytes 393224 | tf_op jit(solution)/shard_map/ppermute | solution.py:39
  13.3 1.5 %collective-permute-start.6 = (bf16[128,512]{1,0:T(8,128)(2,1)S(1)}, bf16[128,512]{1,0:T(8,128)(2,1)S(1)}, u32[]{:S(2)}, u32[]{:S(2)}) collective-permute-start(bf16[128,512]{1,0:T(8,128)(2,1)S(1)} %collective-permute-done.2.refs_2_), channel_id=1, source_target_pairs={{0,2},{1,3},{2,0},{3,1},{4,6},{5,7},{6,4},{7,5},{8,10},{9,11},{10,... | collective-permute-start | bytes 393224 | tf_op jit(solution)/shard_map/ppermute | solution.py:39
  15.6 2.0 %collective-permute-done.3.refs_3_ = bf16[128,512]{1,0:T(8,128)(2,1)S(1)} collective-permute-done((bf16[128,512]{1,0:T(8,128)(2,1)S(1)}, bf16[128,512]{1,0:T(8,128)(2,1)S(1)}, u32[]{:S(2)}, u32[]{:S(2)}) %collective-permute-start.3) | collective-permute-done | bytes 131104 | tf_op jit(solution)/shard_map/ppermute | solution.py:39
  17.6 1.5 %collective-permute-start.7 = (bf16[128,512]{1,0:T(8,128)(2,1)S(1)}, bf16[128,512]{1,0:T(8,128)(2,1)S(1)}, u32[]{:S(2)}, u32[]{:S(2)}) collective-permute-start(bf16[128,512]{1,0:T(8,128)(2,1)S(1)} %collective-permute-done.3.refs_3_), channel_id=1, source_target_pairs={{0,2},{1,3},{2,0},{3,1},{4,6},{5,7},{6,4},{7,5},{8,10},{9,11},{10,... | collective-permute-start | bytes 393224 | tf_op jit(solution)/shard_map/ppermute | solution.py:39
  19.2 1.3 %collective-permute-done.1.refs_1_ = bf16[128,512]{1,0:T(8,128)(2,1)S(1)} collective-permute-done((bf16[128,512]{1,0:T(8,128)(2,1)S(1)}, bf16[128,512]{1,0:T(8,128)(2,1)S(1)}, u32[]{:S(2)}, u32[]{:S(2)}) %collective-permute-start.1) | collective-permute-done | bytes 131104 | tf_op jit(solution)/shard_map/ppermute | solution.py:39
  20.4 1.8 %collective-permute-done.5.refs_5_ = bf16[128,512]{1,0:T(8,128)(2,1)S(1)} collective-permute-done((bf16[128,512]{1,0:T(8,128)(2,1)S(1)}, bf16[128,512]{1,0:T(8,128)(2,1)S(1)}, u32[]{:S(2)}, u32[]{:S(2)}) %collective-permute-start.5) | collective-permute-done | bytes 131104 | tf_op jit(solution)/shard_map/ppermute | solution.py:39
  22.6 2.0 %pairs.1 = (bf16[256,768]{1,0:T(8,128)(2,1)S(1)}, bf16[256,768]{1,0:T(8,128)(2,1)S(1)}) custom-call(s32[1]{0:T(128)} %bitcast.where_ref, bf16[768,2048]{1,0:T(8,128)(2,1)S(1)} %stage.1.own_ref.vec_ref, bf16[768,2048]{1,0:T(8,128)(2,1)S(1)} %collective-permute-done.sib_ref, bf16[128,512]{1,0:T(8,128)(2,1)S(1)} %bitcast.8, ...), custom_call_target="tpu_custom_call" | custom-call | flops 1610612736 | bytes 8126464 | tf_op jit(solution)/shard_map/pairs/pallas_call | solution.py:96
  24.6 1.0 %partial.3 = (bf16[512,512]{1,0:T(8,128)(2,1)S(1)}, bf16[512,512]{1,0:T(8,128)(2,1)S(1)}) custom-call(s32[1]{0:T(128)} %bitcast.where_ref, bf16[256,768]{1,0:T(8,128)(2,1)S(1)} %get-tuple-element.20.left_ref, bf16[768,2048]{1,0:T(8,128)(2,1)S(1)} %stage.1.own_ref.vec_ref), custom_call_target="tpu_custom_call" | custom-call | flops 805306368 | bytes 4587520 | tf_op jit(solution)/shard_map/partial/pallas_call | solution.py:138
  25.7 1.6 %collective-permute-start.10 = (bf16[256,768]{1,0:T(8,128)(2,1)S(1)}, bf16[256,768]{1,0:T(8,128)(2,1)S(1)}, u32[]{:S(2)}, u32[]{:S(2)}) collective-permute-start(bf16[256,768]{1,0:T(8,128)(2,1)S(1)} %get-tuple-element.23), channel_id=1, source_target_pairs={{0,2},{1,3},{2,0},{3,1},{4,6},{5,7},{6,4},{7,5},{8,10},{9,11},{10,... | collective-permute-start | bytes 1179656 | tf_op jit(solution)/shard_map/ppermute | solution.py:39
  27.6 9.5 %collective-permute-done.10.left_ref = bf16[256,768]{1,0:T(8,128)(2,1)S(1)} collective-permute-done((bf16[256,768]{1,0:T(8,128)(2,1)S(1)}, bf16[256,768]{1,0:T(8,128)(2,1)S(1)}, u32[]{:S(2)}, u32[]{:S(2)}) %collective-permute-start.10) | collective-permute-done | bytes 393248 | tf_op jit(solution)/shard_map/ppermute | solution.py:39
  39.0 0.9 %collective-permute-start.15 = (bf16[128,512]{1,0:T(8,128)(2,1)S(1)}, bf16[128,512]{1,0:T(8,128)(2,1)S(1)}, u32[]{:S(2)}, u32[]{:S(2)}) collective-permute-start(bf16[128,512]{1,0:T(8,128)(2,1)S(1)} %add_convert_fusion.3), channel_id=1, source_target_pairs={{0,4},{4,0},{8,12},{12,8},{1,5},{5,1},{9,13},{13,9},{2,6},{6,2},{1... | collective-permute-start | bytes 393224 | tf_op jit(solution)/shard_map/ppermute | solution.py:39
  39.9 1.2 %collective-permute-start.9 = (bf16[256,512]{1,0:T(8,128)(2,1)S(1)}, bf16[256,512]{1,0:T(8,128)(2,1)S(1)}, u32[]{:S(2)}, u32[]{:S(2)}) collective-permute-start(bf16[256,512]{1,0:T(8,128)(2,1)S(1)} %add_convert_fusion), channel_id=1, source_target_pairs={{0,4},{4,0},{8,12},{12,8},{1,5},{5,1},{9,13},{13,9},{2,6},{6,2},{1... | collective-permute-start | bytes 786440 | tf_op jit(solution)/shard_map/ppermute | solution.py:39
  41.1 4.3 %collective-permute-done.15 = bf16[128,512]{1,0:T(8,128)(2,1)S(1)} collective-permute-done((bf16[128,512]{1,0:T(8,128)(2,1)S(1)}, bf16[128,512]{1,0:T(8,128)(2,1)S(1)}, u32[]{:S(2)}, u32[]{:S(2)}) %collective-permute-start.15) | collective-permute-done | bytes 131104 | tf_op jit(solution)/shard_map/ppermute | solution.py:39
  45.6 1.6 %collective-permute-start.16 = (bf16[128,512]{1,0:T(8,128)(2,1)S(1)}, bf16[128,512]{1,0:T(8,128)(2,1)S(1)}, u32[]{:S(2)}, u32[]{:S(2)}) collective-permute-start(bf16[128,512]{1,0:T(8,128)(2,1)S(1)} %get-tuple-element.29), channel_id=1, source_target_pairs={{0,2},{1,3},{2,0},{3,1},{4,6},{5,7},{6,4},{7,5},{8,10},{9,11},{10,... | collective-permute-start | bytes 393224 | tf_op jit(solution)/shard_map/ppermute | solution.py:39
  48.0 3.1 %collective-permute-done.9.refs_0_ = bf16[256,512]{1,0:T(8,128)(2,1)S(1)} collective-permute-done((bf16[256,512]{1,0:T(8,128)(2,1)S(1)}, bf16[256,512]{1,0:T(8,128)(2,1)S(1)}, u32[]{:S(2)}, u32[]{:S(2)}) %collective-permute-start.9) | collective-permute-done | bytes 262176 | tf_op jit(solution)/shard_map/ppermute | solution.py:39
  51.2 2.2 %collective-permute-start.17 = (bf16[128,512]{1,0:T(8,128)(2,1)S(1)}, bf16[128,512]{1,0:T(8,128)(2,1)S(1)}, u32[]{:S(2)}, u32[]{:S(2)}) collective-permute-start(bf16[128,512]{1,0:T(8,128)(2,1)S(1)} %add_convert_fusion.1), channel_id=1, source_target_pairs={{0,8},{4,12},{8,0},{12,4},{1,9},{5,13},{9,1},{13,5},{2,10},{6,14},... | collective-permute-start | bytes 393224 | tf_op jit(solution)/shard_map/ppermute | solution.py:39
  53.4 1.6 %collective-permute-start.13 = (bf16[128,512]{1,0:T(8,128)(2,1)S(1)}, bf16[128,512]{1,0:T(8,128)(2,1)S(1)}, u32[]{:S(2)}, u32[]{:S(2)}) collective-permute-start(bf16[128,512]{1,0:T(8,128)(2,1)S(1)} %add_convert_fusion.4), channel_id=1, source_target_pairs={{0,2},{1,3},{2,0},{3,1},{4,6},{5,7},{6,4},{7,5},{8,10},{9,11},{10,... | collective-permute-start | bytes 393224 | tf_op jit(solution)/shard_map/ppermute | solution.py:39
  55.0 4.1 %collective-permute-done.17.refs_2_ = bf16[128,512]{1,0:T(8,128)(2,1)S(1)} collective-permute-done((bf16[128,512]{1,0:T(8,128)(2,1)S(1)}, bf16[128,512]{1,0:T(8,128)(2,1)S(1)}, u32[]{:S(2)}, u32[]{:S(2)}) %collective-permute-start.17) | collective-permute-done | bytes 131104 | tf_op jit(solution)/shard_map/ppermute | solution.py:39
  59.1 0.8 %finish.1 = f32[64,2,512]{2,1,0:T(2,128)} custom-call(bf16[512,512]{1,0:T(8,128)(2,1)S(1)} %get-tuple-element.21.keep_ref, bf16[512,512]{1,0:T(8,128)(2,1)S(1)} %collective-permute-done.8.got_ref, bf16[256,512]{1,0:T(8,128)(2,1)S(1)} %collective-permute-done.9.refs_0_, bf16[128,512]{1,0:T(8,128)(2,1)S(1)} %collective-permute-done.13.refs_1_, ...), custom_call_target="tpu_custom_call" | custom-call | tf_op jit(solution)/shard_map/finish/pallas_call | solution.py:218
  (27 shorter events, 5.2 us)
Async XLA Ops:
  0.0 22.6 %collective-permute-start = (bf16[768,2048]{1,0:T(8,128)(2,1)}, bf16[768,2048]{1,0:T(8,128)(2,1)S(1)}, u32[]{:S(2)}, u32[]{:S(2)}) collective-permute-start(bf16[768,2048]{1,0:T(8,128)(2,1)} %bitcast.3), channel_id=1, source_target_pairs={{0,1},{1,0},{2,3},{3,2},{4,5},{5,4},{6,7},{7,6},{8,9},{9,8},{10,11... | collective-permute-start | bytes 9437192 | tf_op jit(solution)/shard_map/ppermute | solution.py:39
  0.5 10.8 %collective-permute-start.2 = (bf16[128,512]{1,0:T(8,128)(2,1)}, bf16[128,512]{1,0:T(8,128)(2,1)S(1)}, u32[]{:S(2)}, u32[]{:S(2)}) collective-permute-start(bf16[128,512]{1,0:T(8,128)(2,1)} %bitcast.5), channel_id=1, source_target_pairs={{0,8},{4,12},{8,0},{12,4},{1,9},{5,13},{9,1},{13,5},{2,10},{6,14},... | collective-permute-start | bytes 393224 | tf_op jit(solution)/shard_map/ppermute | solution.py:39
  4.1 10.8 %collective-permute-start.4 = (bf16[128,512]{1,0:T(8,128)(2,1)}, bf16[128,512]{1,0:T(8,128)(2,1)S(1)}, u32[]{:S(2)}, u32[]{:S(2)}) collective-permute-start(bf16[128,512]{1,0:T(8,128)(2,1)} %bitcast.6), channel_id=1, source_target_pairs={{0,2},{1,3},{2,0},{3,1},{4,6},{5,7},{6,4},{7,5},{8,10},{9,11},{10,... | collective-permute-start | bytes 393224 | tf_op jit(solution)/shard_map/ppermute | solution.py:39
  5.6 1.9 %copy-start = (bf16[12,64,2048]{2,1,0:T(8,128)(2,1)S(1)}, bf16[12,64,2048]{2,1,0:T(8,128)(2,1)}, u32[]{:S(2)}) copy-start(bf16[12,64,2048]{2,1,0:T(8,128)(2,1)} %param.2) | copy-start | bytes 9437188
  7.5 4.6 %copy-start.1 = (bf16[2,64,512]{2,1,0:T(8,128)(2,1)S(1)}, bf16[2,64,512]{2,1,0:T(8,128)(2,1)}, u32[]{:S(2)}) copy-start(bf16[2,64,512]{2,1,0:T(8,128)(2,1)} %param.3) | copy-start | bytes 393220
  11.3 6.4 %collective-permute-start.3 = (bf16[128,512]{1,0:T(8,128)(2,1)S(1)}, bf16[128,512]{1,0:T(8,128)(2,1)S(1)}, u32[]{:S(2)}, u32[]{:S(2)}) collective-permute-start(bf16[128,512]{1,0:T(8,128)(2,1)S(1)} %collective-permute-done.2.refs_2_), channel_id=1, source_target_pairs={{0,4},{4,0},{8,12},{12,8},{1,5},{5,1},{9,13},{13,9},{2,6},{6,2},{1... | collective-permute-start | bytes 393224 | tf_op jit(solution)/shard_map/ppermute | solution.py:39
  12.1 8.3 %collective-permute-start.1 = (bf16[128,512]{1,0:T(8,128)(2,1)S(1)}, bf16[128,512]{1,0:T(8,128)(2,1)S(1)}, u32[]{:S(2)}, u32[]{:S(2)}) collective-permute-start(bf16[128,512]{1,0:T(8,128)(2,1)S(1)} %bitcast.7), channel_id=1, source_target_pairs={{0,4},{4,0},{8,12},{12,8},{1,5},{5,1},{9,13},{13,9},{2,6},{6,2},{1... | collective-permute-start | bytes 393224 | tf_op jit(solution)/shard_map/ppermute | solution.py:39
  13.3 8.9 %collective-permute-start.6 = (bf16[128,512]{1,0:T(8,128)(2,1)S(1)}, bf16[128,512]{1,0:T(8,128)(2,1)S(1)}, u32[]{:S(2)}, u32[]{:S(2)}) collective-permute-start(bf16[128,512]{1,0:T(8,128)(2,1)S(1)} %collective-permute-done.2.refs_2_), channel_id=1, source_target_pairs={{0,2},{1,3},{2,0},{3,1},{4,6},{5,7},{6,4},{7,5},{8,10},{9,11},{10,... | collective-permute-start | bytes 393224 | tf_op jit(solution)/shard_map/ppermute | solution.py:39
  14.8 7.4 %collective-permute-start.5 = (bf16[128,512]{1,0:T(8,128)(2,1)S(1)}, bf16[128,512]{1,0:T(8,128)(2,1)S(1)}, u32[]{:S(2)}, u32[]{:S(2)}) collective-permute-start(bf16[128,512]{1,0:T(8,128)(2,1)S(1)} %collective-permute-done.4.refs_4_), channel_id=1, source_target_pairs={{0,4},{4,0},{8,12},{12,8},{1,5},{5,1},{9,13},{13,9},{2,6},{6,2},{1... | collective-permute-start | bytes 393224 | tf_op jit(solution)/shard_map/ppermute | solution.py:39
  17.6 5.0 %collective-permute-start.7 = (bf16[128,512]{1,0:T(8,128)(2,1)S(1)}, bf16[128,512]{1,0:T(8,128)(2,1)S(1)}, u32[]{:S(2)}, u32[]{:S(2)}) collective-permute-start(bf16[128,512]{1,0:T(8,128)(2,1)S(1)} %collective-permute-done.3.refs_3_), channel_id=1, source_target_pairs={{0,2},{1,3},{2,0},{3,1},{4,6},{5,7},{6,4},{7,5},{8,10},{9,11},{10,... | collective-permute-start | bytes 393224 | tf_op jit(solution)/shard_map/ppermute | solution.py:39
  25.6 2.0 %collective-permute-start.8 = (bf16[512,512]{1,0:T(8,128)(2,1)S(1)}, bf16[512,512]{1,0:T(8,128)(2,1)S(1)}, u32[]{:S(2)}, u32[]{:S(2)}) collective-permute-start(bf16[512,512]{1,0:T(8,128)(2,1)S(1)} %get-tuple-element.22), channel_id=1, source_target_pairs={{0,1},{1,0},{2,3},{3,2},{4,5},{5,4},{6,7},{7,6},{8,9},{9,8},{10,11... | collective-permute-start | bytes 1572872 | tf_op jit(solution)/shard_map/ppermute | solution.py:39
  25.7 11.5 %collective-permute-start.10 = (bf16[256,768]{1,0:T(8,128)(2,1)S(1)}, bf16[256,768]{1,0:T(8,128)(2,1)S(1)}, u32[]{:S(2)}, u32[]{:S(2)}) collective-permute-start(bf16[256,768]{1,0:T(8,128)(2,1)S(1)} %get-tuple-element.23), channel_id=1, source_target_pairs={{0,2},{1,3},{2,0},{3,1},{4,6},{5,7},{6,4},{7,5},{8,10},{9,11},{10,... | collective-permute-start | bytes 1179656 | tf_op jit(solution)/shard_map/ppermute | solution.py:39
  37.6 1.4 %collective-permute-start.14 = (bf16[128,512]{1,0:T(8,128)(2,1)S(1)}, bf16[128,512]{1,0:T(8,128)(2,1)S(1)}, u32[]{:S(2)}, u32[]{:S(2)}) collective-permute-start(bf16[128,512]{1,0:T(8,128)(2,1)S(1)} %get-tuple-element.28), channel_id=1, source_target_pairs={{0,1},{1,0},{2,3},{3,2},{4,5},{5,4},{6,7},{7,6},{8,9},{9,8},{10,11... | collective-permute-start | bytes 393224 | tf_op jit(solution)/shard_map/ppermute | solution.py:39
  38.4 7.0 %collective-permute-start.11 = (bf16[384,512]{1,0:T(8,128)(2,1)S(1)}, bf16[384,512]{1,0:T(8,128)(2,1)S(1)}, u32[]{:S(2)}, u32[]{:S(2)}) collective-permute-start(bf16[384,512]{1,0:T(8,128)(2,1)S(1)} %get-tuple-element.26), channel_id=1, source_target_pairs={{0,1},{1,0},{2,3},{3,2},{4,5},{5,4},{6,7},{7,6},{8,9},{9,8},{10,11... | collective-permute-start | bytes 1179656 | tf_op jit(solution)/shard_map/ppermute | solution.py:39
  39.0 6.4 %collective-permute-start.15 = (bf16[128,512]{1,0:T(8,128)(2,1)S(1)}, bf16[128,512]{1,0:T(8,128)(2,1)S(1)}, u32[]{:S(2)}, u32[]{:S(2)}) collective-permute-start(bf16[128,512]{1,0:T(8,128)(2,1)S(1)} %add_convert_fusion.3), channel_id=1, source_target_pairs={{0,4},{4,0},{8,12},{12,8},{1,5},{5,1},{9,13},{13,9},{2,6},{6,2},{1... | collective-permute-start | bytes 393224 | tf_op jit(solution)/shard_map/ppermute | solution.py:39
  39.9 11.1 %collective-permute-start.9 = (bf16[256,512]{1,0:T(8,128)(2,1)S(1)}, bf16[256,512]{1,0:T(8,128)(2,1)S(1)}, u32[]{:S(2)}, u32[]{:S(2)}) collective-permute-start(bf16[256,512]{1,0:T(8,128)(2,1)S(1)} %add_convert_fusion), channel_id=1, source_target_pairs={{0,4},{4,0},{8,12},{12,8},{1,5},{5,1},{9,13},{13,9},{2,6},{6,2},{1... | collective-permute-start | bytes 786440 | tf_op jit(solution)/shard_map/ppermute | solution.py:39
  45.6 5.5 %collective-permute-start.16 = (bf16[128,512]{1,0:T(8,128)(2,1)S(1)}, bf16[128,512]{1,0:T(8,128)(2,1)S(1)}, u32[]{:S(2)}, u32[]{:S(2)}) collective-permute-start(bf16[128,512]{1,0:T(8,128)(2,1)S(1)} %get-tuple-element.29), channel_id=1, source_target_pairs={{0,2},{1,3},{2,0},{3,1},{4,6},{5,7},{6,4},{7,5},{8,10},{9,11},{10,... | collective-permute-start | bytes 393224 | tf_op jit(solution)/shard_map/ppermute | solution.py:39
  47.2 6.2 %collective-permute-start.12 = (bf16[128,512]{1,0:T(8,128)(2,1)S(1)}, bf16[128,512]{1,0:T(8,128)(2,1)S(1)}, u32[]{:S(2)}, u32[]{:S(2)}) collective-permute-start(bf16[128,512]{1,0:T(8,128)(2,1)S(1)} %get-tuple-element.30), channel_id=1, source_target_pairs={{0,4},{4,0},{8,12},{12,8},{1,5},{5,1},{9,13},{13,9},{2,6},{6,2},{1... | collective-permute-start | bytes 393224 | tf_op jit(solution)/shard_map/ppermute | solution.py:39
  51.2 7.9 %collective-permute-start.17 = (bf16[128,512]{1,0:T(8,128)(2,1)S(1)}, bf16[128,512]{1,0:T(8,128)(2,1)S(1)}, u32[]{:S(2)}, u32[]{:S(2)}) collective-permute-start(bf16[128,512]{1,0:T(8,128)(2,1)S(1)} %add_convert_fusion.1), channel_id=1, source_target_pairs={{0,8},{4,12},{8,0},{12,4},{1,9},{5,13},{9,1},{13,5},{2,10},{6,14},... | collective-permute-start | bytes 393224 | tf_op jit(solution)/shard_map/ppermute | solution.py:39
  53.4 5.7 %collective-permute-start.13 = (bf16[128,512]{1,0:T(8,128)(2,1)S(1)}, bf16[128,512]{1,0:T(8,128)(2,1)S(1)}, u32[]{:S(2)}, u32[]{:S(2)}) collective-permute-start(bf16[128,512]{1,0:T(8,128)(2,1)S(1)} %add_convert_fusion.4), channel_id=1, source_target_pairs={{0,2},{1,3},{2,0},{3,1},{4,6},{5,7},{6,4},{7,5},{8,10},{9,11},{10,... | collective-permute-start | bytes 393224 | tf_op jit(solution)/shard_map/ppermute | solution.py:39

commit v4 on v3

--- a/solution.py
+++ b/solution.py
@@ -66,47 +66,80 @@
     )(x)
 
 
+def store_pairs(out_ref, core, sums, walkers, occ_loc):
+    for w in range(walkers):
+        tiles = [
+            sums[start : start + occ_loc, w * occ_loc : (w + 1) * occ_loc]
+            for start in range(0, sums.shape[0], occ_loc)
+        ]
+        first = (core * walkers + w) * occ_loc
+        out_ref[first : first + occ_loc, :] = jnp.concatenate(tiles, axis=1)
+
+
+CONTRACT_LAST = (((1,), (1,)), ((), ()))
+
+
 def pair_kernel(walkers, occ_loc, blocks, where_ref, own_ref, sib_ref, *refs):
-    green_refs, (near_ref, far_ref), flat = refs[: 2 * blocks], refs[2 * blocks : 2 * blocks + 2], refs[-1]
+    green_refs, (near_ref, sums_ref, flat) = refs[: 2 * blocks - 1], refs[2 * blocks - 1 :]
     width = flat.shape[1] // blocks
     rows = walkers * occ_loc
-    for side in range(2):
-        for r in range(blocks):
-            start = pl.multiple_of((where_ref[0] ^ r) * width, width)
-            flat[pl.ds(side * rows, rows), pl.ds(start, width)] = green_refs[side * blocks + r][...]
+    total = own_ref.shape[0]
+    for n in range(2 * blocks):
+        side, r = divmod(n, blocks)
+        start = pl.multiple_of((where_ref[0] ^ r) * width, width)
+        piece = green_refs[n][...] if n < 2 * blocks - 1 else jnp.zeros((rows, width), BF16)
+        flat[pl.ds(side * rows, rows), pl.ds(start, width)] = piece
     for core, vec_ref in enumerate((own_ref, sib_ref)):
-        sums = lax.dot_general(
-            vec_ref[...], flat[...], (((1,), (1,)), ((), ())), preferred_element_type=F32
-        ).astype(BF16)
-        for side, out_ref in enumerate((near_ref, far_ref)):
-            for w in range(walkers):
-                lane = side * rows + w * occ_loc
-                tiles = [
-                    sums[start : start + occ_loc, lane : lane + occ_loc]
-                    for start in range(0, sums.shape[0], occ_loc)
-                ]
-                first = core * rows + w * occ_loc
-                out_ref[first : first + occ_loc, :] = jnp.concatenate(tiles, axis=1)
-
-
-def pair_products(where, own, sib, greens, walkers, occ_loc):
+        sums = lax.dot_general(vec_ref[...], flat[...], CONTRACT_LAST, preferred_element_type=F32)
+        store_pairs(near_ref, core, sums[:, :rows].astype(BF16), walkers, occ_loc)
+        sums_ref[core * total : (core + 1) * total, :] = sums[:, rows:]
+
+
+def last_pair_kernel(walkers, occ_loc, last, where_ref, own_ref, sib_ref, green_ref, sums_ref, far_ref):
+    width = green_ref.shape[1]
+    total = own_ref.shape[0]
+    start = pl.multiple_of((where_ref[0] ^ last) * width, width)
+    for core, vec_ref in enumerate((own_ref, sib_ref)):
+        sums = sums_ref[core * total : (core + 1) * total, :] + lax.dot_general(
+            vec_ref[:, pl.ds(start, width)], green_ref[...], CONTRACT_LAST, preferred_element_type=F32
+        )
+        store_pairs(far_ref, core, sums.astype(BF16), walkers, occ_loc)
+
+
+def pair_products(where, own, sib, near, far, walkers, occ_loc):
     total, orbitals = own.shape
     rows = walkers * occ_loc
-    shape = jax.ShapeDtypeStruct((2 * rows, total), BF16)
-    return pl.pallas_call(
-        functools.partial(pair_kernel, walkers, occ_loc, len(greens) // 2),
-        out_shape=(shape, shape),
-        in_specs=[SMEM] + [VMEM] * (2 + len(greens)),
+    blocks = len(near)
+    greens = [side[r] for side in (near, far) for r in range(blocks)]
+    pairs = jax.ShapeDtypeStruct((2 * rows, total), BF16)
+    sums = jax.ShapeDtypeStruct((2 * total, rows), F32)
+    flops = 8 * total * orbitals * rows
+    first = pl.pallas_call(
+        functools.partial(pair_kernel, walkers, occ_loc, blocks),
+        out_shape=(pairs, sums),
+        in_specs=[SMEM] + [VMEM] * (1 + 2 * blocks),
         out_specs=(VMEM, VMEM),
         scratch_shapes=[pltpu.VMEM((2 * rows, orbitals), BF16)],
         compiler_params=pltpu.CompilerParams(vmem_limit_bytes=14 << 20),
         cost_estimate=pl.CostEstimate(
-            flops=8 * total * orbitals * rows,
-            bytes_accessed=4 * total * orbitals + 4 * rows * orbitals + 4 * shape.size,
-            transcendentals=0,
+            flops=flops, bytes_accessed=4 * total * orbitals + 4 * rows * orbitals + 4 * sums.size, transcendentals=0
         ),
         name="pairs",
-    )(where, own, sib, *greens)
+    )
+    second = pl.pallas_call(
+        functools.partial(last_pair_kernel, walkers, occ_loc, blocks - 1),
+        out_shape=pairs,
+        in_specs=[SMEM] + [VMEM] * 4,
+        out_specs=VMEM,
+        compiler_params=pltpu.CompilerParams(vmem_limit_bytes=10 << 20),
+        cost_estimate=pl.CostEstimate(
+            flops=flops // (2 * blocks), bytes_accessed=4 * total * orbitals // blocks + 4 * sums.size, transcendentals=0
+        ),
+        name="last_pairs",
+    )
+    stay, begun = first(where, own, sib, *greens[:-1])
+    leave = second(where, own, sib, greens[-1], begun)
+    return stay, leave
 
 
 def partial_kernel(which, where_ref, left_ref, vec_ref, keep_ref, send_ref):
@@ -163,22 +196,19 @@
     where = lax.axis_index("chol").astype(jnp.int32).reshape(1)
     chol_rot, green = after(chol_rot, where), after(green, where)
     sib = xor_permute(chol_rot.reshape(total, orbitals), "occ", 1)
-    own = stage(chol_rot.reshape(total, orbitals))
     near = {0: green.reshape(rows, width)}
     far = {0: xor_permute(near[0], "occ", 2)}
+    own = stage(after(chol_rot.reshape(total, orbitals), far[0]))
     bit = n_chol // 2
     while bit:
         near |= {r | bit: xor_permute(piece, "chol", bit) for r, piece in near.items()}
-        if bit * 2 == n_chol:
-            near[bit] = after(near[bit], own)
         bit //= 2
     for r in range(1, n_chol):
-        if r == 1:
-            far[r] = xor_permute(far[0], "chol", r)
+        if r & 1:
+            far[r] = xor_permute(far[r - 1], "chol", 1)
         else:
             far[r] = xor_permute(near[r], "occ", 2)
-    greens = [side[r] for side in (near, far) for r in range(n_chol)]
-    stay, leave = pair_products(where, own, sib, greens, walkers, occ_loc)
+    stay, leave = pair_products(where, own, sib, near, far, walkers, occ_loc)
     come = xor_permute(leave, "occ", 2)
 
     odds = tuple(range(n_chol - 1, 0, -2))
@@ -187,10 +217,10 @@
     def part(x, n):
         return x[n * rows : (n + 1) * rows].astype(F32)
 
-    near_keep, near_got = partial_products(odds + evens, where, stay, own, width)
-    half = len(odds) * rows
-    near_odd = (near_keep[:half].astype(F32) + near_got[:half].astype(F32)).astype(BF16)
-    come = after(come, near_odd)
+    odd_keep, odd_got = partial_products(odds, where, stay, own, width)
+    near_keep, near_got = partial_products(evens, where, stay, own, width)
+    near_odd = (odd_keep.astype(F32) + odd_got.astype(F32)).astype(BF16)
+    come = after(come, (near_odd, near_keep))
     near_came = xor_permute(near_odd, "chol", 1)
     far = {}
     for which in (odds[:1], odds[1:] + evens):
@@ -199,7 +229,7 @@
     far |= {r - 1: far[r - 1] + xor_permute(far[r].astype(BF16), "chol", 1).astype(F32) for r in odds}
     crossed = {r: xor_permute(far[r].astype(BF16), "occ", 2) for r in evens}
     summed = {
-        r: part(near_keep, len(odds) + n) + part(near_got, len(odds) + n) + part(near_came, n)
+        r: part(near_keep, n) + part(near_got, n) + part(near_came, n)
         + crossed[r].astype(F32)
         for n, r in enumerate(evens) if r
     }

time: 60.1 us -> 62.7 us (1.043)
  waiting for transfers between devices: 30.5 us -> 35 us
  starting transfers between devices: 22 us -> 19.2 us
  Pallas kernels: 5.2 us -> 6 us
    ppermute x18 -> x19, waiting for transfers between devices: 30.5 us -> 35 us  [xor_permute(): return lax.ppermute(x, axis, [(i, i ^ bits) for i in range(size)])]
    ppermute x18 -> x19, starting transfers between devices: 22 us -> 19.2 us  [xor_permute(): return lax.ppermute(x, axis, [(i, i ^ bits) for i in range(size)])]
    pallas_call x1 -> x2, Pallas kernels: 1.99 us -> 2.63 us  [the longest x1 1.98 us: pair_products(): stay, begun = first(where, own, sib, *greens[:-1])]
    pallas_call x3 -> x4, Pallas kernels: 2.15 us -> 2.32 us  [partial_products(): keep, send = call(where, left, own)]
  transfers between devices with their start and end apart: 18 -> 19, of which waited for: 10 -> 8; matrix products, arithmetic and copies ran while one was open for 1% -> 0% of each run, Pallas kernels for 2% -> 8%
where the time goes in v4:
time: 62.7 us; the launch traced here: 62.6 us
  waiting for transfers between devices  35 us (56%)
  starting transfers between devices  19.2 us (31%)
  Pallas kernels  6 us (10%)
  local copies, waits for them, and re-layouts  1.89 us (3%)
    ppermute x19, waiting for transfers between devices, xor_permute(): return lax.ppermute(x, axis, [(i, i ^ bits) for i in range(size)])  35 us
    ppermute x19, starting transfers between devices, xor_permute(): return lax.ppermute(x, axis, [(i, i ^ bits) for i in range(size)])  19.2 us
    pallas_call x4, Pallas kernels, partial_products(): keep, send = call(where, left, own)  2.32 us
    pallas_call x1, Pallas kernels, pair_products(): stay, begun = first(where, own, sib, *greens[:-1])  1.98 us
    unnamed x4, local copies, waits for them, and re-layouts  1.89 us
  transfers between devices with their start and end apart: 19, of which 8 were waited for; matrix products, arithmetic and copies ran while one was open for 0% of the time, Pallas kernels for 8%

profile of v4, /device:TPU:0, one launch (start us, length us, event | category | flops | bytes accessed | tf_op | source)
XLA Modules:
  0.0 62.6 jit_solution(7288339144326314645)
XLA Ops:
  0.5 3.6 %collective-permute-start.3 = (bf16[128,512]{1,0:T(8,128)(2,1)}, bf16[128,512]{1,0:T(8,128)(2,1)S(1)}, u32[]{:S(2)}, u32[]{:S(2)}) collective-permute-start(bf16[128,512]{1,0:T(8,128)(2,1)} %bitcast.5), channel_id=1, source_target_pairs={{0,8},{4,12},{8,0},{12,4},{1,9},{5,13},{9,1},{13,5},{2,10},{6,14},... | collective-permute-start | bytes 393224 | tf_op jit(solution)/shard_map/ppermute | solution.py:39
  4.1 1.5 %collective-permute-start = (bf16[128,512]{1,0:T(8,128)(2,1)}, bf16[128,512]{1,0:T(8,128)(2,1)S(1)}, u32[]{:S(2)}, u32[]{:S(2)}) collective-permute-start(bf16[128,512]{1,0:T(8,128)(2,1)} %bitcast.6), channel_id=1, source_target_pairs={{0,2},{1,3},{2,0},{3,1},{4,6},{5,7},{6,4},{7,5},{8,10},{9,11},{10,... | collective-permute-start | bytes 393224 | tf_op jit(solution)/shard_map/ppermute | solution.py:39
  5.6 5.7 %collective-permute-done.3.refs_2_ = bf16[128,512]{1,0:T(8,128)(2,1)S(1)} collective-permute-done((bf16[128,512]{1,0:T(8,128)(2,1)}, bf16[128,512]{1,0:T(8,128)(2,1)S(1)}, u32[]{:S(2)}, u32[]{:S(2)}) %collective-permute-start.3) | collective-permute-done | bytes 131104 | tf_op jit(solution)/shard_map/ppermute | solution.py:39
  11.3 1.5 %collective-permute-start.6 = (bf16[128,512]{1,0:T(8,128)(2,1)S(1)}, bf16[128,512]{1,0:T(8,128)(2,1)S(1)}, u32[]{:S(2)}, u32[]{:S(2)}) collective-permute-start(bf16[128,512]{1,0:T(8,128)(2,1)S(1)} %collective-permute-done.3.refs_2_), channel_id=1, source_target_pairs={{0,2},{1,3},{2,0},{3,1},{4,6},{5,7},{6,4},{7,5},{8,10},{9,11},{10,... | collective-permute-start | bytes 393224 | tf_op jit(solution)/shard_map/ppermute | solution.py:39
  12.8 0.8 %collective-permute-start.2 = (bf16[128,512]{1,0:T(8,128)(2,1)}, bf16[128,512]{1,0:T(8,128)(2,1)S(1)}, u32[]{:S(2)}, u32[]{:S(2)}) collective-permute-start(bf16[128,512]{1,0:T(8,128)(2,1)} %bitcast.7), channel_id=1, source_target_pairs={{0,4},{4,0},{8,12},{12,8},{1,5},{5,1},{9,13},{13,9},{2,6},{6,2},{1... | collective-permute-start | bytes 393224 | tf_op jit(solution)/shard_map/ppermute | solution.py:39
  13.6 1.2 %collective-permute-start.4 = (bf16[128,512]{1,0:T(8,128)(2,1)S(1)}, bf16[128,512]{1,0:T(8,128)(2,1)S(1)}, u32[]{:S(2)}, u32[]{:S(2)}) collective-permute-start(bf16[128,512]{1,0:T(8,128)(2,1)S(1)} %collective-permute-done.3.refs_2_), channel_id=1, source_target_pairs={{0,4},{4,0},{8,12},{12,8},{1,5},{5,1},{9,13},{13,9},{2,6},{6,2},{1... | collective-permute-start | bytes 393224 | tf_op jit(solution)/shard_map/ppermute | solution.py:39
  14.8 0.8 %collective-permute-start.5 = (bf16[128,512]{1,0:T(8,128)(2,1)S(1)}, bf16[128,512]{1,0:T(8,128)(2,1)S(1)}, u32[]{:S(2)}, u32[]{:S(2)}) collective-permute-start(bf16[128,512]{1,0:T(8,128)(2,1)S(1)} %collective-permute-done.refs_4_), channel_id=1, source_target_pairs={{0,4},{4,0},{8,12},{12,8},{1,5},{5,1},{9,13},{13,9},{2,6},{6,2},{1... | collective-permute-start | bytes 393224 | tf_op jit(solution)/shard_map/ppermute | solution.py:39
  15.6 1.9 %copy-done = bf16[12,64,2048]{2,1,0:T(8,128)(2,1)S(1)} copy-done((bf16[12,64,2048]{2,1,0:T(8,128)(2,1)S(1)}, bf16[12,64,2048]{2,1,0:T(8,128)(2,1)}, u32[]{:S(2)}) %copy-start) | copy-done | bytes 3145752
  17.7 1.3 %collective-permute-start.10 = (bf16[128,512]{1,0:T(8,128)(2,1)S(1)}, bf16[128,512]{1,0:T(8,128)(2,1)S(1)}, u32[]{:S(2)}, u32[]{:S(2)}) collective-permute-start(bf16[128,512]{1,0:T(8,128)(2,1)S(1)} %collective-permute-done.6.refs_6_), channel_id=1, source_target_pairs={{0,4},{4,0},{8,12},{12,8},{1,5},{5,1},{9,13},{13,9},{2,6},{6,2},{1... | collective-permute-start | bytes 393224 | tf_op jit(solution)/shard_map/ppermute | solution.py:39
  19.4 2.8 %collective-permute-done.4.refs_3_ = bf16[128,512]{1,0:T(8,128)(2,1)S(1)} collective-permute-done((bf16[128,512]{1,0:T(8,128)(2,1)S(1)}, bf16[128,512]{1,0:T(8,128)(2,1)S(1)}, u32[]{:S(2)}, u32[]{:S(2)}) %collective-permute-start.4) | collective-permute-done | bytes 131104 | tf_op jit(solution)/shard_map/ppermute | solution.py:39
  22.2 2.6 %collective-permute-done.5.refs_5_ = bf16[128,512]{1,0:T(8,128)(2,1)S(1)} collective-permute-done((bf16[128,512]{1,0:T(8,128)(2,1)S(1)}, bf16[128,512]{1,0:T(8,128)(2,1)S(1)}, u32[]{:S(2)}, u32[]{:S(2)}) %collective-permute-start.5) | collective-permute-done | bytes 131104 | tf_op jit(solution)/shard_map/ppermute | solution.py:39
  24.8 2.0 %pairs.1 = (bf16[256,768]{1,0:T(8,128)(2,1)S(1)}, f32[1536,128]{1,0:T(8,128)S(1)}) custom-call(s32[1]{0:T(128)} %bitcast.where_ref, bf16[768,2048]{1,0:T(8,128)(2,1)S(1)} %stage.1.own_ref.vec_ref, bf16[768,2048]{1,0:T(8,128)(2,1)S(1)} %collective-permute-done.1.sib_ref, bf16[128,512]{1,0:T(8,128)(2,1)S(1)} %bitcast.8, ...), custom_call_target="tpu_custom_call" | custom-call | flops 1610612736 | bytes 8126464 | tf_op jit(solution)/shard_map/pairs/pallas_call | solution.py:140
  28.1 0.7 %collective-permute-start.11 = (bf16[256,768]{1,0:T(8,128)(2,1)S(1)}, bf16[256,768]{1,0:T(8,128)(2,1)S(1)}, u32[]{:S(2)}, u32[]{:S(2)}) collective-permute-start(bf16[256,768]{1,0:T(8,128)(2,1)S(1)} %last_pairs.1), channel_id=1, source_target_pairs={{0,2},{1,3},{2,0},{3,1},{4,6},{5,7},{6,4},{7,5},{8,10},{9,11},{10,... | collective-permute-start | bytes 1179656 | tf_op jit(solution)/shard_map/ppermute | solution.py:39
  29.5 10.2 %collective-permute-done.11.left_ref = bf16[256,768]{1,0:T(8,128)(2,1)S(1)} collective-permute-done((bf16[256,768]{1,0:T(8,128)(2,1)S(1)}, bf16[256,768]{1,0:T(8,128)(2,1)S(1)}, u32[]{:S(2)}, u32[]{:S(2)}) %collective-permute-start.11) | collective-permute-done | bytes 393248 | tf_op jit(solution)/shard_map/ppermute | solution.py:39
  40.2 0.8 %partial.6 = (bf16[384,512]{1,0:T(8,128)(2,1)S(1)}, bf16[384,512]{1,0:T(8,128)(2,1)S(1)}) custom-call(s32[1]{0:T(128)} %bitcast.where_ref, bf16[256,768]{1,0:T(8,128)(2,1)S(1)} %collective-permute-done.11.left_ref, bf16[768,2048]{1,0:T(8,128)(2,1)S(1)} %stage.1.own_ref.vec_ref), custom_call_target="tpu_custom_call" | custom-call | flops 603979776 | bytes 3538944 | tf_op jit(solution)/shard_map/partial/pallas_call | solution.py:171
  41.6 1.0 %collective-permute-start.16 = (bf16[128,512]{1,0:T(8,128)(2,1)S(1)}, bf16[128,512]{1,0:T(8,128)(2,1)S(1)}, u32[]{:S(2)}, u32[]{:S(2)}) collective-permute-start(bf16[128,512]{1,0:T(8,128)(2,1)S(1)} %add_convert_fusion.3), channel_id=1, source_target_pairs={{0,4},{4,0},{8,12},{12,8},{1,5},{5,1},{9,13},{13,9},{2,6},{6,2},{1... | collective-permute-start | bytes 393224 | tf_op jit(solution)/shard_map/ppermute | solution.py:39
  42.6 1.1 %collective-permute-start.9 = (bf16[256,512]{1,0:T(8,128)(2,1)S(1)}, bf16[256,512]{1,0:T(8,128)(2,1)S(1)}, u32[]{:S(2)}, u32[]{:S(2)}) collective-permute-start(bf16[256,512]{1,0:T(8,128)(2,1)S(1)} %add_convert_fusion), channel_id=1, source_target_pairs={{0,4},{4,0},{8,12},{12,8},{1,5},{5,1},{9,13},{13,9},{2,6},{6,2},{1... | collective-permute-start | bytes 786440 | tf_op jit(solution)/shard_map/ppermute | solution.py:39
  43.6 4.3 %collective-permute-done.16 = bf16[128,512]{1,0:T(8,128)(2,1)S(1)} collective-permute-done((bf16[128,512]{1,0:T(8,128)(2,1)S(1)}, bf16[128,512]{1,0:T(8,128)(2,1)S(1)}, u32[]{:S(2)}, u32[]{:S(2)}) %collective-permute-start.16) | collective-permute-done | bytes 131104 | tf_op jit(solution)/shard_map/ppermute | solution.py:39
  48.1 0.7 %collective-permute-start.17 = (bf16[128,512]{1,0:T(8,128)(2,1)S(1)}, bf16[128,512]{1,0:T(8,128)(2,1)S(1)}, u32[]{:S(2)}, u32[]{:S(2)}) collective-permute-start(bf16[128,512]{1,0:T(8,128)(2,1)S(1)} %get-tuple-element.33), channel_id=1, source_target_pairs={{0,2},{1,3},{2,0},{3,1},{4,6},{5,7},{6,4},{7,5},{8,10},{9,11},{10,... | collective-permute-start | bytes 393224 | tf_op jit(solution)/shard_map/ppermute | solution.py:39
  48.8 0.8 %collective-permute-start.13 = (bf16[128,512]{1,0:T(8,128)(2,1)S(1)}, bf16[128,512]{1,0:T(8,128)(2,1)S(1)}, u32[]{:S(2)}, u32[]{:S(2)}) collective-permute-start(bf16[128,512]{1,0:T(8,128)(2,1)S(1)} %get-tuple-element.34), channel_id=1, source_target_pairs={{0,4},{4,0},{8,12},{12,8},{1,5},{5,1},{9,13},{13,9},{2,6},{6,2},{1... | collective-permute-start | bytes 393224 | tf_op jit(solution)/shard_map/ppermute | solution.py:39
  49.6 4.0 %collective-permute-done.9.refs_0_ = bf16[256,512]{1,0:T(8,128)(2,1)S(1)} collective-permute-done((bf16[256,512]{1,0:T(8,128)(2,1)S(1)}, bf16[256,512]{1,0:T(8,128)(2,1)S(1)}, u32[]{:S(2)}, u32[]{:S(2)}) %collective-permute-start.9) | collective-permute-done | bytes 262176 | tf_op jit(solution)/shard_map/ppermute | solution.py:39
  53.7 2.3 %collective-permute-start.18 = (bf16[128,512]{1,0:T(8,128)(2,1)S(1)}, bf16[128,512]{1,0:T(8,128)(2,1)S(1)}, u32[]{:S(2)}, u32[]{:S(2)}) collective-permute-start(bf16[128,512]{1,0:T(8,128)(2,1)S(1)} %add_convert_fusion.1), channel_id=1, source_target_pairs={{0,8},{4,12},{8,0},{12,4},{1,9},{5,13},{9,1},{13,5},{2,10},{6,14},... | collective-permute-start | bytes 393224 | tf_op jit(solution)/shard_map/ppermute | solution.py:39
  56.6 5.1 %collective-permute-done.18.refs_2_ = bf16[128,512]{1,0:T(8,128)(2,1)S(1)} collective-permute-done((bf16[128,512]{1,0:T(8,128)(2,1)S(1)}, bf16[128,512]{1,0:T(8,128)(2,1)S(1)}, u32[]{:S(2)}, u32[]{:S(2)}) %collective-permute-start.18) | collective-permute-done | bytes 131104 | tf_op jit(solution)/shard_map/ppermute | solution.py:39
  61.7 0.8 %finish.1 = f32[64,2,512]{2,1,0:T(2,128)} custom-call(bf16[256,512]{1,0:T(8,128)(2,1)S(1)} %get-tuple-element.23.keep_ref, bf16[256,512]{1,0:T(8,128)(2,1)S(1)} %collective-permute-done.7.got_ref, bf16[256,512]{1,0:T(8,128)(2,1)S(1)} %collective-permute-done.9.refs_0_, bf16[128,512]{1,0:T(8,128)(2,1)S(1)} %collective-permute-done.14.refs_1_, ...), custom_call_target="tpu_custom_call" | custom-call | tf_op jit(solution)/shard_map/finish/pallas_call | solution.py:248
  (31 shorter events, 4.9 us)
Async XLA Ops:
  0.0 24.8 %collective-permute-start.1 = (bf16[768,2048]{1,0:T(8,128)(2,1)}, bf16[768,2048]{1,0:T(8,128)(2,1)S(1)}, u32[]{:S(2)}, u32[]{:S(2)}) collective-permute-start(bf16[768,2048]{1,0:T(8,128)(2,1)} %bitcast.3), channel_id=1, source_target_pairs={{0,1},{1,0},{2,3},{3,2},{4,5},{5,4},{6,7},{7,6},{8,9},{9,8},{10,11... | collective-permute-start | bytes 9437192 | tf_op jit(solution)/shard_map/ppermute | solution.py:39
  0.5 10.8 %collective-permute-start.3 = (bf16[128,512]{1,0:T(8,128)(2,1)}, bf16[128,512]{1,0:T(8,128)(2,1)S(1)}, u32[]{:S(2)}, u32[]{:S(2)}) collective-permute-start(bf16[128,512]{1,0:T(8,128)(2,1)} %bitcast.5), channel_id=1, source_target_pairs={{0,8},{4,12},{8,0},{12,4},{1,9},{5,13},{9,1},{13,5},{2,10},{6,14},... | collective-permute-start | bytes 393224 | tf_op jit(solution)/shard_map/ppermute | solution.py:39
  4.1 10.8 %collective-permute-start = (bf16[128,512]{1,0:T(8,128)(2,1)}, bf16[128,512]{1,0:T(8,128)(2,1)S(1)}, u32[]{:S(2)}, u32[]{:S(2)}) collective-permute-start(bf16[128,512]{1,0:T(8,128)(2,1)} %bitcast.6), channel_id=1, source_target_pairs={{0,2},{1,3},{2,0},{3,1},{4,6},{5,7},{6,4},{7,5},{8,10},{9,11},{10,... | collective-permute-start | bytes 393224 | tf_op jit(solution)/shard_map/ppermute | solution.py:39
  11.3 6.5 %collective-permute-start.6 = (bf16[128,512]{1,0:T(8,128)(2,1)S(1)}, bf16[128,512]{1,0:T(8,128)(2,1)S(1)}, u32[]{:S(2)}, u32[]{:S(2)}) collective-permute-start(bf16[128,512]{1,0:T(8,128)(2,1)S(1)} %collective-permute-done.3.refs_2_), channel_id=1, source_target_pairs={{0,2},{1,3},{2,0},{3,1},{4,6},{5,7},{6,4},{7,5},{8,10},{9,11},{10,... | collective-permute-start | bytes 393224 | tf_op jit(solution)/shard_map/ppermute | solution.py:39
  12.8 6.6 %collective-permute-start.2 = (bf16[128,512]{1,0:T(8,128)(2,1)}, bf16[128,512]{1,0:T(8,128)(2,1)S(1)}, u32[]{:S(2)}, u32[]{:S(2)}) collective-permute-start(bf16[128,512]{1,0:T(8,128)(2,1)} %bitcast.7), channel_id=1, source_target_pairs={{0,4},{4,0},{8,12},{12,8},{1,5},{5,1},{9,13},{13,9},{2,6},{6,2},{1... | collective-permute-start | bytes 393224 | tf_op jit(solution)/shard_map/ppermute | solution.py:39
  13.6 8.6 %collective-permute-start.4 = (bf16[128,512]{1,0:T(8,128)(2,1)S(1)}, bf16[128,512]{1,0:T(8,128)(2,1)S(1)}, u32[]{:S(2)}, u32[]{:S(2)}) collective-permute-start(bf16[128,512]{1,0:T(8,128)(2,1)S(1)} %collective-permute-done.3.refs_2_), channel_id=1, source_target_pairs={{0,4},{4,0},{8,12},{12,8},{1,5},{5,1},{9,13},{13,9},{2,6},{6,2},{1... | collective-permute-start | bytes 393224 | tf_op jit(solution)/shard_map/ppermute | solution.py:39
  14.8 10.0 %collective-permute-start.5 = (bf16[128,512]{1,0:T(8,128)(2,1)S(1)}, bf16[128,512]{1,0:T(8,128)(2,1)S(1)}, u32[]{:S(2)}, u32[]{:S(2)}) collective-permute-start(bf16[128,512]{1,0:T(8,128)(2,1)S(1)} %collective-permute-done.refs_4_), channel_id=1, source_target_pairs={{0,4},{4,0},{8,12},{12,8},{1,5},{5,1},{9,13},{13,9},{2,6},{6,2},{1... | collective-permute-start | bytes 393224 | tf_op jit(solution)/shard_map/ppermute | solution.py:39
  15.6 1.9 %copy-start = (bf16[12,64,2048]{2,1,0:T(8,128)(2,1)S(1)}, bf16[12,64,2048]{2,1,0:T(8,128)(2,1)}, u32[]{:S(2)}) copy-start(bf16[12,64,2048]{2,1,0:T(8,128)(2,1)} %param.2) | copy-start | bytes 9437188
  17.5 7.3 %copy-start.1 = (bf16[2,64,512]{2,1,0:T(8,128)(2,1)S(1)}, bf16[2,64,512]{2,1,0:T(8,128)(2,1)}, u32[]{:S(2)}) copy-start(bf16[2,64,512]{2,1,0:T(8,128)(2,1)} %param.3) | copy-start | bytes 393220
  17.7 9.7 %collective-permute-start.10 = (bf16[128,512]{1,0:T(8,128)(2,1)S(1)}, bf16[128,512]{1,0:T(8,128)(2,1)S(1)}, u32[]{:S(2)}, u32[]{:S(2)}) collective-permute-start(bf16[128,512]{1,0:T(8,128)(2,1)S(1)} %collective-permute-done.6.refs_6_), channel_id=1, source_target_pairs={{0,4},{4,0},{8,12},{12,8},{1,5},{5,1},{9,13},{13,9},{2,6},{6,2},{1... | collective-permute-start | bytes 393224 | tf_op jit(solution)/shard_map/ppermute | solution.py:39
  27.4 2.1 %collective-permute-start.8 = (bf16[256,512]{1,0:T(8,128)(2,1)S(1)}, bf16[256,512]{1,0:T(8,128)(2,1)S(1)}, u32[]{:S(2)}, u32[]{:S(2)}) collective-permute-start(bf16[256,512]{1,0:T(8,128)(2,1)S(1)} %get-tuple-element.26), channel_id=1, source_target_pairs={{0,1},{1,0},{2,3},{3,2},{4,5},{5,4},{6,7},{7,6},{8,9},{9,8},{10,11... | collective-permute-start | bytes 786440 | tf_op jit(solution)/shard_map/ppermute | solution.py:39
  28.1 11.6 %collective-permute-start.11 = (bf16[256,768]{1,0:T(8,128)(2,1)S(1)}, bf16[256,768]{1,0:T(8,128)(2,1)S(1)}, u32[]{:S(2)}, u32[]{:S(2)}) collective-permute-start(bf16[256,768]{1,0:T(8,128)(2,1)S(1)} %last_pairs.1), channel_id=1, source_target_pairs={{0,2},{1,3},{2,0},{3,1},{4,6},{5,7},{6,4},{7,5},{8,10},{9,11},{10,... | collective-permute-start | bytes 1179656 | tf_op jit(solution)/shard_map/ppermute | solution.py:39
  40.1 1.4 %collective-permute-start.15 = (bf16[128,512]{1,0:T(8,128)(2,1)S(1)}, bf16[128,512]{1,0:T(8,128)(2,1)S(1)}, u32[]{:S(2)}, u32[]{:S(2)}) collective-permute-start(bf16[128,512]{1,0:T(8,128)(2,1)S(1)} %get-tuple-element.32), channel_id=1, source_target_pairs={{0,1},{1,0},{2,3},{3,2},{4,5},{5,4},{6,7},{7,6},{8,9},{9,8},{10,11... | collective-permute-start | bytes 393224 | tf_op jit(solution)/shard_map/ppermute | solution.py:39
  41.0 7.0 %collective-permute-start.12 = (bf16[384,512]{1,0:T(8,128)(2,1)S(1)}, bf16[384,512]{1,0:T(8,128)(2,1)S(1)}, u32[]{:S(2)}, u32[]{:S(2)}) collective-permute-start(bf16[384,512]{1,0:T(8,128)(2,1)S(1)} %get-tuple-element.30), channel_id=1, source_target_pairs={{0,1},{1,0},{2,3},{3,2},{4,5},{5,4},{6,7},{7,6},{8,9},{9,8},{10,11... | collective-permute-start | bytes 1179656 | tf_op jit(solution)/shard_map/ppermute | solution.py:39
  41.6 6.4 %collective-permute-start.16 = (bf16[128,512]{1,0:T(8,128)(2,1)S(1)}, bf16[128,512]{1,0:T(8,128)(2,1)S(1)}, u32[]{:S(2)}, u32[]{:S(2)}) collective-permute-start(bf16[128,512]{1,0:T(8,128)(2,1)S(1)} %add_convert_fusion.3), channel_id=1, source_target_pairs={{0,4},{4,0},{8,12},{12,8},{1,5},{5,1},{9,13},{13,9},{2,6},{6,2},{1... | collective-permute-start | bytes 393224 | tf_op jit(solution)/shard_map/ppermute | solution.py:39
  42.6 7.1 %collective-permute-start.7 = (bf16[256,512]{1,0:T(8,128)(2,1)S(1)}, bf16[256,512]{1,0:T(8,128)(2,1)S(1)}, u32[]{:S(2)}, u32[]{:S(2)}) collective-permute-start(bf16[256,512]{1,0:T(8,128)(2,1)S(1)} %get-tuple-element.24), channel_id=1, source_target_pairs={{0,1},{1,0},{2,3},{3,2},{4,5},{5,4},{6,7},{7,6},{8,9},{9,8},{10,11... | collective-permute-start | bytes 786440 | tf_op jit(solution)/shard_map/ppermute | solution.py:39
  42.6 11.0 %collective-permute-start.9 = (bf16[256,512]{1,0:T(8,128)(2,1)S(1)}, bf16[256,512]{1,0:T(8,128)(2,1)S(1)}, u32[]{:S(2)}, u32[]{:S(2)}) collective-permute-start(bf16[256,512]{1,0:T(8,128)(2,1)S(1)} %add_convert_fusion), channel_id=1, source_target_pairs={{0,4},{4,0},{8,12},{12,8},{1,5},{5,1},{9,13},{13,9},{2,6},{6,2},{1... | collective-permute-start | bytes 786440 | tf_op jit(solution)/shard_map/ppermute | solution.py:39
  48.1 5.5 %collective-permute-start.17 = (bf16[128,512]{1,0:T(8,128)(2,1)S(1)}, bf16[128,512]{1,0:T(8,128)(2,1)S(1)}, u32[]{:S(2)}, u32[]{:S(2)}) collective-permute-start(bf16[128,512]{1,0:T(8,128)(2,1)S(1)} %get-tuple-element.33), channel_id=1, source_target_pairs={{0,2},{1,3},{2,0},{3,1},{4,6},{5,7},{6,4},{7,5},{8,10},{9,11},{10,... | collective-permute-start | bytes 393224 | tf_op jit(solution)/shard_map/ppermute | solution.py:39
  48.8 7.2 %collective-permute-start.13 = (bf16[128,512]{1,0:T(8,128)(2,1)S(1)}, bf16[128,512]{1,0:T(8,128)(2,1)S(1)}, u32[]{:S(2)}, u32[]{:S(2)}) collective-permute-start(bf16[128,512]{1,0:T(8,128)(2,1)S(1)} %get-tuple-element.34), channel_id=1, source_target_pairs={{0,4},{4,0},{8,12},{12,8},{1,5},{5,1},{9,13},{13,9},{2,6},{6,2},{1... | collective-permute-start | bytes 393224 | tf_op jit(solution)/shard_map/ppermute | solution.py:39
  53.7 8.0 %collective-permute-start.18 = (bf16[128,512]{1,0:T(8,128)(2,1)S(1)}, bf16[128,512]{1,0:T(8,128)(2,1)S(1)}, u32[]{:S(2)}, u32[]{:S(2)}) collective-permute-start(bf16[128,512]{1,0:T(8,128)(2,1)S(1)} %add_convert_fusion.1), channel_id=1, source_target_pairs={{0,8},{4,12},{8,0},{12,4},{1,9},{5,13},{9,1},{13,5},{2,10},{6,14},... | collective-permute-start | bytes 393224 | tf_op jit(solution)/shard_map/ppermute | solution.py:39
  56.0 5.7 %collective-permute-start.14 = (bf16[128,512]{1,0:T(8,128)(2,1)S(1)}, bf16[128,512]{1,0:T(8,128)(2,1)S(1)}, u32[]{:S(2)}, u32[]{:S(2)}) collective-permute-start(bf16[128,512]{1,0:T(8,128)(2,1)S(1)} %add_convert_fusion.4), channel_id=1, source_target_pairs={{0,2},{1,3},{2,0},{3,1},{4,6},{5,7},{6,4},{7,5},{8,10},{9,11},{10,... | collective-permute-start | bytes 393224 | tf_op jit(solution)/shard_map/ppermute | solution.py:39

commit v5 on v4

--- a/solution.py
+++ b/solution.py
@@ -66,14 +66,15 @@
     )(x)
 
 
-def store_pairs(out_ref, core, sums, walkers, occ_loc):
+def store_pairs(out_refs, core, sums, walkers, occ_loc):
+    share = walkers // len(out_refs)
     for w in range(walkers):
         tiles = [
             sums[start : start + occ_loc, w * occ_loc : (w + 1) * occ_loc]
             for start in range(0, sums.shape[0], occ_loc)
         ]
-        first = (core * walkers + w) * occ_loc
-        out_ref[first : first + occ_loc, :] = jnp.concatenate(tiles, axis=1)
+        first = (core * share + w % share) * occ_loc
+        out_refs[w // share][first : first + occ_loc, :] = jnp.concatenate(tiles, axis=1)
 
 
 CONTRACT_LAST = (((1,), (1,)), ((), ()))
@@ -91,11 +92,11 @@
         flat[pl.ds(side * rows, rows), pl.ds(start, width)] = piece
     for core, vec_ref in enumerate((own_ref, sib_ref)):
         sums = lax.dot_general(vec_ref[...], flat[...], CONTRACT_LAST, preferred_element_type=F32)
-        store_pairs(near_ref, core, sums[:, :rows].astype(BF16), walkers, occ_loc)
+        store_pairs((near_ref,), core, sums[:, :rows].astype(BF16), walkers, occ_loc)
         sums_ref[core * total : (core + 1) * total, :] = sums[:, rows:]
 
 
-def last_pair_kernel(walkers, occ_loc, last, where_ref, own_ref, sib_ref, green_ref, sums_ref, far_ref):
+def last_pair_kernel(walkers, occ_loc, last, where_ref, own_ref, sib_ref, green_ref, sums_ref, *far_refs):
     width = green_ref.shape[1]
     total = own_ref.shape[0]
     start = pl.multiple_of((where_ref[0] ^ last) * width, width)
@@ -103,7 +104,7 @@
         sums = sums_ref[core * total : (core + 1) * total, :] + lax.dot_general(
             vec_ref[:, pl.ds(start, width)], green_ref[...], CONTRACT_LAST, preferred_element_type=F32
         )
-        store_pairs(far_ref, core, sums.astype(BF16), walkers, occ_loc)
+        store_pairs(far_refs, core, sums.astype(BF16), walkers, occ_loc)
 
 
 def pair_products(where, own, sib, near, far, walkers, occ_loc):
@@ -112,6 +113,7 @@
     blocks = len(near)
     greens = [side[r] for side in (near, far) for r in range(blocks)]
     pairs = jax.ShapeDtypeStruct((2 * rows, total), BF16)
+    half = jax.ShapeDtypeStruct((rows, total), BF16)
     sums = jax.ShapeDtypeStruct((2 * total, rows), F32)
     flops = 8 * total * orbitals * rows
     first = pl.pallas_call(
@@ -128,9 +130,9 @@
     )
     second = pl.pallas_call(
         functools.partial(last_pair_kernel, walkers, occ_loc, blocks - 1),
-        out_shape=pairs,
+        out_shape=(half, half),
         in_specs=[SMEM] + [VMEM] * 4,
-        out_specs=VMEM,
+        out_specs=(VMEM, VMEM),
         compiler_params=pltpu.CompilerParams(vmem_limit_bytes=10 << 20),
         cost_estimate=pl.CostEstimate(
             flops=flops // (2 * blocks), bytes_accessed=4 * total * orbitals // blocks + 4 * sums.size, transcendentals=0
@@ -172,16 +174,39 @@
     return keep, xor_permute(send, "occ", 1)
 
 
-def finish_kernel(factor, keep_ref, got_ref, *refs):
+def near_sum_kernel(*refs):
+    rows, _ = refs[-1].shape
+    total = refs[0][-rows:].astype(F32)
+    for ref in refs[1:-1]:
+        total = total + ref[-rows:].astype(F32)
+    refs[-1][...] = total
+
+
+def near_sum(near, rows):
+    width = near[0].shape[1]
+    return pl.pallas_call(
+        near_sum_kernel,
+        out_shape=jax.ShapeDtypeStruct((rows, width), F32),
+        in_specs=[VMEM] * len(near),
+        out_specs=VMEM,
+        compiler_params=pltpu.CompilerParams(vmem_limit_bytes=4 << 20),
+        cost_estimate=pl.CostEstimate(flops=3 * rows * width, bytes_accessed=10 * rows * width, transcendentals=0),
+        name="near_sum",
+    )(*near)
+
+
+def finish_kernel(factor, halves, base_ref, crossed_ref, *refs):
     out_ref = refs[-1]
     occ_loc, walkers, _ = out_ref.shape
-    rows = walkers * occ_loc
-    total = keep_ref[-rows:].astype(F32) + got_ref[-rows:].astype(F32)
-    for ref in refs[:-1]:
-        total = total + ref[-rows:].astype(F32)
-    total = total * factor
+    total = base_ref[...] + crossed_ref[...].astype(F32)
+    chunk = total.shape[0] // 2
+    sums = [total[:chunk], total[chunk:]]
+    for h, ref in zip(halves, refs[:-1]):
+        sums[h] = sums[h] + ref[...].astype(F32)
+    share = walkers // 2
     for w in range(walkers):
-        out_ref[:, w, :] = total[w * occ_loc : (w + 1) * occ_loc]
+        first = w % share * occ_loc
+        out_ref[:, w, :] = sums[w // share][first : first + occ_loc] * factor
 
 
 def relative(chol_rot, green):
@@ -209,49 +234,71 @@
         else:
             far[r] = xor_permute(near[r], "occ", 2)
     stay, leave = pair_products(where, own, sib, near, far, walkers, occ_loc)
-    come = xor_permute(leave, "occ", 2)
+    come = [xor_permute(x, "occ", 2) for x in leave]
 
     odds = tuple(range(n_chol - 1, 0, -2))
     evens = tuple(r - 1 for r in odds)
+    chunk = rows // 2
 
     def part(x, n):
-        return x[n * rows : (n + 1) * rows].astype(F32)
+        return x[n * chunk : (n + 1) * chunk].astype(F32)
 
     odd_keep, odd_got = partial_products(odds, where, stay, own, width)
     near_keep, near_got = partial_products(evens, where, stay, own, width)
     near_odd = (odd_keep.astype(F32) + odd_got.astype(F32)).astype(BF16)
-    come = after(come, (near_odd, near_keep))
     near_came = xor_permute(near_odd, "chol", 1)
-    far = {}
-    for which in (odds[:1], odds[1:] + evens):
-        pair = partial_products(which, where, come, own, width)
-        far |= {r: part(pair[0], n) + part(pair[1], n) for n, r in enumerate(which)}
-    far |= {r - 1: far[r - 1] + xor_permute(far[r].astype(BF16), "chol", 1).astype(F32) for r in odds}
-    crossed = {r: xor_permute(far[r].astype(BF16), "occ", 2) for r in evens}
-    summed = {
-        r: part(near_keep, n) + part(near_got, n) + part(near_came, n)
-        + crossed[r].astype(F32)
-        for n, r in enumerate(evens) if r
-    }
+    near = (near_keep, near_got, near_came)
+    earlier = (near_odd, near_keep)
+    far, pairs = [], []
+    for h in range(2):
+        pair = partial_products(odds + evens, where, after(come[h], earlier), own, width)
+        earlier = pair[0]
+        pairs.append(pair)
+        far.append({r: part(pair[0], n) + part(pair[1], n) for n, r in enumerate(odds + evens)})
+
+    crossed, sent = [{}, {}], near_odd
+    for h in range(2):
+        for r in evens:
+            if r:
+                moved = xor_permute(far[h][r + 1].astype(BF16), "chol", 1)
+                moved = after(moved, sent)
+                sent = (far[h][r] + moved.astype(F32)).astype(BF16)
+                crossed[h][r] = xor_permute(sent, "occ", 2)
+    n_one, n_zero = (odds + evens).index(1), (odds + evens).index(0)
+    gated = [tuple(after(x, sent) for x in pair) for pair in pairs]
+
+    def both(n):
+        return jnp.concatenate([part(keep, n) + part(got, n) for keep, got in gated])
+
+    moved = xor_permute(both(n_one).astype(BF16), "chol", 1)
+    first_crossed = xor_permute((both(n_zero) + moved.astype(F32)).astype(BF16), "occ", 2)
     came = []
-    bit = n_chol // 2
-    while bit > 1:
-        for r in evens:
-            if r & bit and r < 2 * bit:
-                moved = xor_permute(summed[r].astype(BF16), "chol", bit)
-                if r == bit:
-                    came.append(moved)
-                else:
-                    summed[r ^ bit] = summed[r ^ bit] + moved.astype(F32)
-        bit //= 2
+    for h in range(2):
+        summed = {}
+        for n, r in enumerate(evens):
+            if r:
+                summed[r] = after(crossed[h][r], sent).astype(F32)
+                for x in near:
+                    summed[r] = summed[r] + part(x, 2 * n + h)
+        bit = n_chol // 2
+        while bit > 1:
+            for r in evens:
+                if r & bit and r < 2 * bit:
+                    sent = summed[r].astype(BF16)
+                    moved = xor_permute(sent, "chol", bit)
+                    if r == bit:
+                        came.append((h, moved))
+                    else:
+                        summed[r ^ bit] = summed[r ^ bit] + moved.astype(F32)
+            bit //= 2
 
     return pl.pallas_call(
-        functools.partial(finish_kernel, factor),
+        functools.partial(finish_kernel, factor, tuple(h for h, _ in came)),
         out_shape=jax.ShapeDtypeStruct((occ_loc, walkers, width), F32),
-        in_specs=[VMEM] * (4 + len(came)),
+        in_specs=[VMEM] * (2 + len(came)),
         compiler_params=pltpu.CompilerParams(vmem_limit_bytes=4 << 20),
         name="finish",
-    )(near_keep, near_got, near_came, crossed[0], *came)
+    )(near_sum(near, rows), first_crossed, *(x for _, x in came))
 
 
 def local(chol_rot, green):
@@ -263,7 +310,7 @@
         and n_chol & (n_chol - 1) == 0
         and width % 128 == 0
         and occ_loc % 16 == 0
-        and green.shape[0] * occ_loc % 32 == 0
+        and green.shape[0] % 2 == 0
         and (chol_rot.shape[0] * occ_loc) % 128 == 0
     )
     return relative(chol_rot, green) if fits else general(chol_rot, green)

time: 62.7 us -> 68.8 us (1.097)
  starting transfers between devices: 19.2 us -> 25.4 us
    ppermute x19 -> x23, starting transfers between devices: 19.2 us -> 25.4 us  [xor_permute(): return lax.ppermute(x, axis, [(i, i ^ bits) for i in range(size)])]
    ppermute x19 -> x23, waiting for transfers between devices: 35 us -> 34.9 us  [xor_permute(): return lax.ppermute(x, axis, [(i, i ^ bits) for i in range(size)])]
  transfers between devices with their start and end apart: 19 -> 23, of which waited for: 8 -> 12; matrix products, arithmetic and copies ran while one was open for 0% -> 0% of each run, Pallas kernels for 8% -> 4%
where the time goes in v5:
time: 68.8 us; the launch traced here: 68.7 us
  waiting for transfers between devices  34.9 us (51%)
  starting transfers between devices  25.4 us (37%)
  Pallas kernels  6.03 us (9%)
  local copies, waits for them, and re-layouts  1.89 us (3%)
    ppermute x23, waiting for transfers between devices, xor_permute(): return lax.ppermute(x, axis, [(i, i ^ bits) for i in range(size)])  34.9 us
    ppermute x23, starting transfers between devices, xor_permute(): return lax.ppermute(x, axis, [(i, i ^ bits) for i in range(size)])  25.4 us
    pallas_call x4, Pallas kernels, partial_products(): keep, send = call(where, left, own)  2.34 us
    pallas_call x1, Pallas kernels, pair_products(): stay, begun = first(where, own, sib, *greens[:-1])  1.98 us
    unnamed x4, local copies, waits for them, and re-layouts  1.89 us
  transfers between devices with their start and end apart: 23, of which 12 were waited for; matrix products, arithmetic and copies ran while one was open for 0% of the time, Pallas kernels for 4%

profile of v5, /device:TPU:0, one launch (start us, length us, event | category | flops | bytes accessed | tf_op | source)
XLA Modules:
  0.0 68.7 jit_solution(8031334674202154784)
XLA Ops:
  0.5 3.6 %collective-permute-start.3 = (bf16[128,512]{1,0:T(8,128)(2,1)}, bf16[128,512]{1,0:T(8,128)(2,1)S(1)}, u32[]{:S(2)}, u32[]{:S(2)}) collective-permute-start(bf16[128,512]{1,0:T(8,128)(2,1)} %bitcast.5), channel_id=1, source_target_pairs={{0,8},{4,12},{8,0},{12,4},{1,9},{5,13},{9,1},{13,5},{2,10},{6,14},... | collective-permute-start | bytes 393224 | tf_op jit(solution)/shard_map/ppermute | solution.py:39
  4.1 1.5 %collective-permute-start = (bf16[128,512]{1,0:T(8,128)(2,1)}, bf16[128,512]{1,0:T(8,128)(2,1)S(1)}, u32[]{:S(2)}, u32[]{:S(2)}) collective-permute-start(bf16[128,512]{1,0:T(8,128)(2,1)} %bitcast.6), channel_id=1, source_target_pairs={{0,2},{1,3},{2,0},{3,1},{4,6},{5,7},{6,4},{7,5},{8,10},{9,11},{10,... | collective-permute-start | bytes 393224 | tf_op jit(solution)/shard_map/ppermute | solution.py:39
  5.6 1.6 %collective-permute-start.2 = (bf16[128,512]{1,0:T(8,128)(2,1)}, bf16[128,512]{1,0:T(8,128)(2,1)S(1)}, u32[]{:S(2)}, u32[]{:S(2)}) collective-permute-start(bf16[128,512]{1,0:T(8,128)(2,1)} %bitcast.7), channel_id=1, source_target_pairs={{0,4},{4,0},{8,12},{12,8},{1,5},{5,1},{9,13},{13,9},{2,6},{6,2},{1... | collective-permute-start | bytes 393224 | tf_op jit(solution)/shard_map/ppermute | solution.py:39
  7.1 4.2 %collective-permute-done.3.refs_2_ = bf16[128,512]{1,0:T(8,128)(2,1)S(1)} collective-permute-done((bf16[128,512]{1,0:T(8,128)(2,1)}, bf16[128,512]{1,0:T(8,128)(2,1)S(1)}, u32[]{:S(2)}, u32[]{:S(2)}) %collective-permute-start.3) | collective-permute-done | bytes 131104 | tf_op jit(solution)/shard_map/ppermute | solution.py:39
  11.4 1.5 %collective-permute-start.6 = (bf16[128,512]{1,0:T(8,128)(2,1)S(1)}, bf16[128,512]{1,0:T(8,128)(2,1)S(1)}, u32[]{:S(2)}, u32[]{:S(2)}) collective-permute-start(bf16[128,512]{1,0:T(8,128)(2,1)S(1)} %collective-permute-done.3.refs_2_), channel_id=1, source_target_pairs={{0,2},{1,3},{2,0},{3,1},{4,6},{5,7},{6,4},{7,5},{8,10},{9,11},{10,... | collective-permute-start | bytes 393224 | tf_op jit(solution)/shard_map/ppermute | solution.py:39
  13.6 1.4 %collective-permute-start.5 = (bf16[128,512]{1,0:T(8,128)(2,1)S(1)}, bf16[128,512]{1,0:T(8,128)(2,1)S(1)}, u32[]{:S(2)}, u32[]{:S(2)}) collective-permute-start(bf16[128,512]{1,0:T(8,128)(2,1)S(1)} %collective-permute-done.refs_4_), channel_id=1, source_target_pairs={{0,4},{4,0},{8,12},{12,8},{1,5},{5,1},{9,13},{13,9},{2,6},{6,2},{1... | collective-permute-start | bytes 393224 | tf_op jit(solution)/shard_map/ppermute | solution.py:39
  14.9 1.9 %copy-done = bf16[12,64,2048]{2,1,0:T(8,128)(2,1)S(1)} copy-done((bf16[12,64,2048]{2,1,0:T(8,128)(2,1)S(1)}, bf16[12,64,2048]{2,1,0:T(8,128)(2,1)}, u32[]{:S(2)}) %copy-start) | copy-done | bytes 3145752
  17.1 1.9 %collective-permute-done.4.refs_3_ = bf16[128,512]{1,0:T(8,128)(2,1)S(1)} collective-permute-done((bf16[128,512]{1,0:T(8,128)(2,1)S(1)}, bf16[128,512]{1,0:T(8,128)(2,1)S(1)}, u32[]{:S(2)}, u32[]{:S(2)}) %collective-permute-start.4) | collective-permute-done | bytes 131104 | tf_op jit(solution)/shard_map/ppermute | solution.py:39
  19.0 1.4 %collective-permute-done.5.refs_5_ = bf16[128,512]{1,0:T(8,128)(2,1)S(1)} collective-permute-done((bf16[128,512]{1,0:T(8,128)(2,1)S(1)}, bf16[128,512]{1,0:T(8,128)(2,1)S(1)}, u32[]{:S(2)}, u32[]{:S(2)}) %collective-permute-start.5) | collective-permute-done | bytes 131104 | tf_op jit(solution)/shard_map/ppermute | solution.py:39
  20.4 2.0 %pairs.1 = (bf16[256,768]{1,0:T(8,128)(2,1)S(1)}, f32[1536,128]{1,0:T(8,128)S(1)}) custom-call(s32[1]{0:T(128)} %bitcast.where_ref, bf16[768,2048]{1,0:T(8,128)(2,1)S(1)} %stage.1.own_ref.vec_ref, bf16[768,2048]{1,0:T(8,128)(2,1)S(1)} %collective-permute-done.1.sib_ref, bf16[128,512]{1,0:T(8,128)(2,1)S(1)} %bitcast.8, ...), custom_call_target="tpu_custom_call" | custom-call | flops 1610612736 | bytes 8126464 | tf_op jit(solution)/shard_map/pairs/pallas_call | solution.py:142
  23.1 1.2 %collective-permute-start.10 = (bf16[128,512]{1,0:T(8,128)(2,1)S(1)}, bf16[128,512]{1,0:T(8,128)(2,1)S(1)}, u32[]{:S(2)}, u32[]{:S(2)}) collective-permute-start(bf16[128,512]{1,0:T(8,128)(2,1)S(1)} %collective-permute-done.6.refs_6_), channel_id=1, source_target_pairs={{0,4},{4,0},{8,12},{12,8},{1,5},{5,1},{9,13},{13,9},{2,6},{6,2},{1... | collective-permute-start | bytes 393224 | tf_op jit(solution)/shard_map/ppermute | solution.py:39
  24.3 4.7 %collective-permute-done.10.green_ref = bf16[128,512]{1,0:T(8,128)(2,1)S(1)} collective-permute-done((bf16[128,512]{1,0:T(8,128)(2,1)S(1)}, bf16[128,512]{1,0:T(8,128)(2,1)S(1)}, u32[]{:S(2)}, u32[]{:S(2)}) %collective-permute-start.10) | collective-permute-done | bytes 131104 | tf_op jit(solution)/shard_map/ppermute | solution.py:39
  30.5 1.2 %collective-permute-start.12 = (bf16[128,768]{1,0:T(8,128)(2,1)S(1)}, bf16[128,768]{1,0:T(8,128)(2,1)S(1)}, u32[]{:S(2)}, u32[]{:S(2)}) collective-permute-start(bf16[128,768]{1,0:T(8,128)(2,1)S(1)} %get-tuple-element.42), channel_id=1, source_target_pairs={{0,2},{1,3},{2,0},{3,1},{4,6},{5,7},{6,4},{7,5},{8,10},{9,11},{10,... | collective-permute-start | bytes 589832 | tf_op jit(solution)/shard_map/ppermute | solution.py:39
  32.4 5.1 %collective-permute-done.11.left_ref = bf16[128,768]{1,0:T(8,128)(2,1)S(1)} collective-permute-done((bf16[128,768]{1,0:T(8,128)(2,1)S(1)}, bf16[128,768]{1,0:T(8,128)(2,1)S(1)}, u32[]{:S(2)}, u32[]{:S(2)}) %collective-permute-start.11) | collective-permute-done | bytes 196640 | tf_op jit(solution)/shard_map/ppermute | solution.py:39
  38.1 2.1 %collective-permute-done.12.left_ref = bf16[128,768]{1,0:T(8,128)(2,1)S(1)} collective-permute-done((bf16[128,768]{1,0:T(8,128)(2,1)S(1)}, bf16[128,768]{1,0:T(8,128)(2,1)S(1)}, u32[]{:S(2)}, u32[]{:S(2)}) %collective-permute-start.12) | collective-permute-done | bytes 196640 | tf_op jit(solution)/shard_map/ppermute | solution.py:39
  41.4 1.2 %collective-permute-start.9 = (bf16[256,512]{1,0:T(8,128)(2,1)S(1)}, bf16[256,512]{1,0:T(8,128)(2,1)S(1)}, u32[]{:S(2)}, u32[]{:S(2)}) collective-permute-start(bf16[256,512]{1,0:T(8,128)(2,1)S(1)} %add_convert_fusion), channel_id=1, source_target_pairs={{0,4},{4,0},{8,12},{12,8},{1,5},{5,1},{9,13},{13,9},{2,6},{6,2},{1... | collective-permute-start | bytes 786440 | tf_op jit(solution)/shard_map/ppermute | solution.py:39
  43.6 1.3 %collective-permute-start.14 = (bf16[64,512]{1,0:T(8,128)(2,1)S(1)}, bf16[64,512]{1,0:T(8,128)(2,1)S(1)}, u32[]{:S(2)}, u32[]{:S(2)}) collective-permute-start(bf16[64,512]{1,0:T(8,128)(2,1)S(1)} %add_convert_fusion.8), channel_id=1, source_target_pairs={{0,4},{4,0},{8,12},{12,8},{1,5},{5,1},{9,13},{13,9},{2,6},{6,2},{1... | collective-permute-start | bytes 196616 | tf_op jit(solution)/shard_map/ppermute | solution.py:39
  44.8 7.0 %collective-permute-done.16 = bf16[64,512]{1,0:T(8,128)(2,1)S(1)} collective-permute-done((bf16[64,512]{1,0:T(8,128)(2,1)S(1)}, bf16[64,512]{1,0:T(8,128)(2,1)S(1)}, u32[]{:S(2)}, u32[]{:S(2)}) %collective-permute-start.16) | collective-permute-done | bytes 65568 | tf_op jit(solution)/shard_map/ppermute | solution.py:39
  52.8 1.3 %collective-permute-start.21 = (bf16[64,512]{1,0:T(8,128)(2,1)S(1)}, bf16[64,512]{1,0:T(8,128)(2,1)S(1)}, u32[]{:S(2)}, u32[]{:S(2)}) collective-permute-start(bf16[64,512]{1,0:T(8,128)(2,1)S(1)} %add_convert_fusion.5), channel_id=1, source_target_pairs={{0,2},{1,3},{2,0},{3,1},{4,6},{5,7},{6,4},{7,5},{8,10},{9,11},{10,... | collective-permute-start | bytes 196616 | tf_op jit(solution)/shard_map/ppermute | solution.py:39
  54.1 1.3 %collective-permute-start.17 = (bf16[128,512]{1,0:T(8,128)(2,1)S(1)}, bf16[128,512]{1,0:T(8,128)(2,1)S(1)}, u32[]{:S(2)}, u32[]{:S(2)}) collective-permute-start(bf16[128,512]{1,0:T(8,128)(2,1)S(1)} %pad_maximum_fusion), channel_id=1, source_target_pairs={{0,4},{4,0},{8,12},{12,8},{1,5},{5,1},{9,13},{13,9},{2,6},{6,2},{1... | collective-permute-start | bytes 393224 | tf_op jit(solution)/shard_map/ppermute | solution.py:39
  57.1 2.1 %collective-permute-done.17 = bf16[128,512]{1,0:T(8,128)(2,1)S(1)} collective-permute-done((bf16[128,512]{1,0:T(8,128)(2,1)S(1)}, bf16[128,512]{1,0:T(8,128)(2,1)S(1)}, u32[]{:S(2)}, u32[]{:S(2)}) %collective-permute-start.17) | collective-permute-done | bytes 131104 | tf_op jit(solution)/shard_map/ppermute | solution.py:39
  60.1 2.6 %collective-permute-start.22 = (bf16[64,512]{1,0:T(8,128)(2,1)S(1)}, bf16[64,512]{1,0:T(8,128)(2,1)S(1)}, u32[]{:S(2)}, u32[]{:S(2)}) collective-permute-start(bf16[64,512]{1,0:T(8,128)(2,1)S(1)} %add_convert_fusion.1), channel_id=1, source_target_pairs={{0,8},{4,12},{8,0},{12,4},{1,9},{5,13},{9,1},{13,5},{2,10},{6,14},... | collective-permute-start | bytes 196616 | tf_op jit(solution)/shard_map/ppermute | solution.py:39
  63.1 3.6 %collective-permute-done.22.refs_1_ = bf16[64,512]{1,0:T(8,128)(2,1)S(1)} collective-permute-done((bf16[64,512]{1,0:T(8,128)(2,1)S(1)}, bf16[64,512]{1,0:T(8,128)(2,1)S(1)}, u32[]{:S(2)}, u32[]{:S(2)}) %collective-permute-start.22) | collective-permute-done | bytes 65568 | tf_op jit(solution)/shard_map/ppermute | solution.py:39
  66.7 1.1 %collective-permute-done.20.refs_0_ = bf16[64,512]{1,0:T(8,128)(2,1)S(1)} collective-permute-done((bf16[64,512]{1,0:T(8,128)(2,1)S(1)}, bf16[64,512]{1,0:T(8,128)(2,1)S(1)}, u32[]{:S(2)}, u32[]{:S(2)}) %collective-permute-start.20) | collective-permute-done | bytes 65568 | tf_op jit(solution)/shard_map/ppermute | solution.py:39
  (45 shorter events, 11.8 us)
Async XLA Ops:
  0.0 20.4 %collective-permute-start.1 = (bf16[768,2048]{1,0:T(8,128)(2,1)}, bf16[768,2048]{1,0:T(8,128)(2,1)S(1)}, u32[]{:S(2)}, u32[]{:S(2)}) collective-permute-start(bf16[768,2048]{1,0:T(8,128)(2,1)} %bitcast.3), channel_id=1, source_target_pairs={{0,1},{1,0},{2,3},{3,2},{4,5},{5,4},{6,7},{7,6},{8,9},{9,8},{10,11... | collective-permute-start | bytes 9437192 | tf_op jit(solution)/shard_map/ppermute | solution.py:39
  0.5 10.9 %collective-permute-start.3 = (bf16[128,512]{1,0:T(8,128)(2,1)}, bf16[128,512]{1,0:T(8,128)(2,1)S(1)}, u32[]{:S(2)}, u32[]{:S(2)}) collective-permute-start(bf16[128,512]{1,0:T(8,128)(2,1)} %bitcast.5), channel_id=1, source_target_pairs={{0,8},{4,12},{8,0},{12,4},{1,9},{5,13},{9,1},{13,5},{2,10},{6,14},... | collective-permute-start | bytes 393224 | tf_op jit(solution)/shard_map/ppermute | solution.py:39
  4.1 9.5 %collective-permute-start = (bf16[128,512]{1,0:T(8,128)(2,1)}, bf16[128,512]{1,0:T(8,128)(2,1)S(1)}, u32[]{:S(2)}, u32[]{:S(2)}) collective-permute-start(bf16[128,512]{1,0:T(8,128)(2,1)} %bitcast.6), channel_id=1, source_target_pairs={{0,2},{1,3},{2,0},{3,1},{4,6},{5,7},{6,4},{7,5},{8,10},{9,11},{10,... | collective-permute-start | bytes 393224 | tf_op jit(solution)/shard_map/ppermute | solution.py:39
  5.6 11.5 %collective-permute-start.2 = (bf16[128,512]{1,0:T(8,128)(2,1)}, bf16[128,512]{1,0:T(8,128)(2,1)S(1)}, u32[]{:S(2)}, u32[]{:S(2)}) collective-permute-start(bf16[128,512]{1,0:T(8,128)(2,1)} %bitcast.7), channel_id=1, source_target_pairs={{0,4},{4,0},{8,12},{12,8},{1,5},{5,1},{9,13},{13,9},{2,6},{6,2},{1... | collective-permute-start | bytes 393224 | tf_op jit(solution)/shard_map/ppermute | solution.py:39
  11.4 5.7 %collective-permute-start.6 = (bf16[128,512]{1,0:T(8,128)(2,1)S(1)}, bf16[128,512]{1,0:T(8,128)(2,1)S(1)}, u32[]{:S(2)}, u32[]{:S(2)}) collective-permute-start(bf16[128,512]{1,0:T(8,128)(2,1)S(1)} %collective-permute-done.3.refs_2_), channel_id=1, source_target_pairs={{0,2},{1,3},{2,0},{3,1},{4,6},{5,7},{6,4},{7,5},{8,10},{9,11},{10,... | collective-permute-start | bytes 393224 | tf_op jit(solution)/shard_map/ppermute | solution.py:39
  12.9 6.1 %collective-permute-start.4 = (bf16[128,512]{1,0:T(8,128)(2,1)S(1)}, bf16[128,512]{1,0:T(8,128)(2,1)S(1)}, u32[]{:S(2)}, u32[]{:S(2)}) collective-permute-start(bf16[128,512]{1,0:T(8,128)(2,1)S(1)} %collective-permute-done.3.refs_2_), channel_id=1, source_target_pairs={{0,4},{4,0},{8,12},{12,8},{1,5},{5,1},{9,13},{13,9},{2,6},{6,2},{1... | collective-permute-start | bytes 393224 | tf_op jit(solution)/shard_map/ppermute | solution.py:39
  13.6 6.8 %collective-permute-start.5 = (bf16[128,512]{1,0:T(8,128)(2,1)S(1)}, bf16[128,512]{1,0:T(8,128)(2,1)S(1)}, u32[]{:S(2)}, u32[]{:S(2)}) collective-permute-start(bf16[128,512]{1,0:T(8,128)(2,1)S(1)} %collective-permute-done.refs_4_), channel_id=1, source_target_pairs={{0,4},{4,0},{8,12},{12,8},{1,5},{5,1},{9,13},{13,9},{2,6},{6,2},{1... | collective-permute-start | bytes 393224 | tf_op jit(solution)/shard_map/ppermute | solution.py:39
  16.8 3.6 %copy-start.1 = (bf16[2,64,512]{2,1,0:T(8,128)(2,1)S(1)}, bf16[2,64,512]{2,1,0:T(8,128)(2,1)}, u32[]{:S(2)}) copy-start(bf16[2,64,512]{2,1,0:T(8,128)(2,1)} %param.3) | copy-start | bytes 393220
  23.0 9.3 %collective-permute-start.8 = (bf16[256,512]{1,0:T(8,128)(2,1)S(1)}, bf16[256,512]{1,0:T(8,128)(2,1)S(1)}, u32[]{:S(2)}, u32[]{:S(2)}) collective-permute-start(bf16[256,512]{1,0:T(8,128)(2,1)S(1)} %get-tuple-element.37), channel_id=1, source_target_pairs={{0,1},{1,0},{2,3},{3,2},{4,5},{5,4},{6,7},{7,6},{8,9},{9,8},{10,11... | collective-permute-start | bytes 786440 | tf_op jit(solution)/shard_map/ppermute | solution.py:39
  23.1 5.9 %collective-permute-start.10 = (bf16[128,512]{1,0:T(8,128)(2,1)S(1)}, bf16[128,512]{1,0:T(8,128)(2,1)S(1)}, u32[]{:S(2)}, u32[]{:S(2)}) collective-permute-start(bf16[128,512]{1,0:T(8,128)(2,1)S(1)} %collective-permute-done.6.refs_6_), channel_id=1, source_target_pairs={{0,4},{4,0},{8,12},{12,8},{1,5},{5,1},{9,13},{13,9},{2,6},{6,2},{1... | collective-permute-start | bytes 393224 | tf_op jit(solution)/shard_map/ppermute | solution.py:39
  29.6 7.8 %collective-permute-start.11 = (bf16[128,768]{1,0:T(8,128)(2,1)S(1)}, bf16[128,768]{1,0:T(8,128)(2,1)S(1)}, u32[]{:S(2)}, u32[]{:S(2)}) collective-permute-start(bf16[128,768]{1,0:T(8,128)(2,1)S(1)} %get-tuple-element.39), channel_id=1, source_target_pairs={{0,2},{1,3},{2,0},{3,1},{4,6},{5,7},{6,4},{7,5},{8,10},{9,11},{10,... | collective-permute-start | bytes 589832 | tf_op jit(solution)/shard_map/ppermute | solution.py:39
  30.5 9.8 %collective-permute-start.12 = (bf16[128,768]{1,0:T(8,128)(2,1)S(1)}, bf16[128,768]{1,0:T(8,128)(2,1)S(1)}, u32[]{:S(2)}, u32[]{:S(2)}) collective-permute-start(bf16[128,768]{1,0:T(8,128)(2,1)S(1)} %get-tuple-element.42), channel_id=1, source_target_pairs={{0,2},{1,3},{2,0},{3,1},{4,6},{5,7},{6,4},{7,5},{8,10},{9,11},{10,... | collective-permute-start | bytes 589832 | tf_op jit(solution)/shard_map/ppermute | solution.py:39
  38.0 4.6 %collective-permute-start.15 = (bf16[256,512]{1,0:T(8,128)(2,1)S(1)}, bf16[256,512]{1,0:T(8,128)(2,1)S(1)}, u32[]{:S(2)}, u32[]{:S(2)}) collective-permute-start(bf16[256,512]{1,0:T(8,128)(2,1)S(1)} %get-tuple-element.46), channel_id=1, source_target_pairs={{0,1},{1,0},{2,3},{3,2},{4,5},{5,4},{6,7},{7,6},{8,9},{9,8},{10,11... | collective-permute-start | bytes 786440 | tf_op jit(solution)/shard_map/ppermute | solution.py:39
  40.9 2.7 %collective-permute-start.13 = (bf16[256,512]{1,0:T(8,128)(2,1)S(1)}, bf16[256,512]{1,0:T(8,128)(2,1)S(1)}, u32[]{:S(2)}, u32[]{:S(2)}) collective-permute-start(bf16[256,512]{1,0:T(8,128)(2,1)S(1)} %get-tuple-element.45), channel_id=1, source_target_pairs={{0,1},{1,0},{2,3},{3,2},{4,5},{5,4},{6,7},{7,6},{8,9},{9,8},{10,11... | collective-permute-start | bytes 786440 | tf_op jit(solution)/shard_map/ppermute | solution.py:39
  40.9 15.3 %collective-permute-start.7 = (bf16[256,512]{1,0:T(8,128)(2,1)S(1)}, bf16[256,512]{1,0:T(8,128)(2,1)S(1)}, u32[]{:S(2)}, u32[]{:S(2)}) collective-permute-start(bf16[256,512]{1,0:T(8,128)(2,1)S(1)} %get-tuple-element.35), channel_id=1, source_target_pairs={{0,1},{1,0},{2,3},{3,2},{4,5},{5,4},{6,7},{7,6},{8,9},{9,8},{10,11... | collective-permute-start | bytes 786440 | tf_op jit(solution)/shard_map/ppermute | solution.py:39
  41.4 14.8 %collective-permute-start.9 = (bf16[256,512]{1,0:T(8,128)(2,1)S(1)}, bf16[256,512]{1,0:T(8,128)(2,1)S(1)}, u32[]{:S(2)}, u32[]{:S(2)}) collective-permute-start(bf16[256,512]{1,0:T(8,128)(2,1)S(1)} %add_convert_fusion), channel_id=1, source_target_pairs={{0,4},{4,0},{8,12},{12,8},{1,5},{5,1},{9,13},{13,9},{2,6},{6,2},{1... | collective-permute-start | bytes 786440 | tf_op jit(solution)/shard_map/ppermute | solution.py:39
  42.7 9.2 %collective-permute-start.16 = (bf16[64,512]{1,0:T(8,128)(2,1)S(1)}, bf16[64,512]{1,0:T(8,128)(2,1)S(1)}, u32[]{:S(2)}, u32[]{:S(2)}) collective-permute-start(bf16[64,512]{1,0:T(8,128)(2,1)S(1)} %add_convert_fusion.7), channel_id=1, source_target_pairs={{0,4},{4,0},{8,12},{12,8},{1,5},{5,1},{9,13},{13,9},{2,6},{6,2},{1... | collective-permute-start | bytes 196616 | tf_op jit(solution)/shard_map/ppermute | solution.py:39
  43.6 9.2 %collective-permute-start.14 = (bf16[64,512]{1,0:T(8,128)(2,1)S(1)}, bf16[64,512]{1,0:T(8,128)(2,1)S(1)}, u32[]{:S(2)}, u32[]{:S(2)}) collective-permute-start(bf16[64,512]{1,0:T(8,128)(2,1)S(1)} %add_convert_fusion.8), channel_id=1, source_target_pairs={{0,4},{4,0},{8,12},{12,8},{1,5},{5,1},{9,13},{13,9},{2,6},{6,2},{1... | collective-permute-start | bytes 196616 | tf_op jit(solution)/shard_map/ppermute | solution.py:39
  51.9 4.3 %collective-permute-start.19 = (bf16[64,512]{1,0:T(8,128)(2,1)S(1)}, bf16[64,512]{1,0:T(8,128)(2,1)S(1)}, u32[]{:S(2)}, u32[]{:S(2)}) collective-permute-start(bf16[64,512]{1,0:T(8,128)(2,1)S(1)} %add_convert_fusion.6), channel_id=1, source_target_pairs={{0,2},{1,3},{2,0},{3,1},{4,6},{5,7},{6,4},{7,5},{8,10},{9,11},{10,... | collective-permute-start | bytes 196616 | tf_op jit(solution)/shard_map/ppermute | solution.py:39
  52.8 4.3 %collective-permute-start.21 = (bf16[64,512]{1,0:T(8,128)(2,1)S(1)}, bf16[64,512]{1,0:T(8,128)(2,1)S(1)}, u32[]{:S(2)}, u32[]{:S(2)}) collective-permute-start(bf16[64,512]{1,0:T(8,128)(2,1)S(1)} %add_convert_fusion.5), channel_id=1, source_target_pairs={{0,2},{1,3},{2,0},{3,1},{4,6},{5,7},{6,4},{7,5},{8,10},{9,11},{10,... | collective-permute-start | bytes 196616 | tf_op jit(solution)/shard_map/ppermute | solution.py:39
  54.1 5.0 %collective-permute-start.17 = (bf16[128,512]{1,0:T(8,128)(2,1)S(1)}, bf16[128,512]{1,0:T(8,128)(2,1)S(1)}, u32[]{:S(2)}, u32[]{:S(2)}) collective-permute-start(bf16[128,512]{1,0:T(8,128)(2,1)S(1)} %pad_maximum_fusion), channel_id=1, source_target_pairs={{0,4},{4,0},{8,12},{12,8},{1,5},{5,1},{9,13},{13,9},{2,6},{6,2},{1... | collective-permute-start | bytes 393224 | tf_op jit(solution)/shard_map/ppermute | solution.py:39
  59.2 8.7 %collective-permute-start.18 = (bf16[128,512]{1,0:T(8,128)(2,1)S(1)}, bf16[128,512]{1,0:T(8,128)(2,1)S(1)}, u32[]{:S(2)}, u32[]{:S(2)}) collective-permute-start(bf16[128,512]{1,0:T(8,128)(2,1)S(1)} %fusion), channel_id=1, source_target_pairs={{0,2},{1,3},{2,0},{3,1},{4,6},{5,7},{6,4},{7,5},{8,10},{9,11},{10,... | collective-permute-start | bytes 393224 | tf_op jit(solution)/shard_map/ppermute | solution.py:39
  60.1 6.6 %collective-permute-start.22 = (bf16[64,512]{1,0:T(8,128)(2,1)S(1)}, bf16[64,512]{1,0:T(8,128)(2,1)S(1)}, u32[]{:S(2)}, u32[]{:S(2)}) collective-permute-start(bf16[64,512]{1,0:T(8,128)(2,1)S(1)} %add_convert_fusion.1), channel_id=1, source_target_pairs={{0,8},{4,12},{8,0},{12,4},{1,9},{5,13},{9,1},{13,5},{2,10},{6,14},... | collective-permute-start | bytes 196616 | tf_op jit(solution)/shard_map/ppermute | solution.py:39
  62.7 5.2 %collective-permute-start.20 = (bf16[64,512]{1,0:T(8,128)(2,1)S(1)}, bf16[64,512]{1,0:T(8,128)(2,1)S(1)}, u32[]{:S(2)}, u32[]{:S(2)}) collective-permute-start(bf16[64,512]{1,0:T(8,128)(2,1)S(1)} %add_convert_fusion.2), channel_id=1, source_target_pairs={{0,8},{4,12},{8,0},{12,4},{1,9},{5,13},{9,1},{13,5},{2,10},{6,14},... | collective-permute-start | bytes 196616 | tf_op jit(solution)/shard_map/ppermute | solution.py:39
  (1 other events, 1.9 us)
